TPU v7x, 32 devices: a whole 2x2x4 slice. The times are simulated.
32 devices in a mesh: dp: 16 (over z, x, core), tensor: 2 (over y).
Axes of the slice: x: 2, y: 2, z: 4, core: 2. Of those that a mesh axis runs over, the one named last changes fastest.
Arguments:
- inputs: bfloat16 [730, 32, 1152], P('tensor', 'dp'), may hold values from -6 to 6
- lengths: int32 [32], P('dp'), may hold values from 364 to 729, as said below
- cotangent: bfloat16 [730, 32, 1152], P('tensor', 'dp'), may hold values from -6 to 6
- ln_gain: float32 [2, 1152], replicated, may hold values from 0.1 to 1.9
- ln_bias: float32 [2, 1152], replicated, may hold values from -3 to 3
- w_qkv: bfloat16 [1152, 3, 1152], P('dp', None, 'tensor')
- qv_bias: float32 [2, 1152], P(None, 'tensor'), may hold values from -2 to 2
- w_out: bfloat16 [1152, 1152], P('tensor', 'dp'), may hold values from -0.75 to 0.75
- out_bias: float32 [2, 1152], replicated, may hold values from -3 to 3
- w_up: bfloat16 [1152, 4304], P('dp', 'tensor'), may hold values from -0.1875 to 0.1875
- up_bias: float32 [4304], P('tensor'), may hold values from -3 to 3
- w_down: bfloat16 [4304, 1152], P('tensor', 'dp'), may hold values from -0.09375 to 0.09375
Outputs:
- output: bfloat16 [730, 32, 1152], P('tensor', 'dp')
- d_inputs: bfloat16 [730, 32, 1152], P('tensor', 'dp')
- g_ln_gain: float32 [2, 1152], replicated
- g_ln_bias: float32 [2, 1152], replicated
- g_qkv: float32 [1152, 3, 1152], P('dp', None, 'tensor')
- g_qv_bias: float32 [2, 1152], P(None, 'tensor')
- g_out: float32 [1152, 1152], P('tensor', 'dp')
- g_out_bias: float32 [2, 1152], replicated
- g_up: float32 [1152, 4304], P('dp', 'tensor')
- g_up_bias: float32 [4304], P('tensor')
- g_down: float32 [4304, 1152], P('tensor', 'dp')
Inputs may be any that keep to these rules, and one draw needn't show every extreme that they name: Each image's valid tokens are its positions 0 to lengths - 1; some image has exactly 729.
All inputs are finite; a program needn't handle non-finite values.
Results may differ from a plain program's by a relative error of at most 0.015.
Values may be sent and summed in bfloat16 or wider, within the bound.
No kernel may reach another device: no remote copies, remote signals or barrier semaphores. Data moves between devices by JAX's collectives and lax.ppermute only.
A program may use at most 256 MiB of HBM per device.

v0:
```python
import jax
import jax.numpy as jnp
from jax import lax
from jax.sharding import PartitionSpec as P

HD = 72


epsilon = 1e-06


def normalize(values, gain, shift):
    mean = jnp.mean(values, axis=-1, keepdims=True)
    centred = values - mean
    variance = jnp.mean(centred * centred, axis=-1, keepdims=True)
    return centred * lax.rsqrt(variance + epsilon) * gain + shift


def gelu_tanh(values):
    return jax.nn.gelu(values, approximate=True)


def on_device(
    inputs,
    lengths,
    cotangent,
    ln_gain,
    ln_bias,
    w_qkv,
    qv_bias,
    w_out,
    out_bias,
    w_up,
    up_bias,
    w_down,
):
    fl = jnp.float32
    bf = jnp.bfloat16
    rows, images, width = inputs.shape
    parts = lax.axis_size("tensor")
    where = lax.axis_index("tensor")
    seq = rows * parts
    cols = w_qkv.shape[2]
    hidden_here = up_bias.shape[0]
    heads_here = cols // HD
    scale = HD ** (-0.5)
    position = where * rows + jnp.arange(rows, dtype=jnp.int32)
    row_valid = (position[:, None] < lengths[None, :]).astype(fl)
    key_valid = jnp.arange(seq, dtype=jnp.int32)[:, None] < lengths[None, :]
    key_mask = key_valid.T[:, None, None, :]
    full_qkv, full_out, full_up, full_down = (
        lax.all_gather(w_qkv, "dp", axis=0, tiled=True),
        lax.all_gather(w_out, "dp", axis=1, tiled=True),
        lax.all_gather(w_up, "dp", axis=0, tiled=True),
        lax.all_gather(w_down, "dp", axis=1, tiled=True),
    )
    x_float = inputs.astype(fl)
    xn1 = normalize(x_float, ln_gain[0], ln_bias[0]).astype(bf)
    xn1_all = lax.all_gather(xn1, "tensor", axis=0, tiled=True)
    bias_three = jnp.stack([qv_bias[0], jnp.zeros_like(qv_bias[0]), qv_bias[1]])
    qkv = (
        jnp.einsum("sid,dkc->sikc", xn1_all, full_qkv, preferred_element_type=fl) + bias_three
    ).astype(bf)
    query = qkv[:, :, 0].reshape(seq, images, heads_here, HD)
    keys = qkv[:, :, 1].reshape(seq, images, heads_here, HD)
    values = qkv[:, :, 2].reshape(seq, images, heads_here, HD)

    def scores_of():
        raw = jnp.einsum("qihe,kihe->ihqk", query, keys, preferred_element_type=fl) * scale
        return jnp.where(key_mask, raw, -jnp.inf)

    raw = scores_of()
    top = jnp.max(raw, axis=-1, keepdims=True)
    lse = top + jnp.log(jnp.sum(jnp.exp(raw - top), axis=-1, keepdims=True))
    probs = jnp.exp(raw - lse).astype(bf)
    attended = (
        jnp.einsum("ihqk,kihe->qihe", probs, values, preferred_element_type=fl)
        .astype(bf)
        .reshape(seq, images, cols)
    )
    block = attended
    h1 = (
        x_float
        + lax.psum_scatter(
            jnp.einsum("sic,cd->sid", block, full_out, preferred_element_type=fl),
            "tensor",
            scatter_dimension=0,
            tiled=True,
        )
        + out_bias[0]
    )
    xn2 = normalize(h1, ln_gain[1], ln_bias[1]).astype(bf)
    xn2_all = lax.all_gather(xn2, "tensor", axis=0, tiled=True)
    pre = jnp.einsum("sid,df->sif", xn2_all, full_up, preferred_element_type=fl) + up_bias
    act = gelu_tanh(pre).astype(bf)
    block = act
    y_float = (
        h1
        + lax.psum_scatter(
            jnp.einsum("sif,fd->sid", block, full_down, preferred_element_type=fl).astype(
                jnp.bfloat16
            ),
            "tensor",
            scatter_dimension=0,
            tiled=True,
        ).astype(jnp.float32)
        + out_bias[1]
    )
    output = (y_float * row_valid[:, :, None]).astype(bf)
    dy_masked = cotangent * row_valid[:, :, None].astype(bf)
    dy_float = dy_masked.astype(fl)
    grad_b2 = jnp.sum(dy_float, axis=(0, 1))
    dy_all = lax.all_gather(dy_masked, "tensor", axis=0, tiled=True)
    full_qkv, full_out, full_up, full_down = (
        lax.all_gather(w_qkv, "dp", axis=0, tiled=True),
        lax.all_gather(w_out, "dp", axis=1, tiled=True),
        lax.all_gather(w_up, "dp", axis=0, tiled=True),
        lax.all_gather(w_down, "dp", axis=1, tiled=True),
    )
    grad_down = jnp.einsum("sif,sid->fd", act, dy_all, preferred_element_type=fl)
    d_act = jnp.einsum("sid,fd->sif", dy_all, full_down, preferred_element_type=fl)
    d_pre = jax.vjp(gelu_tanh, pre)[1](d_act)[0]
    grad_b1 = jnp.sum(d_pre, axis=(0, 1))
    d_pre_b = d_pre.astype(bf)
    grad_up = jnp.einsum("sid,sif->df", xn2_all, d_pre_b, preferred_element_type=fl)
    block = d_pre_b
    d_xn2 = lax.psum_scatter(
        jnp.einsum("sif,df->sid", block, full_up, preferred_element_type=fl),
        "tensor",
        scatter_dimension=0,
        tiled=True,
    )
    d_h1_ln, grad_g2, grad_c2 = jax.vjp(normalize, h1, ln_gain[1], ln_bias[1])[1](d_xn2)
    d_h1 = dy_float + d_h1_ln
    grad_bo = jnp.sum(d_h1, axis=(0, 1))
    d_h1_all = lax.all_gather(d_h1.astype(bf), "tensor", axis=0, tiled=True)
    grad_out = jnp.einsum("sic,sid->cd", attended, d_h1_all, preferred_element_type=fl)
    d_att = (
        jnp.einsum("sid,cd->sic", d_h1_all, full_out, preferred_element_type=fl)
        .astype(bf)
        .reshape(seq, images, heads_here, HD)
    )
    probs_f = jnp.exp(scores_of() - lse)
    d_probs = jnp.einsum("qihe,kihe->ihqk", d_att, values, preferred_element_type=fl)
    delta = jnp.sum(probs_f * d_probs, axis=-1, keepdims=True)
    d_raw = (probs_f * (d_probs - delta) * scale).astype(bf)
    d_query = jnp.einsum("ihqk,kihe->qihe", d_raw, keys, preferred_element_type=fl)
    d_keys = jnp.einsum("ihqk,qihe->kihe", d_raw, query, preferred_element_type=fl)
    d_values = jnp.einsum("ihqk,qihe->kihe", probs_f.astype(bf), d_att, preferred_element_type=fl)
    d_qkv = jnp.stack([d_query, d_keys, d_values], axis=2).reshape(seq, images, 3, cols)
    grad_qv = jnp.stack(
        [jnp.sum(d_qkv[:, :, 0], axis=(0, 1)), jnp.sum(d_qkv[:, :, 2], axis=(0, 1))]
    )
    d_qkv_b = d_qkv.astype(bf)
    grad_qkv = jnp.einsum("sid,sikc->dkc", xn1_all, d_qkv_b, preferred_element_type=fl)
    block = d_qkv_b
    d_xn1 = lax.psum_scatter(
        jnp.einsum("sikc,dkc->sid", block, full_qkv, preferred_element_type=fl),
        "tensor",
        scatter_dimension=0,
        tiled=True,
    )
    d_x_ln, grad_g1, grad_c1 = jax.vjp(normalize, x_float, ln_gain[0], ln_bias[0])[1](d_xn1)
    d_inputs = (d_h1 + d_x_ln).astype(bf)
    g_qkv, g_out, g_up, g_down = (
        lax.psum_scatter(
            grad_qkv.astype(jnp.bfloat16), "dp", scatter_dimension=0, tiled=True
        ).astype(jnp.float32),
        lax.psum_scatter(
            grad_out.astype(jnp.bfloat16), "dp", scatter_dimension=1, tiled=True
        ).astype(jnp.float32),
        lax.psum_scatter(
            grad_up.astype(jnp.bfloat16), "dp", scatter_dimension=0, tiled=True
        ).astype(jnp.float32),
        lax.psum_scatter(
            grad_down.astype(jnp.bfloat16), "dp", scatter_dimension=1, tiled=True
        ).astype(jnp.float32),
    )
    zero_index = jnp.int32(0)
    small = jnp.stack([grad_g1, grad_g2, grad_c1, grad_c2, grad_bo, grad_b2])
    qv_full = lax.dynamic_update_slice(
        jnp.zeros((2, cols * parts), fl), grad_qv, (zero_index, where * cols)
    )
    b1_full = lax.dynamic_update_slice(
        jnp.zeros((hidden_here * parts,), fl), grad_b1, (where * hidden_here,)
    )
    small_sum, qv_sum, b1_sum = lax.psum((small, qv_full, b1_full), ("dp", "tensor"))
    g_qv = lax.dynamic_slice(qv_sum, (zero_index, where * cols), (2, cols))
    g_b1 = lax.dynamic_slice_in_dim(b1_sum, where * hidden_here, hidden_here, 0)
    return (
        output,
        d_inputs,
        small_sum[0:2],
        small_sum[2:4],
        g_qkv,
        g_qv,
        g_out,
        small_sum[4:6],
        g_up,
        g_b1,
        g_down,
    )


def solution(mesh):
    return jax.shard_map(
        on_device,
        mesh=mesh,
        in_specs=(
            P("tensor", "dp", None),
            P("dp"),
            P("tensor", "dp", None),
            P(),
            P(),
            P("dp", None, "tensor"),
            P(None, "tensor"),
            P("tensor", "dp"),
            P(),
            P("dp", "tensor"),
            P("tensor"),
            P("tensor", "dp"),
        ),
        out_specs=(
            P("tensor", "dp", None),
            P("tensor", "dp", None),
            P(),
            P(),
            P("dp", None, "tensor"),
            P(None, "tensor"),
            P("tensor", "dp"),
            P(),
            P("dp", "tensor"),
            P("tensor"),
            P("tensor", "dp"),
        ),
        check_vma=False,
    )
```

profile of v0, /device:TPU:0, one launch (start us, length us, event | category | flops | bytes accessed | tf_op | source)
XLA Modules:
  0.0 1474.4 jit_solution(15695877743092125295)
XLA Ops:
  23.0 48.2 %all-gather.9.cloned.1.call-done = bf16[730,2,1152]{2,1,0:T(2,128)(2,1)} async-done(((bf16[365,2,1152]{2,1,0:T(2,128)(2,1)}), bf16[730,2,1152]{2,1,0:T(2,128)(2,1)}) %all-gather.9.cloned.1.call-update) | async-done | bytes 3363856 | tf_op jit(solution)/shard_map/all_gather | solution.py:59
  71.2 53.9 %all-gather.11.cloned.1.call-done = bf16[1152,3,576]{2,0,1:T(8,128)(2,1)} async-done(((bf16[72,3,576]{2,0,1:T(8,128)(2,1)}), bf16[1152,3,576]{2,0,1:T(8,128)(2,1)}) %all-gather.11.cloned.1.call-update) | async-done | bytes 3981328 | tf_op jit(solution)/shard_map/all_gather | solution.py:52
  135.9 15.7 %fusion.2 = (f32[2,8,730]{2,1,0:T(8,128)S(1)}, f32[2,8,730,730]{2,3,1,0:T(8,128)}) fusion(pred[2,730]{1,0:T(4,128)(4,1)S(1)} %iota_compare_fusion, bf16[730,2,8,72]{0,3,2,1:T(8,128)(2,1)S(1)} %bitcast.94, bf16[730,2,8,72]{0,3,2,1:T(8,128)(2,1)S(1)} %bitcast.92), kind=kOutput, calls=%fused_computation.7 | convolution fusion | flops 1253368960 | bytes 37517620 | tf_op jit(solution)/shard_map/qihe,kihe->ihqk/dot_general | solution.py:69
  151.6 16.8 %exponential_reduce_fusion = f32[2,8,730]{2,1,0:T(8,128)S(1)} fusion(f32[2,8,730,730]{2,3,1,0:T(8,128)} %get-tuple-element.58, f32[2,8,730]{2,1,0:T(8,128)S(1)} %get-tuple-element.57, pred[2,730]{1,0:T(4,128)(4,1)S(1)} %iota_compare_fusion), kind=kLoop, calls=%fused_computation.5 | loop fusion | flops 34093920 | bytes 34200500 | tf_op jit(solution)/shard_map/reduce_sum | solution.py:74
  168.5 16.5 %convolution_convert_fusion = bf16[2,8,72,730]{3,2,1,0:T(8,128)(2,1)} fusion(bf16[730,2,8,72]{0,3,2,1:T(8,128)(2,1)S(1)} %bitcast.96, f32[2,8,730,730]{2,3,1,0:T(8,128)} %get-tuple-element.58, f32[2,8,730]{2,1,0:T(8,128)S(1)} %log_add_fusion, pred[2,730]{1,0:T(4,128)(4,1)S(1)} %iota_compare_fusion), kind=kOutput, calls=%fused_computation.89 | convolution fusion | flops 1262748160 | bytes 37517620 | tf_op jit(solution)/shard_map/ihqk,kihe->qihe/dot_general | solution.py:77
  192.8 10.9 copy.91
  206.4 158.7 %all-reduce.13.cloned.1.call-done = f32[730,2,1152]{2,1,0:T(2,128)} async-done(((f32[730,2,1152]{2,1,0:T(2,128)}), f32[730,2,1152]{2,1,0:T(2,128)}) %all-reduce.13.cloned.1.call-update) | async-done | bytes 6727696
  389.5 32.6 %all-gather.17.cloned.1.call-done = bf16[1152,2152]{1,0:T(8,128)(2,1)} async-done(((bf16[72,2152]{1,0:T(8,128)(2,1)}), bf16[1152,2152]{1,0:T(8,128)(2,1)}) %all-gather.17.cloned.1.call-update) | async-done | bytes 4958224 | tf_op jit(solution)/shard_map/all_gather | solution.py:54
  422.1 48.0 %all-gather.15.cloned.1.call-done = bf16[730,2,1152]{2,1,0:T(2,128)(2,1)} async-done(((bf16[365,2,1152]{2,1,0:T(2,128)(2,1)}), bf16[730,2,1152]{2,1,0:T(2,128)(2,1)}) %all-gather.15.cloned.1.call-update) | async-done | bytes 3363856 | tf_op jit(solution)/shard_map/all_gather | solution.py:93
  470.1 15.1 %fusion.41 = f32[730,2,2152]{2,0,1:T(8,128)} fusion(bf16[1152,2152]{1,0:T(8,128)(2,1)} %all-gather.17.cloned.1.call-done, bf16[730,2,1152]{2,1,0:T(2,128)(2,1)} %all-gather.15.cloned.1.call-done), kind=kOutput, calls=%fused_computation.46 | convolution fusion | flops 7238983680 | bytes 20889728 | tf_op jit(solution)/shard_map/sid,df->sif/dot_general | solution.py:94
  485.1 34.4 %all-gather.21.cloned.1.call-done = bf16[730,2,1152]{2,1,0:T(2,128)(2,1)} async-done(((bf16[365,2,1152]{2,1,0:T(2,128)(2,1)}), bf16[730,2,1152]{2,1,0:T(2,128)(2,1)}) %all-gather.21.cloned.1.call-update) | async-done | bytes 3363856 | tf_op jit(solution)/shard_map/all_gather | solution.py:113
  519.6 56.7 %all-gather.19.cloned.1.call-done = bf16[2152,1152]{0,1:T(8,128)(2,1)} async-done(((bf16[2152,72]{0,1:T(8,128)(2,1)}), bf16[2152,1152]{0,1:T(8,128)(2,1)}) %all-gather.19.cloned.1.call-update) | async-done | bytes 4958224 | tf_op jit(solution)/shard_map/all_gather | solution.py:55
  576.3 19.4 %fusion.115 = (f32[2152]{0:T(1024)}, bf16[730,2,2152]{2,0,1:T(8,128)(2,1)S(1)}) fusion(f32[730,2,2152]{2,0,1:T(8,128)} %fusion.41, f32[2152]{0:T(1024)} %param.22, bf16[2152,1152]{0,1:T(8,128)(2,1)} %all-gather.19.cloned.1.call-done, bf16[730,2,1152]{2,1,0:T(2,128)(2,1)} %all-gather.21.cloned.1.call-done), kind=kOutput, calls=%fused_computation.143 | convolution fusion | flops 7308108288 | bytes 27190784 | tf_op jit(solution)/shard_map/sid,fd->sif/dot_general | solution.py:121
  598.3 13.7 fusion.39
  623.0 16.3 %fusion.43 = bf16[730,2,1152]{2,0,1:T(8,128)(2,1)S(1)} fusion(bf16[2152,1152]{0,1:T(8,128)(2,1)} %all-gather.19.cloned.1.call-done, f32[730,2,2152]{2,0,1:T(8,128)} %fusion.41, f32[2152]{0:T(1024)} %param.22), kind=kOutput, calls=%fused_computation.48 | convolution fusion | flops 7272084992 | bytes 20898336 | tf_op jit(solution)/shard_map/sif,fd->sid/dot_general | solution.py:100
  645.3 139.0 %all-reduce.17.cloned.1.call-done = f32[730,2,1152]{2,1,0:T(2,128)} async-done(((f32[730,2,1152]{2,1,0:T(2,128)}), f32[730,2,1152]{2,1,0:T(2,128)}) %all-reduce.17.cloned.1.call-update) | async-done | bytes 6727696
  797.8 79.7 %all-reduce.15.cloned.1.call-done = bf16[730,2,1152]{2,1,0:T(2,128)(2,1)} async-done(((bf16[730,2,1152]{2,1,0:T(2,128)(2,1)}), bf16[730,2,1152]{2,1,0:T(2,128)(2,1)}) %all-reduce.15.cloned.1.call-update) | async-done | bytes 3363856
  893.5 15.0 %fusion.35 = bf16[2152,1152]{0,1:T(8,128)(2,1)} fusion(bf16[730,2,1152]{2,1,0:T(2,128)(2,1)S(1)} %copy-done.37, f32[730,2,2152]{2,0,1:T(8,128)} %fusion.41, f32[2152]{0:T(1024)S(1)} %copy-done.39), kind=kOutput, calls=%fused_computation.31 | convolution fusion | flops 7272882176 | bytes 20898336 | tf_op jit(solution)/shard_map/sif,sid->fd/dot_general | solution.py:120
  910.4 13.3 fusion.34
  923.8 17.3 %all-gather.23.cloned.1.call-done = bf16[730,2,1152]{2,1,0:T(2,128)(2,1)} async-done(((bf16[365,2,1152]{2,1,0:T(2,128)(2,1)}), bf16[730,2,1152]{2,1,0:T(2,128)(2,1)}) %all-gather.23.cloned.1.call-update) | async-done | bytes 3363856 | tf_op jit(solution)/shard_map/all_gather | solution.py:136
  946.9 16.5 %fusion.116 = f32[2,8,730,730]{2,3,1,0:T(8,128)} fusion(bf16[730,2,8,72]{0,3,2,1:T(8,128)(2,1)S(1)} %bitcast.98, bf16[730,2,8,72]{0,3,2,1:T(8,128)(2,1)S(1)} %bitcast.97), kind=kOutput, calls=%fused_computation.144 | convolution fusion | flops 1227801600 | bytes 37469440 | tf_op jit(solution)/shard_map/qihe,kihe->ihqk/dot_general | solution.py:144
  963.4 59.4 %fusion.76 = bf16[2,8,72,730]{3,2,1,0:T(8,128)(2,1)} fusion(bf16[730,2,8,72]{0,3,2,1:T(8,128)(2,1)S(1)} %bitcast.95, f32[2,8,730,730]{2,3,1,0:T(8,128)} %fusion.116, f32[2,8,730,730]{2,3,1,0:T(8,128)} %get-tuple-element.58, f32[2,8,730]{2,1,0:T(8,128)} %copy-done.26, pred[2,730]{1,0:T(4,128)(4,1)S(1)} %copy-done.25), kind=kOutput, calls=%fused_computation.88 | convolution fusion | flops 1322445312 | bytes 71623216 | tf_op jit(solution)/shard_map/ihqk,qihe->kihe/dot_general | solution.py:148
  1022.8 59.2 %bitcast_convert_fusion.2 = (bf16[730,2,8,72]{0,3,2,1:T(8,128)(2,1)}, f32[2,8,72,730]{3,2,1,0:T(8,128)}) fusion(bf16[730,2,8,72]{0,3,2,1:T(8,128)(2,1)S(1)} %bitcast.93, f32[2,8,730,730]{2,3,1,0:T(8,128)} %fusion.116, f32[2,8,730,730]{2,3,1,0:T(8,128)} %get-tuple-element.58, f32[2,8,730]{2,1,0:T(8,128)} %copy-done.26, pred[2,730]{1,0:T(4,128)(4,1)S(1)} %copy-done.25), kind=kOutput, calls=%fused_computation.57 | convolution fusion | flops 1322445312 | bytes 74987056 | tf_op jit(solution)/shard_map/ihqk,kihe->qihe/dot_general | solution.py:147
  1088.8 17.4 %bitcast_convert_fusion.1 = (bf16[730,2,8,72]{0,3,2,1:T(8,128)(2,1)}, f32[2,8,72,730]{3,2,1,0:T(8,128)}) fusion(bf16[730,2,8,72]{0,3,2,1:T(8,128)(2,1)S(1)} %bitcast.99, f32[2,8,730,730]{2,3,1,0:T(8,128)} %get-tuple-element.58, f32[2,8,730]{2,1,0:T(8,128)S(1)} %copy-done.27, pred[2,730]{1,0:T(4,128)(4,1)S(1)} %copy-done.25), kind=kOutput, calls=%fused_computation.55 | convolution fusion | flops 1262748160 | bytes 40881460 | tf_op jit(solution)/shard_map/ihqk,qihe->kihe/dot_general | solution.py:149
  1106.3 12.3 bitcast_convert_fusion
  1118.5 18.2 %copy.132 = bf16[1152,3,576]{2,1,0:T(4,128)(2,1)} copy(bf16[1152,3,576]{2,0,1:T(8,128)(2,1)S(1)} %bitcast_convert_fusion) | data formatting | bytes 7962624
  1136.8 12.4 reshape.208
  1149.3 13.0 convolution_bitcast_fusion.2
  1162.3 11.0 copy.113
  1185.2 52.2 %reduce-scatter.13.cloned.1.call-done = bf16[72,1728]{1,0:T(8,128)(2,1)} async-done(((bf16[1152,1728]{1,0:T(8,128)(2,1)}), bf16[72,1728]{1,0:T(8,128)(2,1)}) %reduce-scatter.13.cloned.1.call-update) | async-done | bytes 248848
  1239.5 162.0 %all-reduce.19.cloned.1.call-done = f32[730,2,1152]{2,1,0:T(2,128)} async-done(((f32[730,2,1152]{2,1,0:T(2,128)}), f32[730,2,1152]{2,1,0:T(2,128)}) %all-reduce.19.cloned.1.call-update) | async-done | bytes 6727696
  1424.5 40.9 %all-reduce.7 = (f32[6,1152]{1,0:T(8,128)S(1)}, f32[2,1152]{1,0:T(2,128)S(1)}, f32[4304]{0:T(1024)S(1)}) all-reduce(f32[6,1152]{1,0:T(8,128)S(1)} %stack.56, f32[2,1152]{1,0:T(2,128)S(1)} %dynamic_update_slice.6, f32[4304]{0:T(1024)S(1)} %dynamic_update_slice.7), channel_id=1, replica_groups=mesh['dp'=16,'tensor'=2] {'dp','tensor'}, use_global_device_ids=true, to_apply=%region_21.22 | all-reduce | flops 13520 | bytes 108160 | tf_op jit(solution)/shard_map/psum | solution.py:187
  (197 shorter events, 162.8 us)
Async XLA Ops:
  7.2 64.0 %all-gather.9.cloned.1.call-start = ((), (), s32[]{:S(2)}) async-start(), calls=%async_computation.4 | async-start | bytes 5045760 | tf_op jit(solution)/shard_map/all_gather | solution.py:59
  13.0 112.2 %copy-start.12 = (f32[365,2]{1,0:T(8,128)}, f32[365,2]{1,0:T(8,128)S(1)}, u32[]{:S(2)}) copy-start(f32[365,2]{1,0:T(8,128)S(1)} %broadcast_multiply_fusion.2) | copy-start | bytes 8764
  16.9 108.2 %copy-start.30 = (f32[365,2]{0,1:T(2,128)}, f32[365,2]{0,1:T(2,128)S(1)}, u32[]{:S(2)}) copy-start(f32[365,2]{0,1:T(2,128)S(1)} %copy.87) | copy-start | bytes 8764
  17.1 108.0 %copy-start.14 = (f32[365,2]{1,0:T(8,128)}, f32[365,2]{1,0:T(8,128)S(1)}, u32[]{:S(2)}) copy-start(f32[365,2]{1,0:T(8,128)S(1)} %copy.88) | copy-start | bytes 8764
  21.0 104.2 %all-gather.11.cloned.1.call-start = ((), (), s32[]{:S(2)}) async-start(), calls=%async_computation.5 | async-start | bytes 4700160 | tf_op jit(solution)/shard_map/all_gather | solution.py:52
  21.7 163.3 %all-gather.13.cloned.1.call-start = ((), (), s32[]{:S(2)}) async-start(), calls=%async_computation.6 | async-start | bytes 1566720 | tf_op jit(solution)/shard_map/all_gather | solution.py:53
  22.5 342.6 %all-reduce.13.cloned.1.call-start = ((), (), s32[]{:S(2)}) async-start(), calls=%async_computation.13 | async-start | bytes 13455360
  22.8 145.6 %copy-start.24 = (pred[2,730]{1,0:T(4,128)(4,1)}, pred[2,730]{1,0:T(4,128)(4,1)S(1)}, u32[]{:S(2)}) copy-start(pred[2,730]{1,0:T(4,128)(4,1)S(1)} %iota_compare_fusion) | copy-start | bytes 4384
  135.9 32.6 %copy-start.10 = (bf16[730,2,1,576]{0,3,2,1:T(8,128)(2,1)}, bf16[730,2,1,576]{0,3,2,1:T(8,128)(2,1)S(1)}, u32[]{:S(2)}) copy-start(bf16[730,2,1,576]{0,3,2,1:T(8,128)(2,1)S(1)} %get-tuple-element.47) | copy-start | bytes 5045764
  168.4 16.6 %copy-start.26 = (f32[2,8,730]{2,1,0:T(8,128)}, f32[2,8,730]{2,1,0:T(8,128)S(1)}, u32[]{:S(2)}) copy-start(f32[2,8,730]{2,1,0:T(8,128)S(1)} %log_add_fusion) | copy-start | bytes 140164
  203.7 218.4 %all-gather.17.cloned.1.call-start = ((), (), s32[]{:S(2)}) async-start(), calls=%async_computation.8 | async-start | bytes 5326848 | tf_op jit(solution)/shard_map/all_gather | solution.py:54
  204.3 265.7 %all-gather.15.cloned.1.call-start = ((), (), s32[]{:S(2)}) async-start(), calls=%async_computation.7 | async-start | bytes 5045760 | tf_op jit(solution)/shard_map/all_gather | solution.py:93
  381.4 138.1 %all-gather.21.cloned.1.call-start = ((), (), s32[]{:S(2)}) async-start(), calls=%async_computation.10 | async-start | bytes 5045760 | tf_op jit(solution)/shard_map/all_gather | solution.py:113
  388.5 187.8 %all-gather.19.cloned.1.call-start = ((), (), s32[]{:S(2)}) async-start(), calls=%async_computation.9 | async-start | bytes 5326848 | tf_op jit(solution)/shard_map/all_gather | solution.py:55
  389.2 395.1 %all-reduce.17.cloned.1.call-start = ((), (), s32[]{:S(2)}) async-start(), calls=%async_computation.15 | async-start | bytes 13455360
  622.9 254.7 %all-reduce.15.cloned.1.call-start = ((), (), s32[]{:S(2)}) async-start(), calls=%async_computation.14 | async-start | bytes 6727680
  643.8 297.4 %all-gather.23.cloned.1.call-start = ((), (), s32[]{:S(2)}) async-start(), calls=%async_computation.11 | async-start | bytes 5045760 | tf_op jit(solution)/shard_map/all_gather | solution.py:136
  893.4 280.9 %reduce-scatter.19.cloned.1.call-start = ((), (), s32[]{:S(2)}) async-start(), calls=%async_computation.19 | async-start | bytes 5326848
  908.5 267.6 %reduce-scatter.17.cloned.1.call-start = ((), (), s32[]{:S(2)}) async-start(), calls=%async_computation.18 | async-start | bytes 5326848
  923.7 17.4 %copy-start.38 = (bf16[576,1152]{0,1:T(8,128)(2,1)S(1)}, bf16[576,1152]{0,1:T(8,128)(2,1)}, u32[]{:S(2)}) copy-start(bf16[576,1152]{0,1:T(8,128)(2,1)} %all-gather.13.cloned.1.call-done) | copy-start | bytes 3981316
  923.8 23.1 %copy-start.11 = (bf16[730,2,1,576]{0,3,2,1:T(8,128)(2,1)S(1)}, bf16[730,2,1,576]{0,3,2,1:T(8,128)(2,1)}, u32[]{:S(2)}) copy-start(bf16[730,2,1,576]{0,3,2,1:T(8,128)(2,1)} %copy-done.10) | copy-start | bytes 5045764
  923.8 259.9 %reduce-scatter.15.cloned.1.call-start = ((), (), s32[]{:S(2)}) async-start(), calls=%async_computation.17 | async-start | bytes 1566720
  946.9 16.6 %copy-start.9 = (bf16[730,2,1,576]{0,3,2,1:T(8,128)(2,1)S(1)}, bf16[730,2,1,576]{0,3,2,1:T(8,128)(2,1)}, u32[]{:S(2)}) copy-start(bf16[730,2,1,576]{0,3,2,1:T(8,128)(2,1)} %copy-done.8) | copy-start | bytes 5045764
  946.9 16.6 %copy-start.25 = (pred[2,730]{1,0:T(4,128)(4,1)S(1)}, pred[2,730]{1,0:T(4,128)(4,1)}, u32[]{:S(2)}) copy-start(pred[2,730]{1,0:T(4,128)(4,1)} %copy-done.24) | copy-start | bytes 4384
  963.4 59.4 %copy-start.7 = (bf16[730,2,1,576]{0,3,2,1:T(8,128)(2,1)S(1)}, bf16[730,2,1,576]{0,3,2,1:T(8,128)(2,1)}, u32[]{:S(2)}) copy-start(bf16[730,2,1,576]{0,3,2,1:T(8,128)(2,1)} %copy-done.6) | copy-start | bytes 5045764
  1106.2 131.3 %reduce-scatter.13.cloned.1.call-start = ((), (), s32[]{:S(2)}) async-start(), calls=%async_computation.12 | async-start | bytes 4386816
  1149.2 252.2 %all-reduce.19.cloned.1.call-start = ((), (), s32[]{:S(2)}) async-start(), calls=%async_computation.16 | async-start | bytes 13455360
  1178.0 223.5 %copy-start.1 = (bf16[365,2,1152]{2,1,0:T(2,128)(2,1)S(1)}, bf16[365,2,1152]{2,1,0:T(2,128)(2,1)}, u32[]{:S(2)}) copy-start(bf16[365,2,1152]{2,1,0:T(2,128)(2,1)} %param.12) | copy-start | bytes 5045764
  1178.0 223.5 %copy-start.13 = (f32[365,2]{1,0:T(8,128)S(1)}, f32[365,2]{1,0:T(8,128)}, u32[]{:S(2)}) copy-start(f32[365,2]{1,0:T(8,128)} %copy-done.12) | copy-start | bytes 8764
  1178.0 223.5 %copy-start.15 = (f32[365,2]{1,0:T(8,128)S(1)}, f32[365,2]{1,0:T(8,128)}, u32[]{:S(2)}) copy-start(f32[365,2]{1,0:T(8,128)} %copy-done.14) | copy-start | bytes 8764
  1178.0 223.5 %copy-start.23 = (f32[1152]{0:T(1024)S(1)}, f32[1152]{0:T(1024)}, u32[]{:S(2)}) copy-start(f32[1152]{0:T(1024)} %copy-done.22) | copy-start | bytes 13828
  1183.2 226.9 %copy-start.31 = (f32[365,2]{0,1:T(2,128)S(1)}, f32[365,2]{0,1:T(2,128)}, u32[]{:S(2)}) copy-start(f32[365,2]{0,1:T(2,128)} %copy-done.30) | copy-start | bytes 8764
  (28 other events, 192.9 us)
Sparse Core Ops, SparseCore 0:
  21.1 50.0 all-gather.8
  73.4 51.6 all-gather.10
  127.3 37.6 all-gather.12
  203.9 161.1 all-reduce.12
  367.1 54.9 all-gather.16
  424.1 45.9 all-gather.14
  472.2 47.3 all-gather.20
  521.7 54.4 all-gather.18
  623.0 161.2 all-reduce.16
  786.5 91.0 all-reduce.14
  893.5 47.5 all-gather.22
  945.0 76.3 reduce-scatter.18
  1025.4 75.3 reduce-scatter.16
  1106.4 57.7 reduce-scatter.14
  1167.9 69.5 reduce-scatter.12
  1239.8 161.5 all-reduce.18
where the time goes:
time: 1480 us; the launch traced here: 1470 us
  waiting for transfers between devices  886 us (60%)
  matrix products  332 us (22%)
  other arithmetic  104 us (7%)
  local copies, waits for them, and re-layouts  94.2 us (6%)
  blocking collectives  40.9 us (3%)
  between operations  15.7 us (1%)
    unnamed x24, waiting for transfers between devices  594 us
    dot_general x1, matrix products, on_device(): jnp.einsum('ihqk,qihe->kihe', d_raw, query, preferred_element_type=fl)  59.4 us
    dot_general x1, matrix products, on_device(): jnp.einsum('ihqk,kihe->qihe', d_raw, keys, preferred_element_type=fl)  59.2 us
    all_gather x1, waiting for transfers between devices, on_device(): lax.all_gather(w_down, 'dp', axis=1, tiled=True)  56.7 us
    all_gather x1, waiting for transfers between devices, on_device(): lax.all_gather(w_qkv, 'dp', axis=0, tiled=True)  53.9 us
    all_gather x1, waiting for transfers between devices, on_device(): xn1_all = lax.all_gather(xn1, 'tensor', axis=0, tiled=True)  48.2 us
    all_gather x1, waiting for transfers between devices, on_device(): xn2_all = lax.all_gather(xn2, 'tensor', axis=0, tiled=True)  48 us
    psum x1, blocking collectives, on_device(): lax.psum((small, qv_full, b1_full), ('dp', 'tensor'))  40.9 us
  transfers between devices with their start and end apart: 16, of which 12 were waited for; matrix products, arithmetic and copies ran while one was open for 28% of the time, Pallas kernels for 0%

commit v1 on v0

v1 whole, which is shorter than its diff:
```python
import functools

import jax
import jax.numpy as jnp
from jax import lax
from jax.experimental import pallas as pl
from jax.experimental.pallas import tpu as pltpu
from jax.sharding import PartitionSpec as P

HD = 72
epsilon = 1e-06
fl = jnp.float32
bf = jnp.bfloat16


def up_to(n, m):
    return -(-n // m) * m


def dot(a, b, ca, cb):
    return lax.dot_general(a, b, (((ca,), (cb,)), ((), ())), preferred_element_type=fl)


def normalize(values, gain, shift):
    mean = jnp.mean(values, axis=-1, keepdims=True)
    centred = values - mean
    variance = jnp.mean(centred * centred, axis=-1, keepdims=True)
    return centred * lax.rsqrt(variance + epsilon) * gain + shift


def normalize_back(values, gain, grad):
    mean = jnp.mean(values, axis=-1, keepdims=True)
    centred = values - mean
    variance = jnp.mean(centred * centred, axis=-1, keepdims=True)
    inverse = lax.rsqrt(variance + epsilon)
    hat = centred * inverse
    scaled = grad * gain
    first = jnp.mean(scaled, axis=-1, keepdims=True)
    second = jnp.mean(scaled * hat, axis=-1, keepdims=True)
    return inverse * (scaled - first - hat * second), hat


def gelu_tanh(values):
    return jax.nn.gelu(values, approximate=True)


def window(head, colp, win):
    start = jnp.minimum(head * HD // 128 * 128, colp - win)
    return pl.multiple_of(start, 128), head * HD - start


def forward_kernel(bias_ref, qkv_ref, out_ref, lse_ref, *, heads, colp, win):
    scale = HD ** (-0.5)
    out_ref[...] = jnp.zeros_like(out_ref)

    def one_head(head, carry):
        at, off = window(head, colp, win)
        lane = lax.broadcasted_iota(jnp.int32, (1, win), 1)
        mine = (lane >= off) & (lane < off + HD)
        query = qkv_ref[:, pl.ds(at, win)]
        keys = qkv_ref[:, pl.ds(pl.multiple_of(colp + at, 128), win)]
        values = qkv_ref[:, pl.ds(pl.multiple_of(2 * colp + at, 128), win)]
        keys = jnp.where(mine, keys, jnp.zeros_like(keys))
        values = jnp.where(mine, values, jnp.zeros_like(values))
        raw = dot(keys, query, 1, 1) * scale + bias_ref[...]
        top = jnp.max(raw, axis=0, keepdims=True)
        weights = jnp.exp(raw - top)
        total = jnp.sum(weights, axis=0, keepdims=True)
        result = dot(values, weights.astype(bf), 0, 0) / total
        lse_ref[pl.ds(head, 1), :] = top + jnp.log(total)
        out_ref[:, pl.ds(at, win)] = out_ref[:, pl.ds(at, win)] + result.T.astype(bf)
        return carry

    lax.fori_loop(0, heads, one_head, 0)


def attention_forward(qkv, bias, image, size, heads):
    colp = qkv.shape[1] // 3
    win = min(256, colp)
    return pl.pallas_call(
        functools.partial(forward_kernel, heads=heads, colp=colp, win=win),
        grid=(1,),
        out_shape=(
            jax.ShapeDtypeStruct((size, colp), bf),
            jax.ShapeDtypeStruct((heads, size), fl),
        ),
        in_specs=[
            pl.BlockSpec((size, 1), lambda g: (image, 0)),
            pl.BlockSpec((size, 3 * colp), lambda g: (image, 0)),
        ],
        out_specs=(
            pl.BlockSpec((size, colp), lambda g: (0, 0)),
            pl.BlockSpec((heads, size), lambda g: (0, 0)),
        ),
        compiler_params=pltpu.CompilerParams(vmem_limit_bytes=56 * 2**20),
        name="attention_forward",
    )(bias, qkv)


def backward_kernel(
    bias_ref, qkv_ref, out_ref, dout_ref, lse_ref, old_ref, dqkv_ref, *, heads, colp, win
):
    scale = HD ** (-0.5)
    dqkv_ref[...] = jnp.zeros_like(dqkv_ref)

    def one_head(head, carry):
        at, off = window(head, colp, win)
        at_k = pl.multiple_of(colp + at, 128)
        at_v = pl.multiple_of(2 * colp + at, 128)
        lane = lax.broadcasted_iota(jnp.int32, (1, win), 1)
        mine = (lane >= off) & (lane < off + HD)

        def keep(block):
            return jnp.where(mine, block, jnp.zeros_like(block))

        query = keep(qkv_ref[:, pl.ds(at, win)])
        keys = keep(qkv_ref[:, pl.ds(at_k, win)])
        values = keep(qkv_ref[:, pl.ds(at_v, win)])
        d_out = keep(dout_ref[:, pl.ds(at, win)])
        product = d_out.astype(fl) * out_ref[:, pl.ds(at, win)].astype(fl)
        delta = jnp.sum(product, axis=1, keepdims=True).T
        raw = dot(keys, query, 1, 1) * scale + bias_ref[...]
        probs = jnp.exp(raw - lse_ref[pl.ds(head, 1), :])
        d_probs = dot(values, d_out, 1, 1)
        d_raw = (probs * ((d_probs - delta) * scale)).astype(bf)

        def add(place, block):
            dqkv_ref[:, pl.ds(place, win)] = dqkv_ref[:, pl.ds(place, win)] + block.astype(bf)

        add(at_v, dot(probs.astype(bf), d_out, 1, 0))
        add(at_k, dot(d_raw, query, 1, 0))
        add(at, dot(keys, d_raw, 0, 0).T)
        return carry

    lax.fori_loop(0, heads, one_head, 0)


def attention_backward(qkv, bias, attended, d_attended, lse, old, image, size, heads):
    colp = qkv.shape[1] // 3
    win = min(256, colp)
    return pl.pallas_call(
        functools.partial(backward_kernel, heads=heads, colp=colp, win=win),
        grid=(1,),
        out_shape=jax.ShapeDtypeStruct(qkv.shape, bf),
        in_specs=[
            pl.BlockSpec((size, 1), lambda g: (image, 0)),
            pl.BlockSpec((size, 3 * colp), lambda g: (image, 0)),
            pl.BlockSpec((size, colp), lambda g: (0, 0)),
            pl.BlockSpec((size, colp), lambda g: (0, 0)),
            pl.BlockSpec((heads, size), lambda g: (0, 0)),
            pl.BlockSpec(memory_space=pl.ANY),
        ],
        out_specs=pl.BlockSpec((size, 3 * colp), lambda g: (image, 0)),
        input_output_aliases={5: 0},
        compiler_params=pltpu.CompilerParams(vmem_limit_bytes=56 * 2**20),
        name="attention_backward",
    )(bias, qkv, attended, d_attended, lse, old)


def from_others(values, parts):
    return [
        lax.ppermute(values, "tensor", [((j + k) % parts, j) for j in range(parts)])
        for k in range(1, parts)
    ]


def all_blocks(values, where, parts):
    images, rows, width = values.shape
    got = [values] + from_others(values, parts)
    full = jnp.zeros((images, rows * parts, width), values.dtype)
    for k, block in enumerate(got):
        start = (where + k) % parts * rows
        full = lax.dynamic_update_slice(full, block, (jnp.int32(0), start, jnp.int32(0)))
    return full


def sum_blocks(values, where, parts, rows):
    def block(k):
        return lax.dynamic_slice_in_dim(values, (where + k) % parts * rows, rows, 1)

    total = block(0)
    for k in range(1, parts):
        pairs = [(j, (j + k) % parts) for j in range(parts)]
        total = total + lax.ppermute(block(k).astype(bf), "tensor", pairs).astype(fl)
    return total


def sum_everywhere(values, axis):
    size = lax.axis_size(axis)
    if size & (size - 1):
        return lax.psum(values, axis)
    step = 1
    while step < size:
        values = values + lax.ppermute(values, axis, [(j, j ^ step) for j in range(size)])
        step *= 2
    return values


def on_device(
    inputs,
    lengths,
    cotangent,
    ln_gain,
    ln_bias,
    w_qkv,
    qv_bias,
    w_out,
    out_bias,
    w_up,
    up_bias,
    w_down,
):
    rows, images, width = inputs.shape
    parts = lax.axis_size("tensor")
    where = lax.axis_index("tensor")
    cols = w_qkv.shape[2]
    hidden = up_bias.shape[0]
    heads = cols // HD
    here = w_qkv.shape[0]
    rowp, colp, hidp = up_to(rows, 16), up_to(cols, 128), up_to(hidden, 128)
    size = rowp * parts
    both = images * size

    def pad_to(values, axis, n):
        widths = [(0, 0)] * values.ndim
        widths[axis] = (0, n - values.shape[axis])
        return jnp.pad(values, widths)

    shard_qkv = pad_to(w_qkv, 2, colp).reshape(here, 3 * colp)
    full_qkv = lax.all_gather(shard_qkv, "dp", axis=0, tiled=True)
    shard_out = pad_to(w_out.T, 1, colp)
    shard_out = jnp.concatenate([shard_out] + from_others(shard_out, parts), axis=1)
    shard_rest = jnp.concatenate(
        [pad_to(w_up, 1, hidp), pad_to(w_down.T, 1, hidp), shard_out], axis=1
    )
    full_rest = lax.all_gather(shard_rest, "dp", axis=0, tiled=True)
    full_up = full_rest[:, :hidp]
    full_down = full_rest[:, hidp : 2 * hidp]
    full_out = full_rest[:, 2 * hidp :]
    own_out = full_rest[:, 2 * hidp : 2 * hidp + colp]

    place = jnp.arange(size, dtype=jnp.int32)
    position = place // rowp * rows + place % rowp
    valid = (place % rowp < rows)[None, :] & (position[None, :] < lengths[:, None])
    key_bias = jnp.where(valid, 0.0, -1e30).astype(fl).reshape(both, 1)
    own_valid = lax.dynamic_slice_in_dim(valid, where * rowp, rowp, 1)[:, :, None]

    x_own = pad_to(jnp.transpose(inputs, (1, 0, 2)), 1, rowp)
    dy_own = pad_to(jnp.transpose(cotangent, (1, 0, 2)), 1, rowp) * own_valid.astype(bf)
    x_all = all_blocks(x_own, where, parts).reshape(both, width)
    dy_all = all_blocks(dy_own, where, parts).reshape(both, width)

    xn1 = normalize(x_all.astype(fl), ln_gain[0], ln_bias[0]).astype(bf)
    bias_three = pad_to(
        jnp.stack([qv_bias[0], jnp.zeros_like(qv_bias[0]), qv_bias[1]]), 1, colp
    ).reshape(1, 3 * colp)
    qkv = (dot(xn1, full_qkv, 1, 0) + bias_three).astype(bf)

    attended, lses, joined = [], [], []
    for i in range(images):
        out, lse = attention_forward(qkv, key_bias, i, size, heads)
        attended.append(out)
        lses.append(lse)
        joined.append(jnp.concatenate([out] + from_others(out, parts), axis=1))
    joined = jnp.concatenate(joined, axis=0)
    attended_all = jnp.concatenate(attended, axis=0)

    h1 = x_all.astype(fl) + dot(joined, full_out, 1, 1) + out_bias[0]
    xn2 = normalize(h1, ln_gain[1], ln_bias[1]).astype(bf)
    pre = dot(xn2, full_up, 1, 0) + pad_to(up_bias, 0, hidp)
    act, pull = jax.vjp(gelu_tanh, pre)
    act = act.astype(bf)
    d_pre = pull(dot(dy_all, full_down, 1, 0))[0]
    grad_b1 = jnp.sum(d_pre, axis=0)
    d_pre_b = d_pre.astype(bf)

    d_h1, d_h1_b, d_att = [], [], []
    g2, c2, bo = 0.0, 0.0, 0.0
    for i in range(images):
        at = slice(i * size, (i + 1) * size)
        part = dot(d_pre_b[at], full_up, 1, 1).astype(bf)
        total = part.astype(fl)
        for other in from_others(part, parts):
            total = total + other.astype(fl)
        back, hat = normalize_back(h1[at], ln_gain[1], total)
        g2 = g2 + jnp.sum(total * hat, axis=0)
        c2 = c2 + jnp.sum(total, axis=0)
        full = dy_all[at].astype(fl) + back
        bo = bo + jnp.sum(full, axis=0)
        d_h1.append(full)
        d_h1_b.append(full.astype(bf))
        d_att.append(dot(d_h1_b[i], own_out, 1, 0).astype(bf))

    grad_up = dot(xn2, d_pre_b, 0, 0).astype(bf)
    grad_down = dot(dy_all, act, 0, 0).astype(bf)
    mlp_grads = lax.psum_scatter(
        jnp.concatenate([grad_up, grad_down], axis=1), "dp", scatter_dimension=0, tiled=True
    )

    y_part = dot(act, full_down, 1, 1).reshape(images, size, width)
    h1_own = lax.dynamic_slice_in_dim(h1.reshape(images, size, width), where * rowp, rowp, 1)
    y_own = h1_own + sum_blocks(y_part, where, parts, rowp) + out_bias[1]
    output = jnp.where(own_valid, y_own, 0.0).astype(bf)

    d_qkv = jnp.zeros((both, 3 * colp), bf)
    for i in range(images):
        d_qkv = attention_backward(
            qkv, key_bias, attended[i], d_att[i], lses[i], d_qkv, i, size, heads
        )
    sums_qkv = jnp.sum(d_qkv.astype(fl), axis=0)
    grad_qkv = dot(xn1, d_qkv, 0, 0).astype(bf)
    grad_out = dot(jnp.concatenate(d_h1_b, axis=0), attended_all, 0, 0).astype(bf)
    att_grads = lax.psum_scatter(
        jnp.concatenate([grad_qkv, grad_out], axis=1), "dp", scatter_dimension=0, tiled=True
    )

    d_xn1 = sum_blocks(dot(d_qkv, full_qkv, 1, 1).reshape(images, size, width), where, parts, rowp)
    back, hat = normalize_back(x_own.astype(fl), ln_gain[0], d_xn1)
    g1 = jnp.sum(d_xn1 * hat, axis=(0, 1))
    c1 = jnp.sum(d_xn1, axis=(0, 1))
    d_h1_own = jnp.stack([lax.dynamic_slice_in_dim(d, where * rowp, rowp, 0) for d in d_h1])
    d_inputs = (d_h1_own + back).astype(bf)

    b2 = jnp.sum(dy_own.astype(fl), axis=(0, 1))
    pair = jnp.stack([g1, g2 / parts, c1, c2 / parts, bo / parts, b2])
    pair = sum_everywhere(pair, "tensor")
    lone = jnp.concatenate([sums_qkv[:cols], sums_qkv[2 * colp : 2 * colp + cols], grad_b1[:hidden]])
    small = sum_everywhere(jnp.concatenate([pair.reshape(-1), lone]), "dp")
    pair = small[: 6 * width].reshape(6, width)
    lone = small[6 * width :]

    def own_rows(values):
        return jnp.transpose(values[:, :rows], (1, 0, 2))

    att_grads = att_grads.astype(fl)
    mlp_grads = mlp_grads.astype(fl)
    return (
        own_rows(output),
        own_rows(d_inputs),
        pair[0:2],
        pair[2:4],
        att_grads[:, : 3 * colp].reshape(here, 3, colp)[:, :, :cols],
        lone[: 2 * cols].reshape(2, cols),
        att_grads[:, 3 * colp : 3 * colp + cols].T,
        pair[4:6],
        mlp_grads[:, :hidden],
        lone[2 * cols :],
        mlp_grads[:, hidp : hidp + hidden].T,
    )


def solution(mesh):
    return jax.shard_map(
        on_device,
        mesh=mesh,
        in_specs=(
            P("tensor", "dp", None),
            P("dp"),
            P("tensor", "dp", None),
            P(),
            P(),
            P("dp", None, "tensor"),
            P(None, "tensor"),
            P("tensor", "dp"),
            P(),
            P("dp", "tensor"),
            P("tensor"),
            P("tensor", "dp"),
        ),
        out_specs=(
            P("tensor", "dp", None),
            P("tensor", "dp", None),
            P(),
            P(),
            P("dp", None, "tensor"),
            P(None, "tensor"),
            P("tensor", "dp"),
            P(),
            P("dp", "tensor"),
            P("tensor"),
            P("tensor", "dp"),
        ),
        check_vma=False,
    )
```

time: 1480 us -> 598 us (0.40)
  waiting for transfers between devices: 886 us -> 233 us
  matrix products: 332 us -> 150 us
  Pallas kernels: 0 us -> 71.3 us
  other arithmetic: 104 us -> 53.1 us
  local copies, waits for them, and re-layouts: 94.2 us -> 50 us
  blocking collectives: 40.9 us -> 0 us
  starting transfers between devices: 1.25 us -> 16.4 us
    unnamed x24 -> x4, waiting for transfers between devices: 594 us -> 0.07 us
    all_gather x8 -> x2, waiting for transfers between devices: 291 us -> 17.6 us  [the longest x1 17.6 us: on_device(): full_rest = lax.all_gather(shard_rest, 'dp', axis=0, tiled=True)]
    ppermute x0 -> x14, waiting for transfers between devices: none -> 191 us  [the longest x7 125 us: from_others(): lax.ppermute(values, 'tensor', [((j + k) % parts, j) for j in range(parts)])]
    dot_general x18 -> x14, matrix products: 332 us -> 150 us  [dot(): lax.dot_general(a, b, (((ca,), (cb,)), ((), ())), preferred_element_type=fl)]
    pallas_call x0 -> x4, Pallas kernels: none -> 71.3 us  [the longest x2 41.2 us: attention_backward(): pl.pallas_call(functools.partial(backward_kernel, heads=heads, colp=colp,...]
    reduce_sum x8 -> x9, other arithmetic: 64 us -> 19.8 us  [the longest x1 5.05 us: on_device(): bo = bo + jnp.sum(full, axis=0)]
    psum x1 -> x0, blocking collectives: 40.9 us -> none  [on_device(): lax.psum((small, qv_full, b1_full), ('dp', 'tensor'))]
    dot_general x3 -> x0, local copies, waits for them, and re-layouts: 32.7 us -> none  [the longest x1 11 us: on_device(): jnp.einsum('sikc,dkc->sid', block, full_qkv, preferred_element_type=fl)]
  transfers between devices with their start and end apart: 16 -> 18, of which waited for: 12 -> 13; matrix products, arithmetic and copies ran while one was open for 28% -> 26% of each run, Pallas kernels for 0% -> 5%
where the time goes in v1:
time: 598 us; the launch traced here: 589 us
  waiting for transfers between devices  233 us (39%)
  matrix products  150 us (25%)
  Pallas kernels  71.3 us (12%)
  other arithmetic  53.1 us (9%)
  local copies, waits for them, and re-layouts  50 us (8%)
  starting transfers between devices  16.4 us (3%)
  between operations  14.6 us (2%)
    dot_general x14, matrix products, dot(): lax.dot_general(a, b, (((ca,), (cb,)), ((), ())), preferred_element_type=fl)  150 us
    ppermute x7, waiting for transfers between devices, from_others(): lax.ppermute(values, 'tensor', [((j + k) % parts, j) for j in range(parts)])  125 us
    pallas_call x2, Pallas kernels, attention_backward(): pl.pallas_call(functools.partial(backward_kernel, heads=heads, colp=colp,...  41.2 us
    ppermute x5, waiting for transfers between devices, sum_everywhere(): lax.ppermute(values, axis, [(j, j ^ step) for j in range(size)])  38.2 us
    pallas_call x2, Pallas kernels, attention_forward(): pl.pallas_call(functools.partial(forward_kernel, heads=heads, colp=colp,...  30 us
    ppermute x2, waiting for transfers between devices, sum_blocks(): lax.ppermute(block(k).astype(bf), 'tensor', pairs).astype(fl)  27 us
    reduce_scatter x1, waiting for transfers between devices, on_device(): lax.psum_scatter(jnp.concatenate([grad_up, grad_down], axis=1), 'dp', sca...  25.1 us
    all_gather x1, waiting for transfers between devices, on_device(): full_rest = lax.all_gather(shard_rest, 'dp', axis=0, tiled=True)  17.6 us
  transfers between devices with their start and end apart: 18, of which 13 were waited for; matrix products, arithmetic and copies ran while one was open for 26% of the time, Pallas kernels for 5%

profile of v1, /device:TPU:0, one launch (start us, length us, event | category | flops | bytes accessed | tf_op | source)
XLA Modules:
  0.0 588.9 jit_solution(15369459002808419982)
XLA Ops:
  33.7 29.1 %collective-permute-done = bf16[2,368,1152]{2,1,0:T(8,128)(2,1)} collective-permute-done((bf16[2,368,1152]{2,1,0:T(8,128)(2,1)}, bf16[2,368,1152]{2,1,0:T(8,128)(2,1)}, u32[]{:S(2)}, u32[]{:S(2)}) %collective-permute-start) | collective-permute-done | bytes 1695776 | tf_op jit(solution)/shard_map/ppermute | solution.py:162
  69.0 12.4 %add_convert_fusion.qkv_ref = bf16[1472,1920]{1,0:T(8,128)(2,1)} fusion(bf16[1472,1152]{1,0:T(8,128)(2,1)} %fusion.10, bf16[1152,1920]{1,0:T(8,128)(2,1)} %all-gather.3.cloned.1.call-done, f32[1920]{0:T(1024)S(1)} %add.282), kind=kOutput, calls=%fused_computation.13 | convolution fusion | flops 6517309440 | bytes 13475328 | tf_op jit(solution)/shard_map/dot_general | solution.py:21
  81.4 14.8 %attention_forward.3 = (bf16[736,640]{1,0:T(8,128)(2,1)}, f32[8,736]{1,0:T(8,128)}) custom-call(f32[1472,1]{1,0:T(8,128)} %select_n.95.bias_ref, bf16[1472,1920]{1,0:T(8,128)(2,1)} %add_convert_fusion.qkv_ref), custom_call_target="tpu_custom_call" | custom-call | tf_op jit(solution)/shard_map/attention_forward/pallas_call | solution.py:80
  96.2 15.3 %attention_forward.2 = (bf16[736,640]{1,0:T(8,128)(2,1)}, f32[8,736]{1,0:T(8,128)}) custom-call(f32[1472,1]{1,0:T(8,128)} %select_n.95.bias_ref, bf16[1472,1920]{1,0:T(8,128)(2,1)} %add_convert_fusion.qkv_ref), custom_call_target="tpu_custom_call" | custom-call | tf_op jit(solution)/shard_map/attention_forward/pallas_call | solution.py:80
  121.7 13.5 %collective-permute-done.2 = bf16[736,640]{1,0:T(8,128)(2,1)S(1)} collective-permute-done((bf16[736,640]{1,0:T(8,128)(2,1)S(1)}, bf16[736,640]{1,0:T(8,128)(2,1)S(1)}, u32[]{:S(2)}, u32[]{:S(2)}) %collective-permute-start.2) | collective-permute-done | bytes 942112 | tf_op jit(solution)/shard_map/ppermute | solution.py:162
  136.1 14.9 %collective-permute-done.1 = bf16[736,640]{1,0:T(8,128)(2,1)} collective-permute-done((bf16[736,640]{1,0:T(8,128)(2,1)}, bf16[736,640]{1,0:T(8,128)(2,1)}, u32[]{:S(2)}, u32[]{:S(2)}) %collective-permute-start.1) | collective-permute-done | bytes 942112 | tf_op jit(solution)/shard_map/ppermute | solution.py:162
  151.1 17.6 %all-gather.5.cloned.1.call-done = bf16[1152,5632]{1,0:T(8,128)(2,1)} async-done(((bf16[72,5632]{1,0:T(8,128)(2,1)}), bf16[1152,5632]{1,0:T(8,128)(2,1)}) %all-gather.5.cloned.1.call-update) | async-done | bytes 12976144 | tf_op jit(solution)/shard_map/all_gather | solution.py:236
  168.7 8.4 %fusion.97 = (f32[1472]{0:T(1024)S(1)}, f32[1472,1152]{1,0:T(8,128)S(1)}) fusion(f32[1152]{0:T(1024)S(1)} %get-tuple-element.63, bf16[1152,5632]{1,0:T(8,128)(2,1)} %all-gather.5.cloned.1.call-done, bf16[736,640]{1,0:T(8,128)(2,1)} %copy-done.27, bf16[736,640]{1,0:T(8,128)(2,1)} %get-tuple-element.16.out_ref, bf16[736,640]{1,0:T(8,128)(2,1)} %collective-permute-done.1, ...), kind=kOutput, calls=%fused_computation.188 | convolution fusion | flops 4362959360 | bytes 16902400 | tf_op jit(solution)/shard_map/dot_general | solution.py:21
  178.0 16.3 %convolution_add_fusion = f32[1472,2176]{1,0:T(8,128)} fusion(f32[2176]{0:T(1024)S(1)} %pad.36, bf16[1152,5632]{1,0:T(8,128)(2,1)} %all-gather.5.cloned.1.call-done, f32[1472,1152]{1,0:T(8,128)S(1)} %get-tuple-element.94, f32[1152]{0:T(1024)S(1)} %get-tuple-element.61, f32[1152]{0:T(1024)S(1)} %get-tuple-element.59, f32[1472]{0:T(1024)S(1)} %add_rsqrt_fusion, ...), kind=kOutput, calls=%fused_computation.2 | convolution fusion | flops 7391559680 | bytes 24638464 | tf_op jit(solution)/shard_map/dot_general | solution.py:21
  194.2 20.7 %fusion.92 = (f32[2176]{0:T(1024)S(1)}, bf16[1472,2176]{1,0:T(8,128)(2,1)S(1)}) fusion(f32[1472,2176]{1,0:T(8,128)} %convolution_add_fusion, bf16[1472,1152]{1,0:T(8,128)(2,1)} %bitcast.9, bf16[1152,5632]{1,0:T(8,128)(2,1)} %all-gather.5.cloned.1.call-done), kind=kOutput, calls=%fused_computation.183 | convolution fusion | flops 7447140352 | bytes 27632128 | tf_op jit(solution)/shard_map/dot_general | solution.py:21
  215.0 9.3 %fusion.44 = bf16[736,1152]{1,0:T(8,128)(2,1)S(1)} fusion(bf16[1152,5632]{1,0:T(8,128)(2,1)} %all-gather.5.cloned.1.call-done, bf16[1472,2176]{1,0:T(8,128)(2,1)S(1)} %get-tuple-element.77), kind=kOutput, calls=%fused_computation.81 | convolution fusion | flops 3690786816 | bytes 9912320 | tf_op jit(solution)/shard_map/dot_general | solution.py:21
  225.8 7.0 %fusion.47 = bf16[736,1152]{1,0:T(8,128)(2,1)S(1)} fusion(bf16[1152,5632]{1,0:T(8,128)(2,1)} %all-gather.5.cloned.1.call-done, bf16[1472,2176]{1,0:T(8,128)(2,1)S(1)} %get-tuple-element.77), kind=kOutput, calls=%fused_computation.82 | convolution fusion | flops 3690786816 | bytes 9912320 | tf_op jit(solution)/shard_map/dot_general | solution.py:21
  234.7 29.6 %collective-permute-done.6 = bf16[736,1152]{1,0:T(8,128)(2,1)S(1)} collective-permute-done((bf16[736,1152]{1,0:T(8,128)(2,1)S(1)}, bf16[736,1152]{1,0:T(8,128)(2,1)S(1)}, u32[]{:S(2)}, u32[]{:S(2)}) %collective-permute-start.6) | collective-permute-done | bytes 1695776 | tf_op jit(solution)/shard_map/ppermute | solution.py:162
  264.2 35.6 %collective-permute-done.7 = bf16[736,1152]{1,0:T(8,128)(2,1)S(1)} collective-permute-done((bf16[736,1152]{1,0:T(8,128)(2,1)S(1)}, bf16[736,1152]{1,0:T(8,128)(2,1)S(1)}, u32[]{:S(2)}, u32[]{:S(2)}) %collective-permute-start.7) | collective-permute-done | bytes 1695776 | tf_op jit(solution)/shard_map/ppermute | solution.py:162
  299.9 4.5 multiply_reduce_fusion.3
  304.4 5.0 fusion.90
  315.5 3.9 convolution_convert_fusion.3.dout_ref
  322.2 20.5 %attention_backward.2.old_ref = bf16[1472,1920]{1,0:T(8,128)(2,1)} custom-call(f32[1472,1]{1,0:T(8,128)} %select_n.95.bias_ref, bf16[1472,1920]{1,0:T(8,128)(2,1)} %add_convert_fusion.qkv_ref, bf16[736,640]{1,0:T(8,128)(2,1)} %get-tuple-element.15.out_ref, bf16[736,640]{1,0:T(8,128)(2,1)} %convolution_convert_fusion.3.dout_ref, ...), custom_call_target="tpu_custom_call", output_to_operand_aliasing={{}: (5, {})} | custom-call | tf_op jit(solution)/shard_map/attention_backward/pallas_call | solution.py:141
  342.7 3.9 convolution_convert_fusion.4.dout_ref
  346.6 20.8 %attention_backward.3 = bf16[1472,1920]{1,0:T(8,128)(2,1)} custom-call(f32[1472,1]{1,0:T(8,128)} %select_n.95.bias_ref, bf16[1472,1920]{1,0:T(8,128)(2,1)} %add_convert_fusion.qkv_ref, bf16[736,640]{1,0:T(8,128)(2,1)} %get-tuple-element.16.out_ref, bf16[736,640]{1,0:T(8,128)(2,1)} %convolution_convert_fusion.4.dout_ref, ...), custom_call_target="tpu_custom_call", output_to_operand_aliasing={{}: (5, {})} | custom-call | tf_op jit(solution)/shard_map/attention_backward/pallas_call | solution.py:141
  367.3 9.6 %convolution_convert_fusion.2 = bf16[1152,1920]{1,0:T(8,128)(2,1)S(1)} fusion(bf16[1472,1152]{1,0:T(8,128)(2,1)S(1)} %copy-done.9, bf16[1472,1920]{1,0:T(8,128)(2,1)} %attention_backward.3), kind=kOutput, calls=%fused_computation.17 | convolution fusion | flops 6513868800 | bytes 13467648 | tf_op jit(solution)/shard_map/dot_general | solution.py:21
  380.1 13.9 %convolution_convert_fusion = bf16[1152,2176]{1,0:T(8,128)(2,1)S(1)} fusion(bf16[1472,1152]{1,0:T(8,128)(2,1)} %bitcast.9, f32[1472,2176]{1,0:T(8,128)} %convolution_add_fusion), kind=kOutput, calls=%fused_computation.10 | convolution fusion | flops 7411212288 | bytes 21217280 | tf_op jit(solution)/shard_map/dot_general | solution.py:21
  394.0 13.5 %convolution_convert_fusion.1 = bf16[1152,2176]{1,0:T(8,128)(2,1)S(1)} fusion(bf16[1472,2176]{1,0:T(8,128)(2,1)} %copy-done.28, f32[1472,1152]{1,0:T(8,128)} %copy-done, f32[1152]{0:T(1024)S(1)} %get-tuple-element.61, f32[1152]{0:T(1024)S(1)} %get-tuple-element.59, f32[1472]{0:T(1024)S(1)} %add_rsqrt_fusion, f32[1472]{0:T(1024)S(1)} %broadcast_multiply_fusion.1), kind=kOutput, calls=%fused_computation.11 | convolution fusion | flops 7390863360 | bytes 18223616 | tf_op jit(solution)/shard_map/dot_general | solution.py:21
  407.5 4.5 pad_maximum_fusion
  414.5 17.9 %fusion.13 = f32[1472,1152]{1,0:T(8,128)} fusion(bf16[1152,5632]{1,0:T(8,128)(2,1)} %all-gather.5.cloned.1.call-done, f32[1472,2176]{1,0:T(8,128)} %convolution_add_fusion), kind=kOutput, calls=%fused_computation.30 | convolution fusion | flops 7408705536 | bytes 24608768 | tf_op jit(solution)/shard_map/dot_general | solution.py:21
  432.4 10.5 %fusion.98 = f32[1472,1152]{1,0:T(8,128)S(1)} fusion(bf16[1472,1920]{1,0:T(8,128)(2,1)S(1)} %bitcast.73, bf16[1152,1920]{1,0:T(8,128)(2,1)} %all-gather.3.cloned.1.call-done), kind=kOutput, calls=%fused_computation.189 | convolution fusion | flops 6511656960 | bytes 16859136 | tf_op jit(solution)/shard_map/dot_general | solution.py:21
  449.3 3.9 constant_dynamic-slice_fusion.1
  456.0 27.0 %collective-permute-done.8 = bf16[2,368,1152]{2,1,0:T(8,128)(2,1)S(1)} collective-permute-done((bf16[2,368,1152]{2,1,0:T(8,128)(2,1)S(1)}, bf16[2,368,1152]{2,1,0:T(8,128)(2,1)S(1)}, u32[]{:S(2)}, u32[]{:S(2)}) %collective-permute-start.8) | collective-permute-done | bytes 1695776 | tf_op jit(solution)/shard_map/ppermute | solution.py:184
  488.2 30.3 %collective-permute-done.9 = f32[6,1152]{1,0:T(8,128)S(1)} collective-permute-done((f32[6,1152]{1,0:T(8,128)S(1)}, f32[6,1152]{1,0:T(8,128)S(1)}, u32[]{:S(2)}, u32[]{:S(2)}) %collective-permute-start.9) | collective-permute-done | bytes 27680 | tf_op jit(solution)/shard_map/ppermute | solution.py:194
  518.6 15.1 %fusion.68 = bf16[365,2,1152]{2,1,0:T(2,128)(2,1)} fusion(f32[1152]{0:T(1024)S(1)} %copy-done.18, bf16[2,368,1152]{2,0,1:T(2,128)(2,1)} %collective-permute-done.4, f32[2,365,1152]{2,1,0:T(8,128)} %bitcast.79, f32[2,365,1152]{2,1,0:T(8,128)} %bitcast.80, pred[2,365]{0,1:T(8,128)(4,1)S(1)} %copy.75), kind=kLoop, calls=%fused_computation.113 | loop fusion | flops 5045760 | bytes 10096858 | tf_op jit(solution)/shard_map/transpose | solution.py:333
  534.6 4.1 collective-permute-done.11
  554.1 25.1 %reduce-scatter.5.cloned.1.call-done = bf16[72,4352]{1,0:T(8,128)(2,1)} async-done(((bf16[1152,4352]{1,0:T(8,128)(2,1)}), bf16[72,4352]{1,0:T(8,128)(2,1)}) %reduce-scatter.5.cloned.1.call-update) | async-done | bytes 626704 | tf_op jit(solution)/shard_map/reduce_scatter | solution.py:296
  (198 shorter events, 96.0 us)
Async XLA Ops:
  7.2 11.0 %copy-start.12 = (bf16[365,2,1152]{2,1,0:T(2,128)(2,1)S(1)}, bf16[365,2,1152]{2,1,0:T(2,128)(2,1)}, u32[]{:S(2)}) copy-start(bf16[365,2,1152]{2,1,0:T(2,128)(2,1)} %param.12) | copy-start | bytes 5045764
  7.2 61.8 %all-gather.3.cloned.1.call-start = ((), (), s32[]{:S(2)}) async-start(), calls=%async_computation.2 | async-start | bytes 4700160 | tf_op jit(solution)/shard_map/all_gather | solution.py:230
  9.4 159.3 %all-gather.5.cloned.1.call-start = ((), (), s32[]{:S(2)}) async-start(), calls=%async_computation.3 | async-start | bytes 13787136 | tf_op jit(solution)/shard_map/all_gather | solution.py:236
  10.3 5.7 collective-permute-start.3
  18.1 533.0 %reduce-scatter.3.cloned.1.call-start = ((), (), s32[]{:S(2)}) async-start(), calls=%async_computation.4 | async-start | bytes 6266880 | tf_op jit(solution)/shard_map/reduce_scatter | solution.py:313
  22.6 40.2 %collective-permute-start = (bf16[2,368,1152]{2,1,0:T(8,128)(2,1)}, bf16[2,368,1152]{2,1,0:T(8,128)(2,1)}, u32[]{:S(2)}, u32[]{:S(2)}) collective-permute-start(bf16[2,368,1152]{2,1,0:T(8,128)(2,1)} %get-tuple-element.84), channel_id=1, source_target_pairs={{1,0},{0,1},{3,2},{2,3},{5,4},{4,5},{7,6},{6,7},{9,8},{8,9},{11,10... | collective-permute-start | bytes 5087240 | tf_op jit(solution)/shard_map/ppermute | solution.py:162
  31.8 87.1 %collective-permute-start.5 = (bf16[2,368,1152]{2,1,0:T(8,128)(2,1)}, bf16[2,368,1152]{2,1,0:T(8,128)(2,1)}, u32[]{:S(2)}, u32[]{:S(2)}) collective-permute-start(bf16[2,368,1152]{2,1,0:T(8,128)(2,1)} %get-tuple-element.66), channel_id=1, source_target_pairs={{1,0},{0,1},{3,2},{2,3},{5,4},{4,5},{7,6},{6,7},{9,8},{8,9},{11,10... | collective-permute-start | bytes 5087240 | tf_op jit(solution)/shard_map/ppermute | solution.py:162
  33.7 32.6 %copy-start.16 = (f32[1152]{0:T(1024)}, f32[1152]{0:T(1024)S(1)}, u32[]{:S(2)}) copy-start(f32[1152]{0:T(1024)S(1)} %get-tuple-element.60) | copy-start | bytes 13828
  96.2 15.3 %copy-start.13 = (bf16[736,640]{1,0:T(8,128)(2,1)S(1)}, bf16[736,640]{1,0:T(8,128)(2,1)}, u32[]{:S(2)}) copy-start(bf16[736,640]{1,0:T(8,128)(2,1)} %get-tuple-element.16.out_ref) | copy-start | bytes 2826244
  96.2 17.3 %copy-start.20 = (f32[2152]{0:T(1024)S(1)}, f32[2152]{0:T(1024)}, u32[]{:S(2)}) copy-start(f32[2152]{0:T(1024)} %param.22) | copy-start | bytes 25828
  96.2 17.3 %copy-start.23 = (f32[2,1152]{1,0:T(2,128)S(1)}, f32[2,1152]{1,0:T(2,128)}, u32[]{:S(2)}) copy-start(f32[2,1152]{1,0:T(2,128)} %param.20) | copy-start | bytes 27652
  111.5 23.8 %collective-permute-start.2 = (bf16[736,640]{1,0:T(8,128)(2,1)S(1)}, bf16[736,640]{1,0:T(8,128)(2,1)S(1)}, u32[]{:S(2)}, u32[]{:S(2)}) collective-permute-start(bf16[736,640]{1,0:T(8,128)(2,1)S(1)} %copy-done.13), channel_id=1, source_target_pairs={{1,0},{0,1},{3,2},{2,3},{5,4},{4,5},{7,6},{6,7},{9,8},{8,9},{11,10... | collective-permute-start | bytes 2826248 | tf_op jit(solution)/shard_map/ppermute | solution.py:162
  113.3 37.8 %collective-permute-start.1 = (bf16[736,640]{1,0:T(8,128)(2,1)}, bf16[736,640]{1,0:T(8,128)(2,1)}, u32[]{:S(2)}, u32[]{:S(2)}) collective-permute-start(bf16[736,640]{1,0:T(8,128)(2,1)} %get-tuple-element.15.out_ref), channel_id=1, source_target_pairs={{1,0},{0,1},{3,2},{2,3},{5,4},{4,5},{7,6},{6,7},{9,8},{8,9},{11,10... | collective-permute-start | bytes 2826248 | tf_op jit(solution)/shard_map/ppermute | solution.py:162
  177.1 127.3 %copy-start = (f32[1472,1152]{1,0:T(8,128)}, f32[1472,1152]{1,0:T(8,128)S(1)}, u32[]{:S(2)}) copy-start(f32[1472,1152]{1,0:T(8,128)S(1)} %get-tuple-element.94) | copy-start | bytes 20348932
  215.0 10.8 %copy-start.28 = (bf16[1472,2176]{1,0:T(8,128)(2,1)}, bf16[1472,2176]{1,0:T(8,128)(2,1)S(1)}, u32[]{:S(2)}) copy-start(bf16[1472,2176]{1,0:T(8,128)(2,1)S(1)} %get-tuple-element.77) | copy-start | bytes 19218436
  224.3 40.0 %collective-permute-start.6 = (bf16[736,1152]{1,0:T(8,128)(2,1)S(1)}, bf16[736,1152]{1,0:T(8,128)(2,1)S(1)}, u32[]{:S(2)}, u32[]{:S(2)}) collective-permute-start(bf16[736,1152]{1,0:T(8,128)(2,1)S(1)} %fusion.44), channel_id=1, source_target_pairs={{1,0},{0,1},{3,2},{2,3},{5,4},{4,5},{7,6},{6,7},{9,8},{8,9},{11,10... | collective-permute-start | bytes 5087240 | tf_op jit(solution)/shard_map/ppermute | solution.py:162
  232.8 67.1 %collective-permute-start.7 = (bf16[736,1152]{1,0:T(8,128)(2,1)S(1)}, bf16[736,1152]{1,0:T(8,128)(2,1)S(1)}, u32[]{:S(2)}, u32[]{:S(2)}) collective-permute-start(bf16[736,1152]{1,0:T(8,128)(2,1)S(1)} %fusion.47), channel_id=1, source_target_pairs={{1,0},{0,1},{3,2},{2,3},{5,4},{4,5},{7,6},{6,7},{9,8},{8,9},{11,10... | collective-permute-start | bytes 5087240 | tf_op jit(solution)/shard_map/ppermute | solution.py:162
  346.6 20.8 %copy-start.9 = (bf16[1472,1152]{1,0:T(8,128)(2,1)S(1)}, bf16[1472,1152]{1,0:T(8,128)(2,1)}, u32[]{:S(2)}) copy-start(bf16[1472,1152]{1,0:T(8,128)(2,1)} %fusion.10) | copy-start | bytes 10174468
  380.1 199.1 %reduce-scatter.5.cloned.1.call-start = ((), (), s32[]{:S(2)}) async-start(), calls=%async_computation.5 | async-start | bytes 10653696 | tf_op jit(solution)/shard_map/reduce_scatter | solution.py:296
  413.5 18.8 %slice-start.2 = ((s8[5652480]{0:T(1024)(128)(4,1)}), s8[4194304]{0:T(1024)(128)(4,1)S(1)}, s32[]{:S(2)}) async-start(s8[5652480]{0:T(1024)(128)(4,1)} %bitcast.72), calls=%async_computation.8 | async-start | bytes 8388608
  414.5 17.9 %slice-start.3 = ((s8[5652480]{0:T(1024)(128)(4,1)}), s8[1458176]{0:T(1024)(128)(4,1)S(1)}, s32[]{:S(2)}) async-start(s8[5652480]{0:T(1024)(128)(4,1)} %bitcast.72), calls=%async_computation.9 | async-start | bytes 2916352
  443.1 40.0 %collective-permute-start.8 = (bf16[2,368,1152]{2,1,0:T(8,128)(2,1)S(1)}, bf16[2,368,1152]{2,1,0:T(8,128)(2,1)S(1)}, u32[]{:S(2)}, u32[]{:S(2)}) collective-permute-start(bf16[2,368,1152]{2,1,0:T(8,128)(2,1)S(1)} %dynamic-slice_convert_fusion), channel_id=1, source_target_pairs={{0,1},{1,0},{2,3},{3,2},{4,5},{5,4},{6,7},{7,6},{8,9},{9,8},{10,11... | collective-permute-start | bytes 5087240 | tf_op jit(solution)/shard_map/ppermute | solution.py:184
  448.0 70.6 %collective-permute-start.4 = (bf16[2,368,1152]{2,0,1:T(2,128)(2,1)S(1)}, bf16[2,368,1152]{2,0,1:T(2,128)(2,1)}, u32[]{:S(2)}, u32[]{:S(2)}) collective-permute-start(bf16[2,368,1152]{2,0,1:T(2,128)(2,1)S(1)} %copy.76), channel_id=1, source_target_pairs={{0,1},{1,0},{2,3},{3,2},{4,5},{5,4},{6,7},{7,6},{8,9},{9,8},{10,11... | collective-permute-start | bytes 5087240 | tf_op jit(solution)/shard_map/ppermute | solution.py:184
  455.1 27.9 %copy-start.17 = (f32[1152]{0:T(1024)S(1)}, f32[1152]{0:T(1024)}, u32[]{:S(2)}) copy-start(f32[1152]{0:T(1024)} %copy-done.16) | copy-start | bytes 13828
  456.0 62.6 %copy-start.18 = (f32[1152]{0:T(1024)S(1)}, f32[1152]{0:T(1024)}, u32[]{:S(2)}) copy-start(f32[1152]{0:T(1024)} %get-tuple-element.64) | copy-start | bytes 13828
  486.7 31.8 %collective-permute-start.9 = (f32[6,1152]{1,0:T(8,128)S(1)}, f32[6,1152]{1,0:T(8,128)S(1)}, u32[]{:S(2)}, u32[]{:S(2)}) collective-permute-start(f32[6,1152]{1,0:T(8,128)S(1)} %stack.34), channel_id=1, source_target_pairs={{0,1},{1,0},{2,3},{3,2},{4,5},{5,4},{6,7},{7,6},{8,9},{9,8},{10,11... | collective-permute-start | bytes 82952 | tf_op jit(solution)/shard_map/ppermute | solution.py:194
  518.6 15.1 %collective-permute-start.10 = (f32[10216]{0:T(1024)S(1)}, f32[10216]{0:T(1024)S(1)}, u32[]{:S(2)}, u32[]{:S(2)}) collective-permute-start(f32[10216]{0:T(1024)S(1)} %concatenate.31), channel_id=1, source_target_pairs={{0,2},{2,0},{4,6},{6,4},{8,10},{10,8},{12,14},{14,12},{16,18},{18,... | collective-permute-start | bytes 122600 | tf_op jit(solution)/shard_map/ppermute | solution.py:194
  518.6 15.7 %copy-start.4 = (f32[736,1152]{1,0:T(8,128)S(1)}, f32[736,1152]{1,0:T(8,128)}, u32[]{:S(2)}) copy-start(f32[736,1152]{1,0:T(8,128)} %copy-done.3) | copy-start | bytes 10174468
  518.6 15.7 %copy-start.6 = (f32[736,1152]{1,0:T(8,128)S(1)}, f32[736,1152]{1,0:T(8,128)}, u32[]{:S(2)}) copy-start(f32[736,1152]{1,0:T(8,128)} %copy-done.5) | copy-start | bytes 10174468
  533.7 4.9 collective-permute-start.11
  538.7 4.0 collective-permute-start.12
  542.7 5.3 collective-permute-start.13
  (19 other events, 91.7 us)
Sparse Core Ops, SparseCore 0:
  10.7 54.2 all-gather.2
  67.3 101.3 all-gather.4
  380.2 80.6 reduce-scatter.2
  464.9 114.2 reduce-scatter.4

commit v2 on v1

--- a/solution.py
+++ b/solution.py
@@ -6,6 +6,7 @@
 from jax.experimental import pallas as pl
 from jax.experimental.pallas import tpu as pltpu
 from jax.sharding import PartitionSpec as P
+
 
 HD = 72
 epsilon = 1e-06
@@ -38,10 +39,6 @@
     first = jnp.mean(scaled, axis=-1, keepdims=True)
     second = jnp.mean(scaled * hat, axis=-1, keepdims=True)
     return inverse * (scaled - first - hat * second), hat
-
-
-def gelu_tanh(values):
-    return jax.nn.gelu(values, approximate=True)
 
 
 def window(head, colp, win):
@@ -93,13 +90,19 @@
             pl.BlockSpec((heads, size), lambda g: (0, 0)),
         ),
         compiler_params=pltpu.CompilerParams(vmem_limit_bytes=56 * 2**20),
+        cost_estimate=pl.CostEstimate(
+            flops=4 * heads * size * size * win,
+            bytes_accessed=8 * size * colp,
+            transcendentals=heads * size * size,
+        ),
         name="attention_forward",
     )(bias, qkv)
 
 
 def backward_kernel(
-    bias_ref, qkv_ref, out_ref, dout_ref, lse_ref, old_ref, dqkv_ref, *, heads, colp, win
+    bias_ref, qkv_ref, out_ref, dout_ref, lse_ref, *refs, heads, colp, win
 ):
+    dqkv_ref = refs[-1]
     scale = HD ** (-0.5)
     dqkv_ref[...] = jnp.zeros_like(dqkv_ref)
 
@@ -148,13 +151,88 @@
             pl.BlockSpec((size, colp), lambda g: (0, 0)),
             pl.BlockSpec((size, colp), lambda g: (0, 0)),
             pl.BlockSpec((heads, size), lambda g: (0, 0)),
-            pl.BlockSpec(memory_space=pl.ANY),
-        ],
+        ]
+        + [pl.BlockSpec(memory_space=pl.ANY)] * len(old),
         out_specs=pl.BlockSpec((size, 3 * colp), lambda g: (image, 0)),
-        input_output_aliases={5: 0},
+        input_output_aliases={5 + k: k for k in range(len(old))},
         compiler_params=pltpu.CompilerParams(vmem_limit_bytes=56 * 2**20),
+        cost_estimate=pl.CostEstimate(
+            flops=10 * heads * size * size * win,
+            bytes_accessed=16 * size * colp,
+            transcendentals=heads * size * size,
+        ),
         name="attention_backward",
-    )(bias, qkv, attended, d_attended, lse, old)
+    )(bias, qkv, attended, d_attended, lse, *old)
+
+
+def mlp_kernel(xn_ref, dy_ref, up_ref, down_ref, bias_ref, *refs):
+    act_ref, dpre_ref, sum_ref, y_ref, dxn_ref, y_acc, dxn_acc = refs[-7:]
+    step = pl.program_id(0)
+    root = (2.0 / jnp.pi) ** 0.5
+
+    @pl.when(step == 0)
+    def _():
+        y_acc[...] = jnp.zeros_like(y_acc)
+        dxn_acc[...] = jnp.zeros_like(dxn_acc)
+
+    up, down = up_ref[...], down_ref[...]
+    pre = dot(xn_ref[...], up, 1, 0) + bias_ref[...]
+    d_act = dot(dy_ref[...], down, 1, 0)
+    square = pre * pre
+    tanh = jnp.tanh(pre * (root + root * 0.044715 * square))
+    half = 0.5 + 0.5 * tanh
+    slope = half + (pre * (0.5 - 0.5 * tanh * tanh)) * (root + 3.0 * root * 0.044715 * square)
+    d_pre = d_act * slope
+    sum_ref[...] = jnp.sum(d_pre, axis=0, keepdims=True)
+    act = (pre * half).astype(bf)
+    d_pre = d_pre.astype(bf)
+    act_ref[...] = act
+    dpre_ref[...] = d_pre
+    y_acc[...] += dot(act, down, 1, 1)
+    dxn_acc[...] += dot(d_pre, up, 1, 1)
+
+    @pl.when(step == pl.num_programs(0) - 1)
+    def _():
+        y_ref[...] = y_acc[...].astype(bf)
+        dxn_ref[...] = dxn_acc[...].astype(bf)
+
+
+def mlp(xn, dy, weights, bias, old, image, size, tile):
+    both, width = xn.shape
+    hidp = bias.shape[1]
+    steps = hidp // tile
+    rows = pl.BlockSpec((size, width), lambda g: (image, 0))
+    wide = pl.BlockSpec((size, tile), lambda g: (image, g))
+    whole = pl.BlockSpec((size, width), lambda g: (0, 0))
+    return pl.pallas_call(
+        mlp_kernel,
+        grid=(steps,),
+        out_shape=(
+            jax.ShapeDtypeStruct((both, hidp), bf),
+            jax.ShapeDtypeStruct((both, hidp), bf),
+            jax.ShapeDtypeStruct((1, hidp), fl),
+            jax.ShapeDtypeStruct((size, width), bf),
+            jax.ShapeDtypeStruct((size, width), bf),
+        ),
+        in_specs=[
+            rows,
+            rows,
+            pl.BlockSpec((width, tile), lambda g: (0, g)),
+            pl.BlockSpec((width, tile), lambda g: (0, steps + g)),
+            pl.BlockSpec((1, tile), lambda g: (0, g)),
+        ]
+        + [pl.BlockSpec(memory_space=pl.ANY)] * len(old),
+        out_specs=(wide, wide, pl.BlockSpec((1, tile), lambda g: (0, g)), whole, whole),
+        scratch_shapes=[pltpu.VMEM((size, width), fl)] * 2,
+        input_output_aliases={5 + k: k for k in range(len(old))},
+        compiler_params=pltpu.CompilerParams(vmem_limit_bytes=56 * 2**20),
+        cost_estimate=pl.CostEstimate(
+            flops=8 * size * width * hidp,
+            bytes_accessed=4 * width * (hidp + 2 * size) + 4 * size * hidp,
+            transcendentals=size * hidp,
+        ),
+        name="mlp",
+    )(xn, dy, weights, weights, bias, *old)
 
 
 def from_others(values, parts):
@@ -194,6 +272,14 @@
         values = values + lax.ppermute(values, axis, [(j, j ^ step) for j in range(size)])
         step *= 2
     return values
+
+
+def after(values, *others):
+    return lax.optimization_barrier((values, others))[0]
+
+
+def transposed(values):
+    return dot(values, jnp.eye(values.shape[0], dtype=values.dtype), 0, 0)
 
 
 def on_device(
@@ -217,7 +303,8 @@
     hidden = up_bias.shape[0]
     heads = cols // HD
     here = w_qkv.shape[0]
-    rowp, colp, hidp = up_to(rows, 16), up_to(cols, 128), up_to(hidden, 128)
+    rowp, colp, hids, hidp = up_to(rows, 16), up_to(cols, 128), up_to(hidden, 128), up_to(hidden, 256)
+    tile = next(256 * k for k in (3, 2, 1) if hidp % (256 * k) == 0)
     size = rowp * parts
     both = images * size
 
@@ -225,6 +312,9 @@
         widths = [(0, 0)] * values.ndim
         widths[axis] = (0, n - values.shape[axis])
         return jnp.pad(values, widths)
+
+    x_own = pad_to(jnp.transpose(inputs, (1, 0, 2)), 1, rowp)
+    x_all = all_blocks(x_own, where, parts).reshape(both, width)
 
     shard_qkv = pad_to(w_qkv, 2, colp).reshape(here, 3 * colp)
     full_qkv = lax.all_gather(shard_qkv, "dp", axis=0, tiled=True)
@@ -234,8 +324,6 @@
         [pad_to(w_up, 1, hidp), pad_to(w_down.T, 1, hidp), shard_out], axis=1
     )
     full_rest = lax.all_gather(shard_rest, "dp", axis=0, tiled=True)
-    full_up = full_rest[:, :hidp]
-    full_down = full_rest[:, hidp : 2 * hidp]
     full_out = full_rest[:, 2 * hidp :]
     own_out = full_rest[:, 2 * hidp : 2 * hidp + colp]
 
@@ -245,9 +333,7 @@
     key_bias = jnp.where(valid, 0.0, -1e30).astype(fl).reshape(both, 1)
     own_valid = lax.dynamic_slice_in_dim(valid, where * rowp, rowp, 1)[:, :, None]
 
-    x_own = pad_to(jnp.transpose(inputs, (1, 0, 2)), 1, rowp)
     dy_own = pad_to(jnp.transpose(cotangent, (1, 0, 2)), 1, rowp) * own_valid.astype(bf)
-    x_all = all_blocks(x_own, where, parts).reshape(both, width)
     dy_all = all_blocks(dy_own, where, parts).reshape(both, width)
 
     xn1 = normalize(x_all.astype(fl), ln_gain[0], ln_bias[0]).astype(bf)
@@ -267,20 +353,27 @@
 
     h1 = x_all.astype(fl) + dot(joined, full_out, 1, 1) + out_bias[0]
     xn2 = normalize(h1, ln_gain[1], ln_bias[1]).astype(bf)
-    pre = dot(xn2, full_up, 1, 0) + pad_to(up_bias, 0, hidp)
-    act, pull = jax.vjp(gelu_tanh, pre)
-    act = act.astype(bf)
-    d_pre = pull(dot(dy_all, full_down, 1, 0))[0]
-    grad_b1 = jnp.sum(d_pre, axis=0)
-    d_pre_b = d_pre.astype(bf)
-
-    d_h1, d_h1_b, d_att = [], [], []
+    bias_up = pad_to(up_bias, 0, hidp)[None]
+    wide, y_parts, dxn_parts, received, grad_b1 = (), [], [], [], 0.0
+    for i in range(images):
+        act, d_pre, sums, y_part, dxn = mlp(xn2, dy_all, full_rest, bias_up, wide, i, size, tile)
+        wide = (act, d_pre)
+        grad_b1 = grad_b1 + sums[0]
+        y_parts.append(y_part)
+        dxn_parts.append(dxn)
+        received.append(from_others(dxn, parts))
+    grad_up = dot(xn2, d_pre[:, :hids], 0, 0).astype(bf)
+    grad_down = dot(dy_all, act[:, :hids], 0, 0).astype(bf)
+    mlp_grads = jnp.concatenate([grad_up, grad_down], axis=1)
+    mlp_sums = lax.psum_scatter(mlp_grads, "dp", scatter_dimension=0, tiled=True)
+
+    d_h1, d_h1_b, d_qkv = [], [], ()
     g2, c2, bo = 0.0, 0.0, 0.0
     for i in range(images):
         at = slice(i * size, (i + 1) * size)
-        part = dot(d_pre_b[at], full_up, 1, 1).astype(bf)
-        total = part.astype(fl)
-        for other in from_others(part, parts):
+        got = after(received[i], mlp_grads, *d_qkv)
+        total = dxn_parts[i].astype(fl)
+        for other in got:
             total = total + other.astype(fl)
         back, hat = normalize_back(h1[at], ln_gain[1], total)
         g2 = g2 + jnp.sum(total * hat, axis=0)
@@ -289,32 +382,26 @@
         bo = bo + jnp.sum(full, axis=0)
         d_h1.append(full)
         d_h1_b.append(full.astype(bf))
-        d_att.append(dot(d_h1_b[i], own_out, 1, 0).astype(bf))
-
-    grad_up = dot(xn2, d_pre_b, 0, 0).astype(bf)
-    grad_down = dot(dy_all, act, 0, 0).astype(bf)
-    mlp_grads = lax.psum_scatter(
-        jnp.concatenate([grad_up, grad_down], axis=1), "dp", scatter_dimension=0, tiled=True
-    )
-
-    y_part = dot(act, full_down, 1, 1).reshape(images, size, width)
+        d_att = dot(d_h1_b[i], own_out, 1, 0).astype(bf)
+        d_qkv = (
+            attention_backward(qkv, key_bias, attended[i], d_att, lses[i], d_qkv, i, size, heads),
+        )
+    (d_qkv,) = d_qkv
+
+    y_all = after(jnp.stack(y_parts), got)
     h1_own = lax.dynamic_slice_in_dim(h1.reshape(images, size, width), where * rowp, rowp, 1)
-    y_own = h1_own + sum_blocks(y_part, where, parts, rowp) + out_bias[1]
+    y_own = h1_own + sum_blocks(y_all, where, parts, rowp) + out_bias[1]
     output = jnp.where(own_valid, y_own, 0.0).astype(bf)
 
-    d_qkv = jnp.zeros((both, 3 * colp), bf)
-    for i in range(images):
-        d_qkv = attention_backward(
-            qkv, key_bias, attended[i], d_att[i], lses[i], d_qkv, i, size, heads
-        )
-    sums_qkv = jnp.sum(d_qkv.astype(fl), axis=0)
     grad_qkv = dot(xn1, d_qkv, 0, 0).astype(bf)
     grad_out = dot(jnp.concatenate(d_h1_b, axis=0), attended_all, 0, 0).astype(bf)
-    att_grads = lax.psum_scatter(
-        jnp.concatenate([grad_qkv, grad_out], axis=1), "dp", scatter_dimension=0, tiled=True
-    )
-
-    d_xn1 = sum_blocks(dot(d_qkv, full_qkv, 1, 1).reshape(images, size, width), where, parts, rowp)
+    att_grads = jnp.concatenate([grad_qkv, grad_out], axis=1)
+    att_sums = lax.psum_scatter(att_grads, "dp", scatter_dimension=0, tiled=True)
+
+    d_qkv = after(d_qkv, att_grads)
+    sums_qkv = jnp.sum(d_qkv.astype(fl), axis=0)
+    d_xn1 = dot(d_qkv, full_qkv, 1, 1).astype(bf).reshape(images, size, width)
+    d_xn1 = sum_blocks(d_xn1, where, parts, rowp)
     back, hat = normalize_back(x_own.astype(fl), ln_gain[0], d_xn1)
     g1 = jnp.sum(d_xn1 * hat, axis=(0, 1))
     c1 = jnp.sum(d_xn1, axis=(0, 1))
@@ -332,20 +419,18 @@
     def own_rows(values):
         return jnp.transpose(values[:, :rows], (1, 0, 2))
 
-    att_grads = att_grads.astype(fl)
-    mlp_grads = mlp_grads.astype(fl)
     return (
         own_rows(output),
         own_rows(d_inputs),
         pair[0:2],
         pair[2:4],
-        att_grads[:, : 3 * colp].reshape(here, 3, colp)[:, :, :cols],
+        att_sums[:, : 3 * colp].reshape(here, 3, colp)[:, :, :cols].astype(fl),
         lone[: 2 * cols].reshape(2, cols),
-        att_grads[:, 3 * colp : 3 * colp + cols].T,
+        transposed(att_sums[:, 3 * colp : 3 * colp + cols]),
         pair[4:6],
-        mlp_grads[:, :hidden],
+        mlp_sums[:, :hidden].astype(fl),
         lone[2 * cols :],
-        mlp_grads[:, hidp : hidp + hidden].T,
+        transposed(mlp_sums[:, hids : hids + hidden]),
     )
 
 

time: 598 us -> 613 us (1.025)
  matrix products: 150 us -> 80.7 us
  Pallas kernels: 71.3 us -> 131 us
  waiting for transfers between devices: 233 us -> 272 us
  local copies, waits for them, and re-layouts: 50 us -> 43.1 us
    dot_general x14 -> x11, matrix products: 150 us -> 80.7 us  [dot(): lax.dot_general(a, b, (((ca,), (cb,)), ((), ())), preferred_element_type=fl)]
    reduce_scatter x2, waiting for transfers between devices: 25.1 us -> 82.9 us  [the longest x1 82.9 us: on_device(): lax.psum_scatter(mlp_grads, 'dp', scatter_dimension=0, tiled=True)]
    pallas_call x0 -> x2, Pallas kernels: none -> 50.5 us  [mlp(): pl.pallas_call(mlp_kernel, grid=(steps,), out_shape=(jax.ShapeDtypeStruct...]
    ppermute x7, waiting for transfers between devices: 125 us -> 87.9 us  [from_others(): lax.ppermute(values, 'tensor', [((j + k) % parts, j) for j in range(parts)])]
    transpose x2, other arithmetic: 16 us -> 2.37 us  [own_rows(): return jnp.transpose(values[:, :rows], (1, 0, 2))]
    all_gather x1, waiting for transfers between devices: 17.6 us -> 31.2 us  [on_device(): full_rest = lax.all_gather(shard_rest, 'dp', axis=0, tiled=True)]
    pallas_call x2, Pallas kernels: 30 us -> 39.2 us  [attention_forward(): pl.pallas_call(functools.partial(forward_kernel, heads=heads, colp=colp,...]
    unnamed x74 -> x85, local copies, waits for them, and re-layouts: 17.3 us -> 19.4 us
  transfers between devices with their start and end apart: 18 -> 18, of which waited for: 13 -> 10; matrix products, arithmetic and copies ran while one was open for 26% -> 20% of each run, Pallas kernels for 5% -> 10%
where the time goes in v2:
time: 613 us; the launch traced here: 605 us
  waiting for transfers between devices  272 us (44%)
  Pallas kernels  131 us (21%)
  matrix products  80.7 us (13%)
  other arithmetic  48.6 us (8%)
  local copies, waits for them, and re-layouts  43.1 us (7%)
  starting transfers between devices  14.9 us (2%)
  between operations  14.8 us (2%)
    ppermute x7, waiting for transfers between devices, from_others(): lax.ppermute(values, 'tensor', [((j + k) % parts, j) for j in range(parts)])  87.9 us
    reduce_scatter x1, waiting for transfers between devices, on_device(): lax.psum_scatter(mlp_grads, 'dp', scatter_dimension=0, tiled=True)  82.9 us
    dot_general x11, matrix products, dot(): lax.dot_general(a, b, (((ca,), (cb,)), ((), ())), preferred_element_type=fl)  80.7 us
    pallas_call x2, Pallas kernels, mlp(): pl.pallas_call(mlp_kernel, grid=(steps,), out_shape=(jax.ShapeDtypeStruct...  50.5 us
    pallas_call x2, Pallas kernels, attention_backward(): pl.pallas_call(functools.partial(backward_kernel, heads=heads, colp=colp,...  41 us
    pallas_call x2, Pallas kernels, attention_forward(): pl.pallas_call(functools.partial(forward_kernel, heads=heads, colp=colp,...  39.2 us
    ppermute x5, waiting for transfers between devices, sum_everywhere(): lax.ppermute(values, axis, [(j, j ^ step) for j in range(size)])  37.2 us
    ppermute x2, waiting for transfers between devices, sum_blocks(): lax.ppermute(block(k).astype(bf), 'tensor', pairs).astype(fl)  32.1 us
  transfers between devices with their start and end apart: 18, of which 10 were waited for; matrix products, arithmetic and copies ran while one was open for 20% of the time, Pallas kernels for 10%

profile of v2, /device:TPU:0, one launch (start us, length us, event | category | flops | bytes accessed | tf_op | source)
XLA Modules:
  0.0 604.7 jit_solution(14990462745924141329)
XLA Ops:
  10.3 3.1 collective-permute-start.3
  28.1 3.7 convert_reduce_fusion.3
  33.7 29.1 %collective-permute-done = bf16[2,368,1152]{2,1,0:T(8,128)(2,1)} collective-permute-done((bf16[2,368,1152]{2,1,0:T(8,128)(2,1)}, bf16[2,368,1152]{2,1,0:T(8,128)(2,1)}, u32[]{:S(2)}, u32[]{:S(2)}) %collective-permute-start) | collective-permute-done | bytes 1695776 | tf_op jit(solution)/shard_map/ppermute | solution.py:240
  69.0 12.4 %add_convert_fusion.qkv_ref = bf16[1472,1920]{1,0:T(8,128)(2,1)} fusion(bf16[1472,1152]{1,0:T(8,128)(2,1)} %fusion.4, bf16[1152,1920]{1,0:T(8,128)(2,1)} %all-gather.3.cloned.1.call-done, f32[1920]{0:T(1024)S(1)} %add.271), kind=kOutput, calls=%fused_computation.3 | convolution fusion | flops 6517309440 | bytes 13475328 | tf_op jit(solution)/shard_map/dot_general | solution.py:22
  81.4 14.8 %attention_forward.3 = (bf16[736,640]{1,0:T(8,128)(2,1)}, f32[8,736]{1,0:T(8,128)}) custom-call(f32[1472,1]{1,0:T(8,128)} %select_n.95.bias_ref, bf16[1472,1920]{1,0:T(8,128)(2,1)} %add_convert_fusion.qkv_ref), custom_call_target="tpu_custom_call" | custom-call | flops 4437573632 | bytes 3768320 | tf_op jit(solution)/shard_map/attention_forward/pallas_call | solution.py:77
  98.0 24.4 %attention_forward.2 = (bf16[736,640]{1,0:T(8,128)(2,1)}, f32[8,736]{1,0:T(8,128)}) custom-call(f32[1472,1]{1,0:T(8,128)} %select_n.95.bias_ref, bf16[1472,1920]{1,0:T(8,128)(2,1)} %add_convert_fusion.qkv_ref), custom_call_target="tpu_custom_call" | custom-call | flops 4437573632 | bytes 3768320 | tf_op jit(solution)/shard_map/attention_forward/pallas_call | solution.py:77
  131.5 9.6 %collective-permute-done.1 = bf16[736,640]{1,0:T(8,128)(2,1)} collective-permute-done((bf16[736,640]{1,0:T(8,128)(2,1)}, bf16[736,640]{1,0:T(8,128)(2,1)}, u32[]{:S(2)}, u32[]{:S(2)}) %collective-permute-start.1) | collective-permute-done | bytes 942112 | tf_op jit(solution)/shard_map/ppermute | solution.py:240
  141.1 31.2 %all-gather.5.cloned.1.call-done.up_ref.down_ref = bf16[1152,5888]{1,0:T(8,128)(2,1)} async-done(((bf16[72,5888]{1,0:T(8,128)(2,1)}), bf16[1152,5888]{1,0:T(8,128)(2,1)}) %all-gather.5.cloned.1.call-update) | async-done | bytes 13565968 | tf_op jit(solution)/shard_map/all_gather | solution.py:326
  172.3 8.9 %fusion.79 = (f32[1472]{0:T(1024)S(1)}, f32[1472,1152]{1,0:T(8,128)S(1)}) fusion(f32[1152]{0:T(1024)S(1)} %get-tuple-element.89, bf16[1152,5888]{1,0:T(8,128)(2,1)} %all-gather.5.cloned.1.call-done.up_ref.down_ref, bf16[736,640]{1,0:T(8,128)(2,1)} %collective-permute-done.2, bf16[736,640]{1,0:T(8,128)(2,1)S(1)} %copy-done.32, ...), kind=kOutput, calls=%fused_computation.171 | convolution fusion | flops 4362959360 | bytes 16902400 | tf_op jit(solution)/shard_map/dot_general | solution.py:22
  185.0 25.1 %mlp.2 = (bf16[1472,2304]{1,0:T(8,128)(2,1)}, bf16[1472,2304]{1,0:T(8,128)(2,1)}, f32[1,2304]{1,0:T(1,128)}, bf16[736,1152]{1,0:T(8,128)(2,1)}, bf16[736,1152]{1,0:T(8,128)(2,1)}) custom-call(bf16[1472,1152]{1,0:T(8,128)(2,1)} %add_convert_fusion.1.xn_ref, bf16[1472,1152]{1,0:T(8,128)(2,1)} %bitcast.6.dy_ref, ...), custom_call_target="tpu_custom_call" | custom-call | flops 15627976704 | bytes 24182784 | tf_op jit(solution)/shard_map/mlp/pallas_call | solution.py:207
  210.1 25.4 %mlp.3 = (bf16[1472,2304]{1,0:T(8,128)(2,1)}, bf16[1472,2304]{1,0:T(8,128)(2,1)}, f32[1,2304]{1,0:T(1,128)}, bf16[736,1152]{1,0:T(8,128)(2,1)}, bf16[736,1152]{1,0:T(8,128)(2,1)}) custom-call(bf16[1472,1152]{1,0:T(8,128)(2,1)} %add_convert_fusion.1.xn_ref, bf16[1472,1152]{1,0:T(8,128)(2,1)} %bitcast.6.dy_ref, ...), custom_call_target="tpu_custom_call", output_to_operand_aliasing={{0}: (5, {}), {1}: (6, {})} | custom-call | flops 15627976704 | bytes 24182784 | tf_op jit(solution)/shard_map/mlp/pallas_call | solution.py:207
  237.0 12.2 %convolution_convert_fusion = bf16[1152,2176]{1,0:T(8,128)(2,1)S(1)} fusion(bf16[1472,1152]{1,0:T(8,128)(2,1)} %bitcast.6.dy_ref, bf16[1472,2304]{1,0:T(8,128)(2,1)} %get-tuple-element.37), kind=kOutput, calls=%fused_computation | convolution fusion | flops 7382384640 | bytes 14811136 | tf_op jit(solution)/shard_map/dot_general | solution.py:22
  249.2 9.8 %convolution_convert_fusion.1 = bf16[1152,2176]{1,0:T(8,128)(2,1)S(1)} fusion(bf16[1472,1152]{1,0:T(8,128)(2,1)S(1)} %copy-done.12, bf16[1472,2304]{1,0:T(8,128)(2,1)S(1)} %copy-done.34), kind=kOutput, calls=%fused_computation.1 | convolution fusion | flops 7382384640 | bytes 14811136 | tf_op jit(solution)/shard_map/dot_general | solution.py:22
  260.4 4.5 pad_maximum_fusion
  264.9 46.5 %collective-permute-done.6 = bf16[736,1152]{1,0:T(8,128)(2,1)} collective-permute-done((bf16[736,1152]{1,0:T(8,128)(2,1)}, bf16[736,1152]{1,0:T(8,128)(2,1)}, u32[]{:S(2)}, u32[]{:S(2)}) %collective-permute-start.6) | collective-permute-done | bytes 1695776 | tf_op jit(solution)/shard_map/ppermute | solution.py:240
  311.4 5.1 multiply_reduce_fusion.3
  316.6 3.3 fusion.72
  320.1 5.0 convolution_convert_fusion.5.dout_ref
  325.1 20.4 %attention_backward.2.refs_0_ = bf16[1472,1920]{1,0:T(8,128)(2,1)} custom-call(f32[1472,1]{1,0:T(8,128)} %select_n.95.bias_ref, bf16[1472,1920]{1,0:T(8,128)(2,1)} %add_convert_fusion.qkv_ref, bf16[736,640]{1,0:T(8,128)(2,1)} %get-tuple-element.29.out_ref, bf16[736,640]{1,0:T(8,128)(2,1)} %convolution_convert_fusion.5.dout_ref, ...), custom_call_target="tpu_custom_call" | custom-call | flops 11093934080 | bytes 7536640 | tf_op jit(solution)/shard_map/attention_backward/pallas_call | solution.py:144
  345.6 3.7 multiply_reduce_fusion.2
  349.3 3.3 fusion.71
  355.6 3.0 fusion.28
  358.6 3.9 convolution_convert_fusion.4.dout_ref
  362.6 20.5 %attention_backward.3 = bf16[1472,1920]{1,0:T(8,128)(2,1)} custom-call(f32[1472,1]{1,0:T(8,128)} %select_n.95.bias_ref, bf16[1472,1920]{1,0:T(8,128)(2,1)} %add_convert_fusion.qkv_ref, bf16[736,640]{1,0:T(8,128)(2,1)} %get-tuple-element.30.out_ref, bf16[736,640]{1,0:T(8,128)(2,1)} %convolution_convert_fusion.4.dout_ref, ...), custom_call_target="tpu_custom_call", output_to_operand_aliasing={{}: (5, {})} | custom-call | flops 11093934080 | bytes 7536640 | tf_op jit(solution)/shard_map/attention_backward/pallas_call | solution.py:144
  383.1 9.6 %convolution_convert_fusion.2 = bf16[1152,1920]{1,0:T(8,128)(2,1)S(1)} fusion(bf16[1472,1152]{1,0:T(8,128)(2,1)S(1)} %copy-done.13, bf16[1472,1920]{1,0:T(8,128)(2,1)} %attention_backward.3), kind=kOutput, calls=%fused_computation.7 | convolution fusion | flops 6513868800 | bytes 13467648 | tf_op jit(solution)/shard_map/dot_general | solution.py:22
  392.7 3.0 pad_maximum_fusion.1
  398.1 11.9 %convolution_convert_fusion.3 = bf16[1472,1152]{1,0:T(8,128)(2,1)S(1)} fusion(bf16[1472,1920]{1,0:T(8,128)(2,1)} %attention_backward.3, bf16[1152,1920]{1,0:T(8,128)(2,1)} %all-gather.3.cloned.1.call-done), kind=kOutput, calls=%fused_computation.8 | convolution fusion | flops 6513352704 | bytes 13467648 | tf_op jit(solution)/shard_map/dot_general | solution.py:22
  418.1 32.1 %collective-permute-done.8 = bf16[2,368,1152]{2,1,0:T(8,128)(2,1)S(1)} collective-permute-done((bf16[2,368,1152]{2,1,0:T(8,128)(2,1)S(1)}, bf16[2,368,1152]{2,1,0:T(8,128)(2,1)S(1)}, u32[]{:S(2)}, u32[]{:S(2)}) %collective-permute-start.8) | collective-permute-done | bytes 1695776 | tf_op jit(solution)/shard_map/ppermute | solution.py:262
  450.2 3.6 fusion.37
  455.2 30.3 %collective-permute-done.9 = f32[6,1152]{1,0:T(8,128)S(1)} collective-permute-done((f32[6,1152]{1,0:T(8,128)S(1)}, f32[6,1152]{1,0:T(8,128)S(1)}, u32[]{:S(2)}, u32[]{:S(2)}) %collective-permute-start.9) | collective-permute-done | bytes 27680 | tf_op jit(solution)/shard_map/ppermute | solution.py:272
  488.8 4.0 collective-permute-done.11
  511.1 82.9 %reduce-scatter.5.cloned.1.call-done = bf16[72,4352]{1,0:T(8,128)(2,1)} async-done(((bf16[1152,4352]{1,0:T(8,128)(2,1)}), bf16[72,4352]{1,0:T(8,128)(2,1)}) %reduce-scatter.5.cloned.1.call-update) | async-done | bytes 626704 | tf_op jit(solution)/shard_map/reduce_scatter | solution.py:368
  (208 shorter events, 83.5 us)
Async XLA Ops:
  7.2 11.0 %copy-start.18 = (bf16[365,2,1152]{2,1,0:T(2,128)(2,1)S(1)}, bf16[365,2,1152]{2,1,0:T(2,128)(2,1)}, u32[]{:S(2)}) copy-start(bf16[365,2,1152]{2,1,0:T(2,128)(2,1)} %param.12) | copy-start | bytes 5045764
  7.2 61.9 %all-gather.3.cloned.1.call-start = ((), (), s32[]{:S(2)}) async-start(), calls=%async_computation.2 | async-start | bytes 4700160 | tf_op jit(solution)/shard_map/all_gather | solution.py:320
  9.4 162.9 %all-gather.5.cloned.1.call-start = ((), (), s32[]{:S(2)}) async-start(), calls=%async_computation.3 | async-start | bytes 14413824 | tf_op jit(solution)/shard_map/all_gather | solution.py:326
  10.3 5.7 collective-permute-start.3
  18.1 489.2 %reduce-scatter.3.cloned.1.call-start = ((), (), s32[]{:S(2)}) async-start(), calls=%async_computation.4 | async-start | bytes 6266880 | tf_op jit(solution)/shard_map/reduce_scatter | solution.py:399
  22.6 40.2 %collective-permute-start = (bf16[2,368,1152]{2,1,0:T(8,128)(2,1)}, bf16[2,368,1152]{2,1,0:T(8,128)(2,1)}, u32[]{:S(2)}, u32[]{:S(2)}) collective-permute-start(bf16[2,368,1152]{2,1,0:T(8,128)(2,1)} %get-tuple-element.105), channel_id=1, source_target_pairs={{1,0},{0,1},{3,2},{2,3},{5,4},{4,5},{7,6},{6,7},{9,8},{8,9},{11,10... | collective-permute-start | bytes 5087240 | tf_op jit(solution)/shard_map/ppermute | solution.py:240
  24.5 9.1 %copy-start.24 = (f32[2,1152]{1,0:T(2,128)S(1)}, f32[2,1152]{1,0:T(2,128)}, u32[]{:S(2)}) copy-start(f32[2,1152]{1,0:T(2,128)} %param.16) | copy-start | bytes 27652
  24.5 9.2 %copy-start.25 = (f32[2,1152]{1,0:T(2,128)S(1)}, f32[2,1152]{1,0:T(2,128)}, u32[]{:S(2)}) copy-start(f32[2,1152]{1,0:T(2,128)} %param.15) | copy-start | bytes 27652
  31.8 96.9 %collective-permute-start.4 = (bf16[2,368,1152]{2,1,0:T(8,128)(2,1)}, bf16[2,368,1152]{2,1,0:T(8,128)(2,1)}, u32[]{:S(2)}, u32[]{:S(2)}) collective-permute-start(bf16[2,368,1152]{2,1,0:T(8,128)(2,1)} %get-tuple-element.91), channel_id=1, source_target_pairs={{1,0},{0,1},{3,2},{2,3},{5,4},{4,5},{7,6},{6,7},{9,8},{8,9},{11,10... | collective-permute-start | bytes 5087240 | tf_op jit(solution)/shard_map/ppermute | solution.py:240
  33.7 32.6 %copy-start.19 = (f32[1152]{0:T(1024)}, f32[1152]{0:T(1024)S(1)}, u32[]{:S(2)}) copy-start(f32[1152]{0:T(1024)S(1)} %get-tuple-element.85) | copy-start | bytes 13828
  96.2 26.5 %copy-start.23 = (f32[2152]{0:T(1024)S(1)}, f32[2152]{0:T(1024)}, u32[]{:S(2)}) copy-start(f32[2152]{0:T(1024)} %param.22) | copy-start | bytes 25828
  96.2 27.1 %copy-start.26 = (f32[2,1152]{1,0:T(2,128)S(1)}, f32[2,1152]{1,0:T(2,128)}, u32[]{:S(2)}) copy-start(f32[2,1152]{1,0:T(2,128)} %param.20) | copy-start | bytes 27652
  96.2 35.3 %collective-permute-start.2 = (bf16[736,640]{1,0:T(8,128)(2,1)}, bf16[736,640]{1,0:T(8,128)(2,1)}, u32[]{:S(2)}, u32[]{:S(2)}) collective-permute-start(bf16[736,640]{1,0:T(8,128)(2,1)} %get-tuple-element.30.out_ref), channel_id=1, source_target_pairs={{1,0},{0,1},{3,2},{2,3},{5,4},{4,5},{7,6},{6,7},{9,8},{8,9},{11,10... | collective-permute-start | bytes 2826248 | tf_op jit(solution)/shard_map/ppermute | solution.py:240
  122.4 18.7 %collective-permute-start.1 = (bf16[736,640]{1,0:T(8,128)(2,1)}, bf16[736,640]{1,0:T(8,128)(2,1)}, u32[]{:S(2)}, u32[]{:S(2)}) collective-permute-start(bf16[736,640]{1,0:T(8,128)(2,1)} %get-tuple-element.29.out_ref), channel_id=1, source_target_pairs={{1,0},{0,1},{3,2},{2,3},{5,4},{4,5},{7,6},{6,7},{9,8},{8,9},{11,10... | collective-permute-start | bytes 2826248 | tf_op jit(solution)/shard_map/ppermute | solution.py:240
  125.8 46.5 %copy-start.32 = (bf16[736,640]{1,0:T(8,128)(2,1)S(1)}, bf16[736,640]{1,0:T(8,128)(2,1)}, u32[]{:S(2)}) copy-start(bf16[736,640]{1,0:T(8,128)(2,1)} %get-tuple-element.30.out_ref) | copy-start | bytes 2826244
  181.2 78.5 %copy-start = (f32[1472,1152]{1,0:T(8,128)}, f32[1472,1152]{1,0:T(8,128)S(1)}, u32[]{:S(2)}) copy-start(f32[1472,1152]{1,0:T(8,128)S(1)} %get-tuple-element.115) | copy-start | bytes 20348932
  235.5 110.1 %collective-permute-start.5 = (bf16[736,1152]{1,0:T(8,128)(2,1)}, bf16[736,1152]{1,0:T(8,128)(2,1)}, u32[]{:S(2)}, u32[]{:S(2)}) collective-permute-start(bf16[736,1152]{1,0:T(8,128)(2,1)} %get-tuple-element.35), channel_id=1, source_target_pairs={{1,0},{0,1},{3,2},{2,3},{5,4},{4,5},{7,6},{6,7},{9,8},{8,9},{11,10... | collective-permute-start | bytes 5087240 | tf_op jit(solution)/shard_map/ppermute | solution.py:240
  237.0 12.2 %copy-start.12 = (bf16[1472,1152]{1,0:T(8,128)(2,1)S(1)}, bf16[1472,1152]{1,0:T(8,128)(2,1)}, u32[]{:S(2)}) copy-start(bf16[1472,1152]{1,0:T(8,128)(2,1)} %add_convert_fusion.1.xn_ref) | copy-start | bytes 10174468
  237.0 12.2 %copy-start.34 = (bf16[1472,2304]{1,0:T(8,128)(2,1)S(1)}, bf16[1472,2304]{1,0:T(8,128)(2,1)}, u32[]{:S(2)}) copy-start(bf16[1472,2304]{1,0:T(8,128)(2,1)} %get-tuple-element.36) | copy-start | bytes 20348932
  259.1 52.3 %collective-permute-start.6 = (bf16[736,1152]{1,0:T(8,128)(2,1)}, bf16[736,1152]{1,0:T(8,128)(2,1)}, u32[]{:S(2)}, u32[]{:S(2)}) collective-permute-start(bf16[736,1152]{1,0:T(8,128)(2,1)} %get-tuple-element.38), channel_id=1, source_target_pairs={{1,0},{0,1},{3,2},{2,3},{5,4},{4,5},{7,6},{6,7},{9,8},{8,9},{11,10... | collective-permute-start | bytes 5087240 | tf_op jit(solution)/shard_map/ppermute | solution.py:240
  264.9 51.7 %copy-start.1 = (f32[1472,1152]{1,0:T(8,128)S(1)}, f32[1472,1152]{1,0:T(8,128)}, u32[]{:S(2)}) copy-start(f32[1472,1152]{1,0:T(8,128)} %copy-done) | copy-start | bytes 20348932
  362.6 20.5 %copy-start.13 = (bf16[1472,1152]{1,0:T(8,128)(2,1)S(1)}, bf16[1472,1152]{1,0:T(8,128)(2,1)}, u32[]{:S(2)}) copy-start(bf16[1472,1152]{1,0:T(8,128)(2,1)} %fusion.4) | copy-start | bytes 10174468
  395.8 198.2 %reduce-scatter.5.cloned.1.call-start = ((), (), s32[]{:S(2)}) async-start(), calls=%async_computation.5 | async-start | bytes 10653696 | tf_op jit(solution)/shard_map/reduce_scatter | solution.py:368
  410.2 40.0 %collective-permute-start.8 = (bf16[2,368,1152]{2,1,0:T(8,128)(2,1)S(1)}, bf16[2,368,1152]{2,1,0:T(8,128)(2,1)S(1)}, u32[]{:S(2)}, u32[]{:S(2)}) collective-permute-start(bf16[2,368,1152]{2,1,0:T(8,128)(2,1)S(1)} %constant_dynamic-slice_fusion.1), channel_id=1, source_target_pairs={{0,1},{1,0},{2,3},{3,2},{4,5},{5,4},{6,7},{7,6},{8,9},{9,8},{10,11... | collective-permute-start | bytes 5087240 | tf_op jit(solution)/shard_map/ppermute | solution.py:262
  415.8 34.4 %copy-start.20 = (f32[1152]{0:T(1024)S(1)}, f32[1152]{0:T(1024)}, u32[]{:S(2)}) copy-start(f32[1152]{0:T(1024)} %copy-done.19) | copy-start | bytes 13828
  415.8 82.0 %collective-permute-start.7 = (bf16[2,368,1152]{2,1,0:T(8,128)(2,1)}, bf16[2,368,1152]{2,1,0:T(8,128)(2,1)S(1)}, u32[]{:S(2)}, u32[]{:S(2)}) collective-permute-start(bf16[2,368,1152]{2,1,0:T(8,128)(2,1)} %constant_dynamic-slice_fusion), channel_id=1, source_target_pairs={{0,1},{1,0},{2,3},{3,2},{4,5},{5,4},{6,7},{7,6},{8,9},{9,8},{10,11... | collective-permute-start | bytes 5087240 | tf_op jit(solution)/shard_map/ppermute | solution.py:262
  453.8 31.7 %collective-permute-start.9 = (f32[6,1152]{1,0:T(8,128)S(1)}, f32[6,1152]{1,0:T(8,128)S(1)}, u32[]{:S(2)}, u32[]{:S(2)}) collective-permute-start(f32[6,1152]{1,0:T(8,128)S(1)} %stack.46), channel_id=1, source_target_pairs={{0,1},{1,0},{2,3},{3,2},{4,5},{5,4},{6,7},{7,6},{8,9},{9,8},{10,11... | collective-permute-start | bytes 82952 | tf_op jit(solution)/shard_map/ppermute | solution.py:272
  485.7 2.8 collective-permute-start.10
  485.7 12.1 %slice-start = ((s8[6782976]{0:T(1024)(128)(4,1)}), s8[4194304]{0:T(1024)(128)(4,1)S(1)}, s32[]{:S(2)}) async-start(s8[6782976]{0:T(1024)(128)(4,1)} %bitcast.61), calls=%async_computation.6 | async-start | bytes 8388608
  488.5 4.3 collective-permute-start.11
  492.8 4.0 collective-permute-start.12
  496.8 7.4 %collective-permute-start.13 = (f32[10216]{0:T(1024)S(1)}, f32[10216]{0:T(1024)S(1)}, u32[]{:S(2)}, u32[]{:S(2)}) collective-permute-start(f32[10216]{0:T(1024)S(1)} %add.304), channel_id=1, source_target_pairs={{0,16},{2,18},{4,20},{6,22},{8,24},{10,26},{12,28},{14,30},{16,0},... | collective-permute-start | bytes 122600 | tf_op jit(solution)/shard_map/ppermute | solution.py:272
  (25 other events, 96.5 us)
Sparse Core Ops, SparseCore 0:
  10.7 54.2 all-gather.2
  67.2 105.0 all-gather.4
  395.9 80.5 reduce-scatter.2
  480.5 113.4 reduce-scatter.4

commit v3 on v2

--- a/solution.py
+++ b/solution.py
@@ -242,9 +242,10 @@
     ]
 
 
-def all_blocks(values, where, parts):
+def all_blocks(values, got, where):
     images, rows, width = values.shape
-    got = [values] + from_others(values, parts)
+    got = [values] + got
+    parts = len(got)
     full = jnp.zeros((images, rows * parts, width), values.dtype)
     for k, block in enumerate(got):
         start = (where + k) % parts * rows
@@ -261,6 +262,32 @@
         pairs = [(j, (j + k) % parts) for j in range(parts)]
         total = total + lax.ppermute(block(k).astype(bf), "tensor", pairs).astype(fl)
     return total
+
+
+def gather_by_halves(values, axis):
+    size = lax.axis_size(axis)
+    rows, width = values.shape
+    if size & (size - 1):
+        return lax.all_gather(values, axis, axis=0, tiled=True)
+    have = values[None]
+    step = size // 2
+    while step:
+        got = lax.ppermute(have, axis, [(j, j ^ step) for j in range(size)])
+        first = lax.axis_index(axis) // step % 2 == 0
+        low, high = jnp.where(first, have, got), jnp.where(first, got, have)
+        have = jnp.stack([low, high], axis=1).reshape(-1, rows, width)
+        step //= 2
+    return have.reshape(-1, width)
+
+
+def exchange_half(values, axis, step):
+    size = lax.axis_size(axis)
+    blocks, rows, width = values.shape
+    split = values.reshape(blocks // 2, 2, rows, width)
+    mine = lax.axis_index(axis) // step % 2
+    send = lax.dynamic_index_in_dim(split, 1 - mine, 1, False)
+    keep = lax.dynamic_index_in_dim(split, mine, 1, False)
+    return keep, lax.ppermute(send, axis, [(j, j ^ step) for j in range(size)])
 
 
 def sum_everywhere(values, axis):
@@ -314,18 +341,16 @@
         return jnp.pad(values, widths)
 
     x_own = pad_to(jnp.transpose(inputs, (1, 0, 2)), 1, rowp)
-    x_all = all_blocks(x_own, where, parts).reshape(both, width)
+    x_all = all_blocks(x_own, from_others(x_own, parts), where).reshape(both, width)
 
     shard_qkv = pad_to(w_qkv, 2, colp).reshape(here, 3 * colp)
     full_qkv = lax.all_gather(shard_qkv, "dp", axis=0, tiled=True)
     shard_out = pad_to(w_out.T, 1, colp)
     shard_out = jnp.concatenate([shard_out] + from_others(shard_out, parts), axis=1)
-    shard_rest = jnp.concatenate(
-        [pad_to(w_up, 1, hidp), pad_to(w_down.T, 1, hidp), shard_out], axis=1
-    )
-    full_rest = lax.all_gather(shard_rest, "dp", axis=0, tiled=True)
-    full_out = full_rest[:, 2 * hidp :]
-    own_out = full_rest[:, 2 * hidp : 2 * hidp + colp]
+    shard_mlp = jnp.concatenate([pad_to(w_up, 1, hidp), pad_to(w_down.T, 1, hidp)], axis=1)
+    full_mlp = lax.all_gather(shard_mlp, "dp", axis=0, tiled=True)
+    full_out = gather_by_halves(shard_out, "dp")
+    own_out = full_out[:, :colp]
 
     place = jnp.arange(size, dtype=jnp.int32)
     position = place // rowp * rows + place % rowp
@@ -334,7 +359,7 @@
     own_valid = lax.dynamic_slice_in_dim(valid, where * rowp, rowp, 1)[:, :, None]
 
     dy_own = pad_to(jnp.transpose(cotangent, (1, 0, 2)), 1, rowp) * own_valid.astype(bf)
-    dy_all = all_blocks(dy_own, where, parts).reshape(both, width)
+    dy_others = from_others(dy_own, parts)
 
     xn1 = normalize(x_all.astype(fl), ln_gain[0], ln_bias[0]).astype(bf)
     bias_three = pad_to(
@@ -348,6 +373,8 @@
         attended.append(out)
         lses.append(lse)
         joined.append(jnp.concatenate([out] + from_others(out, parts), axis=1))
+    dy_others = after(dy_others, *attended)
+    dy_all = all_blocks(dy_own, dy_others, where).reshape(both, width)
     joined = jnp.concatenate(joined, axis=0)
     attended_all = jnp.concatenate(attended, axis=0)
 
@@ -356,22 +383,44 @@
     bias_up = pad_to(up_bias, 0, hidp)[None]
     wide, y_parts, dxn_parts, received, grad_b1 = (), [], [], [], 0.0
     for i in range(images):
-        act, d_pre, sums, y_part, dxn = mlp(xn2, dy_all, full_rest, bias_up, wide, i, size, tile)
+        act, d_pre, sums, y_part, dxn = mlp(
+            xn2, dy_all, full_mlp, bias_up, wide, i, size, tile
+        )
         wide = (act, d_pre)
         grad_b1 = grad_b1 + sums[0]
         y_parts.append(y_part)
         dxn_parts.append(dxn)
         received.append(from_others(dxn, parts))
+    grad_down = dot(dy_all, act[:, :hids], 0, 0).astype(bf)
+    down_sums = lax.psum_scatter(grad_down, "dp", scatter_dimension=0, tiled=True)
+    down_sums = lax.optimization_barrier(down_sums)
+    d_pre = after(d_pre, grad_down)
     grad_up = dot(xn2, d_pre[:, :hids], 0, 0).astype(bf)
-    grad_down = dot(dy_all, act[:, :hids], 0, 0).astype(bf)
-    mlp_grads = jnp.concatenate([grad_up, grad_down], axis=1)
-    mlp_sums = lax.psum_scatter(mlp_grads, "dp", scatter_dimension=0, tiled=True)
+    ring = lax.axis_size("dp")
+    halving = not ring & (ring - 1)
+    if halving:
+        up_sums, step = grad_up.reshape(ring, here, hids), 1
+        pending = exchange_half(up_sums, "dp", step)
+    else:
+        up_sums, step, pending = lax.psum_scatter(grad_up, "dp", tiled=True), ring, ()
+
+    def next_half(pending, step, *others):
+        if not halving or step == ring:
+            return pending, step
+        keep, got = pending
+        if others:
+            got = after(got, *others)
+        total = (keep.astype(fl) + got.astype(fl)).astype(bf)
+        step *= 2
+        if step == ring:
+            return total, step
+        return exchange_half(total, "dp", step), step
 
     d_h1, d_h1_b, d_qkv = [], [], ()
     g2, c2, bo = 0.0, 0.0, 0.0
     for i in range(images):
         at = slice(i * size, (i + 1) * size)
-        got = after(received[i], mlp_grads, *d_qkv)
+        got = after(received[i], grad_up, grad_down, *d_qkv)
         total = dxn_parts[i].astype(fl)
         for other in got:
             total = total + other.astype(fl)
@@ -386,6 +435,7 @@
         d_qkv = (
             attention_backward(qkv, key_bias, attended[i], d_att, lses[i], d_qkv, i, size, heads),
         )
+        pending, step = next_half(pending, step, *d_qkv)
     (d_qkv,) = d_qkv
 
     y_all = after(jnp.stack(y_parts), got)
@@ -398,6 +448,7 @@
     att_grads = jnp.concatenate([grad_qkv, grad_out], axis=1)
     att_sums = lax.psum_scatter(att_grads, "dp", scatter_dimension=0, tiled=True)
 
+    pending, step = next_half(pending, step, att_grads)
     d_qkv = after(d_qkv, att_grads)
     sums_qkv = jnp.sum(d_qkv.astype(fl), axis=0)
     d_xn1 = dot(d_qkv, full_qkv, 1, 1).astype(bf).reshape(images, size, width)
@@ -416,6 +467,11 @@
     pair = small[: 6 * width].reshape(6, width)
     lone = small[6 * width :]
 
+    while halving and step < ring:
+        pending, step = next_half(pending, step)
+    if halving:
+        up_sums = pending[0]
+
     def own_rows(values):
         return jnp.transpose(values[:, :rows], (1, 0, 2))
 
@@ -428,9 +484,9 @@
         lone[: 2 * cols].reshape(2, cols),
         transposed(att_sums[:, 3 * colp : 3 * colp + cols]),
         pair[4:6],
-        mlp_sums[:, :hidden].astype(fl),
+        up_sums[:, :hidden].astype(fl),
         lone[2 * cols :],
-        transposed(mlp_sums[:, hids : hids + hidden]),
+        transposed(down_sums)[:hidden],
     )
 
 

time: 613 us -> 540 us (0.88)
  waiting for transfers between devices: 272 us -> 175 us
  other arithmetic: 48.6 us -> 61.6 us
  local copies, waits for them, and re-layouts: 43.1 us -> 55.6 us
  starting transfers between devices: 14.9 us -> 25.3 us
  Pallas kernels: 131 us -> 123 us
    ppermute x0 -> x8, waiting for transfers between devices: none -> 93.9 us  [the longest x4 51.3 us: gather_by_halves(): got = lax.ppermute(have, axis, [(j, j ^ step) for j in range(size)])]
    reduce_scatter x1 -> x0, waiting for transfers between devices: 82.9 us -> none  [on_device(): lax.psum_scatter(mlp_grads, 'dp', scatter_dimension=0, tiled=True)]
    all_gather x1, waiting for transfers between devices: 31.2 us -> 0.01 us  [on_device(): full_mlp = lax.all_gather(shard_mlp, 'dp', axis=0, tiled=True)]
    ppermute x7, waiting for transfers between devices: 87.9 us -> 59.1 us  [from_others(): lax.ppermute(values, 'tensor', [((j + k) % parts, j) for j in range(parts)])]
    ppermute x2, waiting for transfers between devices: 32.1 us -> 5.66 us  [sum_blocks(): lax.ppermute(block(k).astype(bf), 'tensor', pairs).astype(fl)]
    ppermute x5, waiting for transfers between devices: 37.2 us -> 16.8 us  [sum_everywhere(): lax.ppermute(values, axis, [(j, j ^ step) for j in range(size)])]
    unnamed x85 -> x129, local copies, waits for them, and re-layouts: 19.4 us -> 28.9 us
    pallas_call x2, Pallas kernels: 39.2 us -> 30 us  [attention_forward(): pl.pallas_call(functools.partial(forward_kernel, heads=heads, colp=colp,...]
  transfers between devices with their start and end apart: 18 -> 26, of which waited for: 10 -> 10; matrix products, arithmetic and copies ran while one was open for 20% -> 32% of each run, Pallas kernels for 10% -> 13%
where the time goes in v3:
time: 540 us; the launch traced here: 533 us
  waiting for transfers between devices  175 us (32%)
  Pallas kernels  123 us (23%)
  matrix products  77 us (14%)
  other arithmetic  61.6 us (11%)
  local copies, waits for them, and re-layouts  55.6 us (10%)
  starting transfers between devices  25.3 us (5%)
  between operations  15.1 us (3%)
    dot_general x11, matrix products, dot(): lax.dot_general(a, b, (((ca,), (cb,)), ((), ())), preferred_element_type=fl)  77 us
    ppermute x7, waiting for transfers between devices, from_others(): lax.ppermute(values, 'tensor', [((j + k) % parts, j) for j in range(parts)])  59.1 us
    pallas_call x2, Pallas kernels, mlp(): pl.pallas_call(mlp_kernel, grid=(steps,), out_shape=(jax.ShapeDtypeStruct...  51.7 us
    ppermute x4, waiting for transfers between devices, gather_by_halves(): got = lax.ppermute(have, axis, [(j, j ^ step) for j in range(size)])  51.3 us
    ppermute x4, waiting for transfers between devices, exchange_half(): lax.ppermute(send, axis, [(j, j ^ step) for j in range(size)])  42.6 us
    pallas_call x2, Pallas kernels, attention_backward(): pl.pallas_call(functools.partial(backward_kernel, heads=heads, colp=colp,...  41 us
    pallas_call x2, Pallas kernels, attention_forward(): pl.pallas_call(functools.partial(forward_kernel, heads=heads, colp=colp,...  30 us
    unnamed x129, local copies, waits for them, and re-layouts  28.9 us
  transfers between devices with their start and end apart: 26, of which 10 were waited for; matrix products, arithmetic and copies ran while one was open for 32% of the time, Pallas kernels for 13%

profile of v3, /device:TPU:0, one launch (start us, length us, event | category | flops | bytes accessed | tf_op | source)
XLA Modules:
  0.0 532.9 jit_solution(5527957441552807059)
XLA Ops:
  11.5 3.1 collective-permute-start.3
  22.6 3.1 convert_reduce_fusion.3
  33.1 10.0 %collective-permute-done.4 = bf16[1,72,1280]{2,1,0:T(8,128)(2,1)S(1)} collective-permute-done((bf16[1,72,1280]{2,1,0:T(8,128)(2,1)S(1)}, bf16[1,72,1280]{2,1,0:T(8,128)(2,1)S(1)}, u32[]{:S(2)}, u32[]{:S(2)}) %collective-permute-start.4) | collective-permute-done | bytes 184352 | tf_op jit(solution)/shard_map/ppermute | solution.py:275
  46.3 26.2 %collective-permute-done.5 = bf16[2,72,1280]{2,1,0:T(8,128)(2,1)} collective-permute-done((bf16[2,72,1280]{2,1,0:T(8,128)(2,1)}, bf16[2,72,1280]{2,1,0:T(8,128)(2,1)}, u32[]{:S(2)}, u32[]{:S(2)}) %collective-permute-start.5) | collective-permute-done | bytes 368672 | tf_op jit(solution)/shard_map/ppermute | solution.py:275
  84.6 15.1 %collective-permute-done.6 = bf16[4,72,1280]{2,1,0:T(8,128)(2,1)} collective-permute-done((bf16[4,72,1280]{2,1,0:T(8,128)(2,1)}, bf16[4,72,1280]{2,1,0:T(8,128)(2,1)}, u32[]{:S(2)}, u32[]{:S(2)}) %collective-permute-start.6) | collective-permute-done | bytes 737312 | tf_op jit(solution)/shard_map/ppermute | solution.py:275
  106.0 3.0 fusion.4
  109.0 12.3 %add_convert_fusion.qkv_ref = bf16[1472,1920]{1,0:T(8,128)(2,1)} fusion(bf16[1472,1152]{1,0:T(8,128)(2,1)} %fusion.4, bf16[1152,1920]{1,0:T(8,128)(2,1)} %all-gather.3.cloned.1.call-done, f32[1920]{0:T(1024)S(1)} %add.335), kind=kOutput, calls=%fused_computation.3 | convolution fusion | flops 6517309440 | bytes 13475328 | tf_op jit(solution)/shard_map/dot_general | solution.py:22
  121.3 14.8 %attention_forward.3 = (bf16[736,640]{1,0:T(8,128)(2,1)}, f32[8,736]{1,0:T(8,128)}) custom-call(f32[1472,1]{1,0:T(8,128)} %select_n.237.bias_ref, bf16[1472,1920]{1,0:T(8,128)(2,1)} %add_convert_fusion.qkv_ref), custom_call_target="tpu_custom_call" | custom-call | flops 4437573632 | bytes 3768320 | tf_op jit(solution)/shard_map/attention_forward/pallas_call | solution.py:77
  137.5 15.3 %attention_forward.2 = (bf16[736,640]{1,0:T(8,128)(2,1)}, f32[8,736]{1,0:T(8,128)}) custom-call(f32[1472,1]{1,0:T(8,128)} %select_n.237.bias_ref, bf16[1472,1920]{1,0:T(8,128)(2,1)} %add_convert_fusion.qkv_ref), custom_call_target="tpu_custom_call" | custom-call | flops 4437573632 | bytes 3768320 | tf_op jit(solution)/shard_map/attention_forward/pallas_call | solution.py:77
  160.5 19.2 %collective-permute-done.1 = bf16[736,640]{1,0:T(8,128)(2,1)S(1)} collective-permute-done((bf16[736,640]{1,0:T(8,128)(2,1)}, bf16[736,640]{1,0:T(8,128)(2,1)S(1)}, u32[]{:S(2)}, u32[]{:S(2)}) %collective-permute-start.1) | collective-permute-done | bytes 942112 | tf_op jit(solution)/shard_map/ppermute | solution.py:240
  179.7 5.7 %fusion.79 = (f32[1472]{0:T(1024)S(1)}, f32[1472,1152]{1,0:T(8,128)S(1)}) fusion(f32[1152]{0:T(1024)S(1)} %get-tuple-element.121, bf16[1152,1280]{1,0:T(8,128)(2,1)S(1)} %bitcast.144, bf16[736,640]{1,0:T(8,128)(2,1)S(1)} %collective-permute-done.2, bf16[736,640]{1,0:T(8,128)(2,1)S(1)} %copy-done.53, bf16[736,640]{1,0:T(8,128)(2,1)S(1)} %collective-permute-done.1, ...), kind=kOutput, calls=%fused_computation.190 | convolution fusion | flops 4362959360 | bytes 16902400 | tf_op jit(solution)/shard_map/dot_general | solution.py:22
  190.7 25.7 %mlp.2 = (bf16[1472,2304]{1,0:T(8,128)(2,1)}, bf16[1472,2304]{1,0:T(8,128)(2,1)}, f32[1,2304]{1,0:T(1,128)}, bf16[736,1152]{1,0:T(8,128)(2,1)}, bf16[736,1152]{1,0:T(8,128)(2,1)}) custom-call(bf16[1472,1152]{1,0:T(8,128)(2,1)} %add_convert_fusion.1.xn_ref, bf16[1472,1152]{1,0:T(8,128)(2,1)} %bitcast.130, ...), custom_call_target="tpu_custom_call" | custom-call | flops 15627976704 | bytes 24182784 | tf_op jit(solution)/shard_map/mlp/pallas_call | solution.py:207
  216.5 25.9 %mlp.3 = (bf16[1472,2304]{1,0:T(8,128)(2,1)}, bf16[1472,2304]{1,0:T(8,128)(2,1)}, f32[1,2304]{1,0:T(1,128)}, bf16[736,1152]{1,0:T(8,128)(2,1)}, bf16[736,1152]{1,0:T(8,128)(2,1)}) custom-call(bf16[1472,1152]{1,0:T(8,128)(2,1)} %add_convert_fusion.1.xn_ref, bf16[1472,1152]{1,0:T(8,128)(2,1)} %bitcast.131, ...), custom_call_target="tpu_custom_call", output_to_operand_aliasing={{0}: (5, {}), {1}: (6, {})} | custom-call | flops 15627976704 | bytes 24182784 | tf_op jit(solution)/shard_map/mlp/pallas_call | solution.py:207
  243.9 12.9 %convolution_convert_fusion.1 = bf16[1152,2176]{1,0:T(8,128)(2,1)} fusion(bf16[1472,1152]{1,0:T(8,128)(2,1)S(1)} %bitcast.132, bf16[1472,2304]{1,0:T(8,128)(2,1)} %get-tuple-element.43), kind=kOutput, calls=%fused_computation.1 | convolution fusion | flops 7382384640 | bytes 14811136 | tf_op jit(solution)/shard_map/dot_general | solution.py:22
  257.6 13.2 %convolution_convert_fusion = bf16[1152,2176]{1,0:T(8,128)(2,1)S(1)} fusion(bf16[1472,1152]{1,0:T(8,128)(2,1)} %add_convert_fusion.1.xn_ref, bf16[1472,2304]{1,0:T(8,128)(2,1)} %get-tuple-element.44), kind=kOutput, calls=%fused_computation | convolution fusion | flops 7382384640 | bytes 14811136 | tf_op jit(solution)/shard_map/dot_general | solution.py:22
  277.7 39.9 %collective-permute-done.10 = bf16[736,1152]{1,0:T(8,128)(2,1)S(1)} collective-permute-done((bf16[736,1152]{1,0:T(8,128)(2,1)}, bf16[736,1152]{1,0:T(8,128)(2,1)S(1)}, u32[]{:S(2)}, u32[]{:S(2)}) %collective-permute-start.10) | collective-permute-done | bytes 1695776 | tf_op jit(solution)/shard_map/ppermute | solution.py:240
  327.6 20.5 %attention_backward.2.refs_0_ = bf16[1472,1920]{1,0:T(8,128)(2,1)} custom-call(f32[1472,1]{1,0:T(8,128)} %select_n.237.bias_ref, bf16[1472,1920]{1,0:T(8,128)(2,1)} %add_convert_fusion.qkv_ref, bf16[736,640]{1,0:T(8,128)(2,1)} %get-tuple-element.34.out_ref, bf16[736,640]{1,0:T(8,128)(2,1)} %convolution_convert_fusion.5.dout_ref, ...), custom_call_target="tpu_custom_call" | custom-call | flops 11093934080 | bytes 7536640 | tf_op jit(solution)/shard_map/attention_backward/pallas_call | solution.py:144
  352.4 3.5 multiply_reduce_fusion.2
  356.0 3.1 fusion.71
  364.6 3.0 fusion.29
  367.7 20.6 %attention_backward.3 = bf16[1472,1920]{1,0:T(8,128)(2,1)} custom-call(f32[1472,1]{1,0:T(8,128)} %select_n.237.bias_ref, bf16[1472,1920]{1,0:T(8,128)(2,1)} %add_convert_fusion.qkv_ref, bf16[736,640]{1,0:T(8,128)(2,1)} %get-tuple-element.35.out_ref, bf16[736,640]{1,0:T(8,128)(2,1)} %convolution_convert_fusion.4.dout_ref, ...), custom_call_target="tpu_custom_call", output_to_operand_aliasing={{}: (5, {})} | custom-call | flops 11093934080 | bytes 7536640 | tf_op jit(solution)/shard_map/attention_backward/pallas_call | solution.py:144
  388.3 9.6 %convolution_convert_fusion.2 = bf16[1152,1920]{1,0:T(8,128)(2,1)S(1)} fusion(bf16[1472,1152]{1,0:T(8,128)(2,1)S(1)} %copy-done.23, bf16[1472,1920]{1,0:T(8,128)(2,1)} %attention_backward.3), kind=kOutput, calls=%fused_computation.6 | convolution fusion | flops 6513868800 | bytes 13467648 | tf_op jit(solution)/shard_map/dot_general | solution.py:22
  397.9 3.0 pad_maximum_fusion
  400.9 11.4 %convolution_convert_fusion.3 = bf16[1472,1152]{1,0:T(8,128)(2,1)S(1)} fusion(bf16[1472,1920]{1,0:T(8,128)(2,1)} %attention_backward.3, bf16[1152,1920]{1,0:T(8,128)(2,1)} %all-gather.3.cloned.1.call-done), kind=kOutput, calls=%fused_computation.7 | convolution fusion | flops 6513352704 | bytes 13467648 | tf_op jit(solution)/shard_map/dot_general | solution.py:22
  415.3 3.2 fusion.7
  424.7 21.9 %collective-permute-done.19 = bf16[4,72,2176]{2,1,0:T(8,128)(2,1)S(1)} collective-permute-done((bf16[4,72,2176]{2,1,0:T(8,128)(2,1)S(1)}, bf16[4,72,2176]{2,1,0:T(8,128)(2,1)S(1)}, u32[]{:S(2)}, u32[]{:S(2)}) %collective-permute-start.19) | collective-permute-done | bytes 1253408 | tf_op jit(solution)/shard_map/ppermute | solution.py:290
  446.6 5.7 %collective-permute-done.12 = bf16[2,368,1152]{2,1,0:T(8,128)(2,1)S(1)} collective-permute-done((bf16[2,368,1152]{2,1,0:T(8,128)(2,1)}, bf16[2,368,1152]{2,1,0:T(8,128)(2,1)S(1)}, u32[]{:S(2)}, u32[]{:S(2)}) %collective-permute-start.12) | collective-permute-done | bytes 1695776 | tf_op jit(solution)/shard_map/ppermute | solution.py:263
  452.3 3.6 fusion.38
  456.6 3.3 fusion.42
  463.4 4.2 fusion.46
  472.1 16.7 %collective-permute-done.16 = f32[10216]{0:T(1024)S(1)} collective-permute-done((f32[10216]{0:T(1024)S(1)}, f32[10216]{0:T(1024)S(1)}, u32[]{:S(2)}, u32[]{:S(2)}) %collective-permute-start.16) | collective-permute-done | bytes 40896 | tf_op jit(solution)/shard_map/ppermute | solution.py:299
  498.6 20.7 %collective-permute-done.21 = bf16[1,72,2176]{2,1,0:T(8,128)(2,1)S(1)} collective-permute-done((bf16[1,72,2176]{2,1,0:T(8,128)(2,1)S(1)}, bf16[1,72,2176]{2,1,0:T(8,128)(2,1)S(1)}, u32[]{:S(2)}, u32[]{:S(2)}) %collective-permute-start.21) | collective-permute-done | bytes 313376 | tf_op jit(solution)/shard_map/ppermute | solution.py:290
  (286 shorter events, 118.7 us)
Async XLA Ops:
  7.2 101.8 %all-gather.3.cloned.1.call-start = ((), (), s32[]{:S(2)}) async-start(), calls=%async_computation.2 | async-start | bytes 4700160 | tf_op jit(solution)/shard_map/all_gather | solution.py:347
  9.4 181.3 %all-gather.5.cloned.1.call-start = ((), (), s32[]{:S(2)}) async-start(), calls=%async_computation.3 | async-start | bytes 11280384 | tf_op jit(solution)/shard_map/all_gather | solution.py:351
  11.4 508.8 %reduce-scatter.7.cloned.1.call-start = ((), (), s32[]{:S(2)}) async-start(), calls=%async_computation.5 | async-start | bytes 5326848
  11.5 18.0 %collective-permute-start.3 = (bf16[72,640]{1,0:T(8,128)(2,1)S(1)}, bf16[72,640]{1,0:T(8,128)(2,1)}, u32[]{:S(2)}, u32[]{:S(2)}) collective-permute-start(bf16[72,640]{1,0:T(8,128)(2,1)S(1)} %pad.33), channel_id=1, source_target_pairs={{1,0},{0,1},{3,2},{2,3},{5,4},{4,5},{7,6},{6,7},{9,8},{8,9},{11,10... | collective-permute-start | bytes 276488 | tf_op jit(solution)/shard_map/ppermute | solution.py:240
  18.9 83.6 %collective-permute-start = (bf16[2,368,1152]{2,1,0:T(8,128)(2,1)}, bf16[2,368,1152]{2,1,0:T(8,128)(2,1)}, u32[]{:S(2)}, u32[]{:S(2)}) collective-permute-start(bf16[2,368,1152]{2,1,0:T(8,128)(2,1)} %get-tuple-element.139), channel_id=1, source_target_pairs={{1,0},{0,1},{3,2},{2,3},{5,4},{4,5},{7,6},{6,7},{9,8},{8,9},{11,10... | collective-permute-start | bytes 5087240 | tf_op jit(solution)/shard_map/ppermute | solution.py:240
  25.7 130.2 %collective-permute-start.8 = (bf16[2,368,1152]{2,1,0:T(8,128)(2,1)}, bf16[2,368,1152]{2,1,0:T(8,128)(2,1)}, u32[]{:S(2)}, u32[]{:S(2)}) collective-permute-start(bf16[2,368,1152]{2,1,0:T(8,128)(2,1)} %get-tuple-element.123), channel_id=1, source_target_pairs={{1,0},{0,1},{3,2},{2,3},{5,4},{4,5},{7,6},{6,7},{9,8},{8,9},{11,10... | collective-permute-start | bytes 5087240 | tf_op jit(solution)/shard_map/ppermute | solution.py:240
  27.8 50.8 %copy-start.45 = (f32[2152]{0:T(1024)S(1)}, f32[2152]{0:T(1024)}, u32[]{:S(2)}) copy-start(f32[2152]{0:T(1024)} %param.22) | copy-start | bytes 25828
  30.5 12.7 %collective-permute-start.4 = (bf16[1,72,1280]{2,1,0:T(8,128)(2,1)S(1)}, bf16[1,72,1280]{2,1,0:T(8,128)(2,1)S(1)}, u32[]{:S(2)}, u32[]{:S(2)}) collective-permute-start(bf16[1,72,1280]{2,1,0:T(8,128)(2,1)S(1)} %maximum_bitcast_fusion.1), channel_id=1, source_target_pairs={{0,16},{2,18},{4,20},{6,22},{8,24},{10,26},{12,28},{14,30},{16,0},... | collective-permute-start | bytes 552968 | tf_op jit(solution)/shard_map/ppermute | solution.py:275
  33.1 48.7 %copy-start.42 = (f32[2,368]{1,0:T(2,128)}, f32[2,368]{1,0:T(2,128)S(1)}, u32[]{:S(2)}) copy-start(f32[2,368]{1,0:T(2,128)S(1)} %broadcast_multiply_fusion.10) | copy-start | bytes 8836
  45.5 27.0 %collective-permute-start.5 = (bf16[2,72,1280]{2,1,0:T(8,128)(2,1)}, bf16[2,72,1280]{2,1,0:T(8,128)(2,1)}, u32[]{:S(2)}, u32[]{:S(2)}) collective-permute-start(bf16[2,72,1280]{2,1,0:T(8,128)(2,1)} %maximum_bitcast_fusion), channel_id=1, source_target_pairs={{0,8},{2,10},{4,12},{6,14},{8,0},{10,2},{12,4},{14,6},{16,24},{18,... | collective-permute-start | bytes 1105928 | tf_op jit(solution)/shard_map/ppermute | solution.py:275
  74.7 25.0 %collective-permute-start.6 = (bf16[4,72,1280]{2,1,0:T(8,128)(2,1)}, bf16[4,72,1280]{2,1,0:T(8,128)(2,1)}, u32[]{:S(2)}, u32[]{:S(2)}) collective-permute-start(bf16[4,72,1280]{2,1,0:T(8,128)(2,1)} %bitcast.10), channel_id=1, source_target_pairs={{0,4},{2,6},{4,0},{6,2},{8,12},{10,14},{12,8},{14,10},{16,20},{18,... | collective-permute-start | bytes 2211848 | tf_op jit(solution)/shard_map/ppermute | solution.py:275
  102.5 50.9 %collective-permute-start.7 = (bf16[8,72,1280]{2,1,0:T(8,128)(2,1)}, bf16[8,72,1280]{2,1,0:T(8,128)(2,1)}, u32[]{:S(2)}, u32[]{:S(2)}) collective-permute-start(bf16[8,72,1280]{2,1,0:T(8,128)(2,1)} %bitcast.13), channel_id=1, source_target_pairs={{0,2},{2,0},{4,6},{6,4},{8,10},{10,8},{12,14},{14,12},{16,18},{18,... | collective-permute-start | bytes 4423688 | tf_op jit(solution)/shard_map/ppermute | solution.py:275
  136.1 24.4 %collective-permute-start.2 = (bf16[736,640]{1,0:T(8,128)(2,1)}, bf16[736,640]{1,0:T(8,128)(2,1)S(1)}, u32[]{:S(2)}, u32[]{:S(2)}) collective-permute-start(bf16[736,640]{1,0:T(8,128)(2,1)} %get-tuple-element.35.out_ref), channel_id=1, source_target_pairs={{1,0},{0,1},{3,2},{2,3},{5,4},{4,5},{7,6},{6,7},{9,8},{8,9},{11,10... | collective-permute-start | bytes 2826248 | tf_op jit(solution)/shard_map/ppermute | solution.py:240
  152.7 27.0 %collective-permute-start.1 = (bf16[736,640]{1,0:T(8,128)(2,1)}, bf16[736,640]{1,0:T(8,128)(2,1)S(1)}, u32[]{:S(2)}, u32[]{:S(2)}) collective-permute-start(bf16[736,640]{1,0:T(8,128)(2,1)} %get-tuple-element.34.out_ref), channel_id=1, source_target_pairs={{1,0},{0,1},{3,2},{2,3},{5,4},{4,5},{7,6},{6,7},{9,8},{8,9},{11,10... | collective-permute-start | bytes 2826248 | tf_op jit(solution)/shard_map/ppermute | solution.py:240
  242.4 105.7 %collective-permute-start.9 = (bf16[736,1152]{1,0:T(8,128)(2,1)}, bf16[736,1152]{1,0:T(8,128)(2,1)}, u32[]{:S(2)}, u32[]{:S(2)}) collective-permute-start(bf16[736,1152]{1,0:T(8,128)(2,1)} %get-tuple-element.41), channel_id=1, source_target_pairs={{1,0},{0,1},{3,2},{2,3},{5,4},{4,5},{7,6},{6,7},{9,8},{8,9},{11,10... | collective-permute-start | bytes 5087240 | tf_op jit(solution)/shard_map/ppermute | solution.py:240
  256.8 60.8 %slice-start = ((s8[6782976]{0:T(1024)(128)(4,1)}), s8[2588672]{0:T(1024)(128)(4,1)S(1)}, s32[]{:S(2)}) async-start(s8[6782976]{0:T(1024)(128)(4,1)} %bitcast.123), calls=%async_computation.6 | async-start | bytes 5177344
  256.8 265.5 %reduce-scatter.5.cloned.1.call-start = ((), (), s32[]{:S(2)}) async-start(), calls=%async_computation.4 | async-start | bytes 6266880 | tf_op jit(solution)/shard_map/reduce_scatter | solution.py:449
  256.9 60.7 %slice-start.1 = ((s8[6782976]{0:T(1024)(128)(4,1)}), s8[4194304]{0:T(1024)(128)(4,1)S(1)}, s32[]{:S(2)}) async-start(s8[6782976]{0:T(1024)(128)(4,1)} %bitcast.123), calls=%async_computation.7 | async-start | bytes 8388608
  256.9 60.7 %collective-permute-start.10 = (bf16[736,1152]{1,0:T(8,128)(2,1)}, bf16[736,1152]{1,0:T(8,128)(2,1)S(1)}, u32[]{:S(2)}, u32[]{:S(2)}) collective-permute-start(bf16[736,1152]{1,0:T(8,128)(2,1)} %get-tuple-element.45), channel_id=1, source_target_pairs={{1,0},{0,1},{3,2},{2,3},{5,4},{4,5},{7,6},{6,7},{9,8},{8,9},{11,10... | collective-permute-start | bytes 5087240 | tf_op jit(solution)/shard_map/ppermute | solution.py:240
  272.5 95.2 %collective-permute-start.18 = (bf16[8,72,2176]{2,1,0:T(8,128)(2,1)}, bf16[8,72,2176]{2,1,0:T(8,128)(2,1)}, u32[]{:S(2)}, u32[]{:S(2)}) collective-permute-start(bf16[8,72,2176]{2,1,0:T(8,128)(2,1)} %dynamic-slice_bitcast_fusion), channel_id=1, source_target_pairs={{0,2},{2,0},{4,6},{6,4},{8,10},{10,8},{12,14},{14,12},{16,18},{18,... | collective-permute-start | bytes 7520264 | tf_op jit(solution)/shard_map/ppermute | solution.py:290
  275.6 42.0 %copy-start.19 = (bf16[736,1152]{1,0:T(8,128)(2,1)S(1)}, bf16[736,1152]{1,0:T(8,128)(2,1)}, u32[]{:S(2)}) copy-start(bf16[736,1152]{1,0:T(8,128)(2,1)} %get-tuple-element.45) | copy-start | bytes 5087236
  277.7 42.5 %copy-start.14 = (bf16[2,736,1152]{2,1,0:T(8,128)(2,1)S(1)}, bf16[2,736,1152]{2,1,0:T(8,128)(2,1)}, u32[]{:S(2)}) copy-start(bf16[2,736,1152]{2,1,0:T(8,128)(2,1)} %copy-done.12) | copy-start | bytes 10174468
  351.0 112.3 %collective-permute-start.11 = (bf16[2,368,1152]{2,1,0:T(8,128)(2,1)}, bf16[2,368,1152]{2,1,0:T(8,128)(2,1)}, u32[]{:S(2)}, u32[]{:S(2)}) collective-permute-start(bf16[2,368,1152]{2,1,0:T(8,128)(2,1)} %constant_dynamic-slice_fusion.1), channel_id=1, source_target_pairs={{0,1},{1,0},{2,3},{3,2},{4,5},{5,4},{6,7},{7,6},{8,9},{9,8},{10,11... | collective-permute-start | bytes 5087240 | tf_op jit(solution)/shard_map/ppermute | solution.py:263
  414.6 37.6 %collective-permute-start.12 = (bf16[2,368,1152]{2,1,0:T(8,128)(2,1)}, bf16[2,368,1152]{2,1,0:T(8,128)(2,1)S(1)}, u32[]{:S(2)}, u32[]{:S(2)}) collective-permute-start(bf16[2,368,1152]{2,1,0:T(8,128)(2,1)} %constant_dynamic-slice_fusion), channel_id=1, source_target_pairs={{0,1},{1,0},{2,3},{3,2},{4,5},{5,4},{6,7},{7,6},{8,9},{9,8},{10,11... | collective-permute-start | bytes 5087240 | tf_op jit(solution)/shard_map/ppermute | solution.py:263
  418.6 28.0 %collective-permute-start.19 = (bf16[4,72,2176]{2,1,0:T(8,128)(2,1)S(1)}, bf16[4,72,2176]{2,1,0:T(8,128)(2,1)S(1)}, u32[]{:S(2)}, u32[]{:S(2)}) collective-permute-start(bf16[4,72,2176]{2,1,0:T(8,128)(2,1)S(1)} %dynamic-slice_bitcast_fusion.3), channel_id=1, source_target_pairs={{0,4},{2,6},{4,0},{6,2},{8,12},{10,14},{12,8},{14,10},{16,20},{18,... | collective-permute-start | bytes 3760136 | tf_op jit(solution)/shard_map/ppermute | solution.py:290
  456.0 4.0 collective-permute-start.13
  460.1 1.2 collective-permute-start.14
  461.2 29.1 %collective-permute-start.20 = (bf16[2,72,2176]{2,1,0:T(8,128)(2,1)S(1)}, bf16[2,72,2176]{2,1,0:T(8,128)(2,1)S(1)}, u32[]{:S(2)}, u32[]{:S(2)}) collective-permute-start(bf16[2,72,2176]{2,1,0:T(8,128)(2,1)S(1)} %dynamic-slice_bitcast_fusion.4), channel_id=1, source_target_pairs={{0,8},{2,10},{4,12},{6,14},{8,0},{10,2},{12,4},{14,6},{16,24},{18,... | collective-permute-start | bytes 1880072 | tf_op jit(solution)/shard_map/ppermute | solution.py:290
  461.3 8.7 %collective-permute-start.15 = (f32[10216]{0:T(1024)S(1)}, f32[10216]{0:T(1024)S(1)}, u32[]{:S(2)}, u32[]{:S(2)}) collective-permute-start(f32[10216]{0:T(1024)S(1)} %add.370), channel_id=1, source_target_pairs={{0,4},{2,6},{4,0},{6,2},{8,12},{10,14},{12,8},{14,10},{16,20},{18,... | collective-permute-start | bytes 122600 | tf_op jit(solution)/shard_map/ppermute | solution.py:299
  470.0 18.8 %collective-permute-start.16 = (f32[10216]{0:T(1024)S(1)}, f32[10216]{0:T(1024)S(1)}, u32[]{:S(2)}, u32[]{:S(2)}) collective-permute-start(f32[10216]{0:T(1024)S(1)} %add.371), channel_id=1, source_target_pairs={{0,8},{2,10},{4,12},{6,14},{8,0},{10,2},{12,4},{14,6},{16,24},{18,... | collective-permute-start | bytes 122600 | tf_op jit(solution)/shard_map/ppermute | solution.py:299
  488.8 6.7 %collective-permute-start.17 = (f32[10216]{0:T(1024)S(1)}, f32[10216]{0:T(1024)S(1)}, u32[]{:S(2)}, u32[]{:S(2)}) collective-permute-start(f32[10216]{0:T(1024)S(1)} %add.372), channel_id=1, source_target_pairs={{0,16},{2,18},{4,20},{6,22},{8,24},{10,26},{12,28},{14,30},{16,0},... | collective-permute-start | bytes 122600 | tf_op jit(solution)/shard_map/ppermute | solution.py:299
  490.6 28.7 %collective-permute-start.21 = (bf16[1,72,2176]{2,1,0:T(8,128)(2,1)S(1)}, bf16[1,72,2176]{2,1,0:T(8,128)(2,1)S(1)}, u32[]{:S(2)}, u32[]{:S(2)}) collective-permute-start(bf16[1,72,2176]{2,1,0:T(8,128)(2,1)S(1)} %constant_dynamic-slice_fusion.2), channel_id=1, source_target_pairs={{0,16},{2,18},{4,20},{6,22},{8,24},{10,26},{12,28},{14,30},{16,0},... | collective-permute-start | bytes 940040 | tf_op jit(solution)/shard_map/ppermute | solution.py:290
  (55 other events, 693.6 us)
Sparse Core Ops, SparseCore 0:
  10.7 63.8 all-gather.2
  76.9 89.6 all-gather.4
  257.0 75.6 reduce-scatter.6
  415.4 104.5 reduce-scatter.4

commit v4 on v3

--- a/solution.py
+++ b/solution.py
@@ -253,31 +253,30 @@
     return full
 
 
-def sum_blocks(values, where, parts, rows):
+def send_blocks(values, where, parts, rows):
     def block(k):
         return lax.dynamic_slice_in_dim(values, (where + k) % parts * rows, rows, 1)
 
-    total = block(0)
+    shares = [block(0)]
     for k in range(1, parts):
         pairs = [(j, (j + k) % parts) for j in range(parts)]
-        total = total + lax.ppermute(block(k).astype(bf), "tensor", pairs).astype(fl)
-    return total
-
-
-def gather_by_halves(values, axis):
+        shares.append(lax.ppermute(block(k), "tensor", pairs))
+    return shares
+
+
+def sum_of(shares):
+    return functools.reduce(jnp.add, [share.astype(fl) for share in shares])
+
+
+def start_doubling(have, axis, step):
     size = lax.axis_size(axis)
-    rows, width = values.shape
-    if size & (size - 1):
-        return lax.all_gather(values, axis, axis=0, tiled=True)
-    have = values[None]
-    step = size // 2
-    while step:
-        got = lax.ppermute(have, axis, [(j, j ^ step) for j in range(size)])
-        first = lax.axis_index(axis) // step % 2 == 0
-        low, high = jnp.where(first, have, got), jnp.where(first, got, have)
-        have = jnp.stack([low, high], axis=1).reshape(-1, rows, width)
-        step //= 2
-    return have.reshape(-1, width)
+    return have, lax.ppermute(have, axis, [(j, j ^ step) for j in range(size)])
+
+
+def end_doubling(have, got, axis, step):
+    first = lax.axis_index(axis) // step % 2 == 0
+    low, high = jnp.where(first, have, got), jnp.where(first, got, have)
+    return jnp.stack([low, high], axis=1).reshape(-1, *have.shape[1:])
 
 
 def exchange_half(values, axis, step):
@@ -347,10 +346,10 @@
     full_qkv = lax.all_gather(shard_qkv, "dp", axis=0, tiled=True)
     shard_out = pad_to(w_out.T, 1, colp)
     shard_out = jnp.concatenate([shard_out] + from_others(shard_out, parts), axis=1)
+    ring = lax.axis_size("dp")
+    halving = not ring & (ring - 1)
     shard_mlp = jnp.concatenate([pad_to(w_up, 1, hidp), pad_to(w_down.T, 1, hidp)], axis=1)
     full_mlp = lax.all_gather(shard_mlp, "dp", axis=0, tiled=True)
-    full_out = gather_by_halves(shard_out, "dp")
-    own_out = full_out[:, :colp]
 
     place = jnp.arange(size, dtype=jnp.int32)
     position = place // rowp * rows + place % rowp
@@ -365,18 +364,45 @@
     bias_three = pad_to(
         jnp.stack([qv_bias[0], jnp.zeros_like(qv_bias[0]), qv_bias[1]]), 1, colp
     ).reshape(1, 3 * colp)
+    doubling = ring // 2
+    if halving:
+        pending = start_doubling(after(shard_out, full_qkv)[None], "dp", doubling)
     qkv = (dot(xn1, full_qkv, 1, 0) + bias_three).astype(bf)
 
+    def next_double(pending, step, *others):
+        if not halving or not step:
+            return pending, step
+        have, got = pending
+        if others:
+            got = after(got, *others)
+        have = end_doubling(have, got, "dp", step)
+        step //= 2
+        return (start_doubling(have, "dp", step) if step else (have,)), step
+
+    if halving:
+        pending, doubling = next_double(pending, doubling, qkv)
     attended, lses, joined = [], [], []
     for i in range(images):
         out, lse = attention_forward(qkv, key_bias, i, size, heads)
         attended.append(out)
         lses.append(lse)
-        joined.append(jnp.concatenate([out] + from_others(out, parts), axis=1))
+        if halving:
+            pending, doubling = next_double(pending, doubling, out)
+    attended = after(attended, *attended)
+    for i in range(images):
+        others = from_others(attended[i], parts)
+        joined.append(jnp.concatenate([attended[i]] + others, axis=1))
+    if halving:
+        while doubling:
+            pending, doubling = next_double(pending, doubling)
+        full_out = pending[0].reshape(width, -1)
+    else:
+        full_out = lax.all_gather(shard_out, "dp", axis=0, tiled=True)
+    own_out = full_out[:, :colp]
     dy_others = after(dy_others, *attended)
     dy_all = all_blocks(dy_own, dy_others, where).reshape(both, width)
     joined = jnp.concatenate(joined, axis=0)
-    attended_all = jnp.concatenate(attended, axis=0)
+    attended_all = joined[:, :colp]
 
     h1 = x_all.astype(fl) + dot(joined, full_out, 1, 1) + out_bias[0]
     xn2 = normalize(h1, ln_gain[1], ln_bias[1]).astype(bf)
@@ -394,15 +420,6 @@
     grad_down = dot(dy_all, act[:, :hids], 0, 0).astype(bf)
     down_sums = lax.psum_scatter(grad_down, "dp", scatter_dimension=0, tiled=True)
     down_sums = lax.optimization_barrier(down_sums)
-    d_pre = after(d_pre, grad_down)
-    grad_up = dot(xn2, d_pre[:, :hids], 0, 0).astype(bf)
-    ring = lax.axis_size("dp")
-    halving = not ring & (ring - 1)
-    if halving:
-        up_sums, step = grad_up.reshape(ring, here, hids), 1
-        pending = exchange_half(up_sums, "dp", step)
-    else:
-        up_sums, step, pending = lax.psum_scatter(grad_up, "dp", tiled=True), ring, ()
 
     def next_half(pending, step, *others):
         if not halving or step == ring:
@@ -420,7 +437,7 @@
     g2, c2, bo = 0.0, 0.0, 0.0
     for i in range(images):
         at = slice(i * size, (i + 1) * size)
-        got = after(received[i], grad_up, grad_down, *d_qkv)
+        got = after(received[i], grad_down, *d_qkv)
         total = dxn_parts[i].astype(fl)
         for other in got:
             total = total + other.astype(fl)
@@ -435,12 +452,11 @@
         d_qkv = (
             attention_backward(qkv, key_bias, attended[i], d_att, lses[i], d_qkv, i, size, heads),
         )
-        pending, step = next_half(pending, step, *d_qkv)
     (d_qkv,) = d_qkv
 
     y_all = after(jnp.stack(y_parts), got)
     h1_own = lax.dynamic_slice_in_dim(h1.reshape(images, size, width), where * rowp, rowp, 1)
-    y_own = h1_own + sum_blocks(y_all, where, parts, rowp) + out_bias[1]
+    y_own = h1_own + sum_of(send_blocks(y_all, where, parts, rowp)) + out_bias[1]
     output = jnp.where(own_valid, y_own, 0.0).astype(bf)
 
     grad_qkv = dot(xn1, d_qkv, 0, 0).astype(bf)
@@ -448,14 +464,25 @@
     att_grads = jnp.concatenate([grad_qkv, grad_out], axis=1)
     att_sums = lax.psum_scatter(att_grads, "dp", scatter_dimension=0, tiled=True)
 
-    pending, step = next_half(pending, step, att_grads)
     d_qkv = after(d_qkv, att_grads)
     sums_qkv = jnp.sum(d_qkv.astype(fl), axis=0)
     d_xn1 = dot(d_qkv, full_qkv, 1, 1).astype(bf).reshape(images, size, width)
-    d_xn1 = sum_blocks(d_xn1, where, parts, rowp)
+    shares = send_blocks(d_xn1, where, parts, rowp)
+    d_pre = after(d_pre, d_xn1)
+    grad_up = dot(xn2, d_pre[:, :hids], 0, 0).astype(bf)
+    if halving:
+        up_sums, step = grad_up.reshape(ring, here, hids), 1
+        pending = exchange_half(up_sums, "dp", step)
+    else:
+        up_sums, step, pending = lax.psum_scatter(grad_up, "dp", tiled=True), ring, ()
+    pending, step = next_half(pending, step)
+    if halving:
+        shares = after(shares, *pending[:1])
+    d_xn1 = sum_of(shares)
     back, hat = normalize_back(x_own.astype(fl), ln_gain[0], d_xn1)
     g1 = jnp.sum(d_xn1 * hat, axis=(0, 1))
     c1 = jnp.sum(d_xn1, axis=(0, 1))
+    pending, step = next_half(pending, step, g1)
     d_h1_own = jnp.stack([lax.dynamic_slice_in_dim(d, where * rowp, rowp, 0) for d in d_h1])
     d_inputs = (d_h1_own + back).astype(bf)
 

time: 540 us -> 592 us (1.096)
  waiting for transfers between devices: 175 us -> 221 us
  Pallas kernels: 123 us -> 133 us
    ppermute x7, waiting for transfers between devices: 59.1 us -> 132 us  [from_others(): lax.ppermute(values, 'tensor', [((j + k) % parts, j) for j in range(parts)])]
    ppermute x4, waiting for transfers between devices: 42.6 us -> 3.16 us  [exchange_half(): lax.ppermute(send, axis, [(j, j ^ step) for j in range(size)])]
    ppermute x6, waiting for transfers between devices: 57 us -> 68.9 us  [the longest x2 60.1 us: send_blocks(): shares.append(lax.ppermute(block(k), 'tensor', pairs))]
    pallas_call x2, Pallas kernels: 30 us -> 40.4 us  [attention_forward(): pl.pallas_call(functools.partial(forward_kernel, heads=heads, colp=colp,...]
    unnamed x129 -> x111, local copies, waits for them, and re-layouts: 28.9 us -> 21.4 us
  transfers between devices with their start and end apart: 26 -> 26, of which waited for: 10 -> 11; matrix products, arithmetic and copies ran while one was open for 32% -> 29% of each run, Pallas kernels for 13% -> 14%
where the time goes in v4:
time: 592 us; the launch traced here: 582 us
  waiting for transfers between devices  221 us (37%)
  Pallas kernels  133 us (22%)
  matrix products  75.6 us (13%)
  other arithmetic  59.1 us (10%)
  local copies, waits for them, and re-layouts  49.7 us (8%)
  starting transfers between devices  28.5 us (5%)
  between operations  15.3 us (3%)
    ppermute x7, waiting for transfers between devices, from_others(): lax.ppermute(values, 'tensor', [((j + k) % parts, j) for j in range(parts)])  132 us
    dot_general x11, matrix products, dot(): lax.dot_general(a, b, (((ca,), (cb,)), ((), ())), preferred_element_type=fl)  75.6 us
    ppermute x2, waiting for transfers between devices, send_blocks(): shares.append(lax.ppermute(block(k), 'tensor', pairs))  60.1 us
    pallas_call x2, Pallas kernels, mlp(): pl.pallas_call(mlp_kernel, grid=(steps,), out_shape=(jax.ShapeDtypeStruct...  51.7 us
    pallas_call x2, Pallas kernels, attention_backward(): pl.pallas_call(functools.partial(backward_kernel, heads=heads, colp=colp,...  41.2 us
    pallas_call x2, Pallas kernels, attention_forward(): pl.pallas_call(functools.partial(forward_kernel, heads=heads, colp=colp,...  40.4 us
    unnamed x111, local copies, waits for them, and re-layouts  21.4 us
    ppermute x5, waiting for transfers between devices, sum_everywhere(): lax.ppermute(values, axis, [(j, j ^ step) for j in range(size)])  16.5 us
  transfers between devices with their start and end apart: 26, of which 11 were waited for; matrix products, arithmetic and copies ran while one was open for 29% of the time, Pallas kernels for 14%

profile of v4, /device:TPU:0, one launch (start us, length us, event | category | flops | bytes accessed | tf_op | source)
XLA Modules:
  0.0 582.5 jit_solution(13527821177566405729)
XLA Ops:
  15.9 3.0 collective-permute-start
  20.9 37.2 %collective-permute-done.3 = bf16[72,640]{1,0:T(8,128)(2,1)} collective-permute-done((bf16[72,640]{1,0:T(8,128)(2,1)S(1)}, bf16[72,640]{1,0:T(8,128)(2,1)}, u32[]{:S(2)}, u32[]{:S(2)}) %collective-permute-start.3) | collective-permute-done | bytes 92192 | tf_op jit(solution)/shard_map/ppermute | solution.py:240
  68.7 12.3 %add_convert_fusion.qkv_ref = bf16[1472,1920]{1,0:T(8,128)(2,1)} fusion(bf16[1472,1152]{1,0:T(8,128)(2,1)} %fusion.4, bf16[1152,1920]{1,0:T(8,128)(2,1)} %all-gather.3.cloned.1.call-done, f32[1920]{0:T(1024)S(1)} %add.335), kind=kOutput, calls=%fused_computation.3 | convolution fusion | flops 6517309440 | bytes 13475328 | tf_op jit(solution)/shard_map/dot_general | solution.py:22
  82.9 14.8 %attention_forward.2 = (bf16[736,640]{1,0:T(8,128)(2,1)}, f32[8,736]{1,0:T(8,128)}) custom-call(f32[1472,1]{1,0:T(8,128)} %select_n.237.bias_ref, bf16[1472,1920]{1,0:T(8,128)(2,1)} %add_convert_fusion.qkv_ref), custom_call_target="tpu_custom_call" | custom-call | flops 4437573632 | bytes 3768320 | tf_op jit(solution)/shard_map/attention_forward/pallas_call | solution.py:77
  97.7 8.8 %collective-permute-done.5 = bf16[2,72,1280]{2,1,0:T(8,128)(2,1)S(1)} collective-permute-done((bf16[2,72,1280]{2,1,0:T(8,128)(2,1)S(1)}, bf16[2,72,1280]{2,1,0:T(8,128)(2,1)S(1)}, u32[]{:S(2)}, u32[]{:S(2)}) %collective-permute-start.5) | collective-permute-done | bytes 368672 | tf_op jit(solution)/shard_map/ppermute | solution.py:273
  113.5 25.6 %attention_forward.3 = (bf16[736,640]{1,0:T(8,128)(2,1)}, f32[8,736]{1,0:T(8,128)}) custom-call(f32[1472,1]{1,0:T(8,128)} %select_n.237.bias_ref, bf16[1472,1920]{1,0:T(8,128)(2,1)} %add_convert_fusion.qkv_ref), custom_call_target="tpu_custom_call" | custom-call | flops 4437573632 | bytes 3768320 | tf_op jit(solution)/shard_map/attention_forward/pallas_call | solution.py:77
  156.3 15.4 %collective-permute-done.2 = bf16[736,640]{1,0:T(8,128)(2,1)S(1)} collective-permute-done((bf16[736,640]{1,0:T(8,128)(2,1)S(1)}, bf16[736,640]{1,0:T(8,128)(2,1)S(1)}, u32[]{:S(2)}, u32[]{:S(2)}) %collective-permute-start.2) | collective-permute-done | bytes 942112 | tf_op jit(solution)/shard_map/ppermute | solution.py:240
  171.6 19.7 %collective-permute-done.1 = bf16[736,640]{1,0:T(8,128)(2,1)S(1)} collective-permute-done((bf16[736,640]{1,0:T(8,128)(2,1)S(1)}, bf16[736,640]{1,0:T(8,128)(2,1)S(1)}, u32[]{:S(2)}, u32[]{:S(2)}) %collective-permute-start.1) | collective-permute-done | bytes 942112 | tf_op jit(solution)/shard_map/ppermute | solution.py:240
  191.4 5.5 fusion.82
  202.2 25.6 %mlp.2 = (bf16[1472,2304]{1,0:T(8,128)(2,1)}, bf16[1472,2304]{1,0:T(8,128)(2,1)}, f32[1,2304]{1,0:T(1,128)}, bf16[736,1152]{1,0:T(8,128)(2,1)}, bf16[736,1152]{1,0:T(8,128)(2,1)}) custom-call(bf16[1472,1152]{1,0:T(8,128)(2,1)} %add_convert_fusion.1.xn_ref, bf16[1472,1152]{1,0:T(8,128)(2,1)} %bitcast.19.dy_ref, ...), custom_call_target="tpu_custom_call" | custom-call | flops 15627976704 | bytes 24182784 | tf_op jit(solution)/shard_map/mlp/pallas_call | solution.py:207
  227.9 26.1 %mlp.3 = (bf16[1472,2304]{1,0:T(8,128)(2,1)}, bf16[1472,2304]{1,0:T(8,128)(2,1)}, f32[1,2304]{1,0:T(1,128)}, bf16[736,1152]{1,0:T(8,128)(2,1)}, bf16[736,1152]{1,0:T(8,128)(2,1)}) custom-call(bf16[1472,1152]{1,0:T(8,128)(2,1)} %add_convert_fusion.1.xn_ref, bf16[1472,1152]{1,0:T(8,128)(2,1)} %bitcast.19.dy_ref, ...), custom_call_target="tpu_custom_call", output_to_operand_aliasing={{0}: (5, {}), {1}: (6, {})} | custom-call | flops 15627976704 | bytes 24182784 | tf_op jit(solution)/shard_map/mlp/pallas_call | solution.py:207
  256.1 14.1 %convolution_convert_fusion.1 = bf16[1152,2176]{1,0:T(8,128)(2,1)} fusion(bf16[1472,1152]{1,0:T(8,128)(2,1)} %bitcast.19.dy_ref, bf16[1472,2304]{1,0:T(8,128)(2,1)} %get-tuple-element.54), kind=kOutput, calls=%fused_computation.1 | convolution fusion | flops 7382384640 | bytes 14811136 | tf_op jit(solution)/shard_map/dot_general | solution.py:22
  270.3 58.9 %collective-permute-done.10 = bf16[736,1152]{1,0:T(8,128)(2,1)S(1)} collective-permute-done((bf16[736,1152]{1,0:T(8,128)(2,1)S(1)}, bf16[736,1152]{1,0:T(8,128)(2,1)S(1)}, u32[]{:S(2)}, u32[]{:S(2)}) %collective-permute-start.10) | collective-permute-done | bytes 1695776 | tf_op jit(solution)/shard_map/ppermute | solution.py:240
  329.2 4.7 multiply_reduce_fusion.3
  333.9 3.4 fusion.75
  343.0 20.6 %attention_backward.2.refs_0_ = bf16[1472,1920]{1,0:T(8,128)(2,1)} custom-call(f32[1472,1]{1,0:T(8,128)} %select_n.237.bias_ref, bf16[1472,1920]{1,0:T(8,128)(2,1)} %add_convert_fusion.qkv_ref, bf16[736,640]{1,0:T(8,128)(2,1)} %get-tuple-element.42.out_ref, bf16[736,640]{1,0:T(8,128)(2,1)} %convolution_convert_fusion.5.dout_ref, ...), custom_call_target="tpu_custom_call" | custom-call | flops 11093934080 | bytes 7536640 | tf_op jit(solution)/shard_map/attention_backward/pallas_call | solution.py:144
  363.6 3.7 multiply_reduce_fusion.2
  367.4 3.2 fusion.74
  376.2 20.6 %attention_backward.3 = bf16[1472,1920]{1,0:T(8,128)(2,1)} custom-call(f32[1472,1]{1,0:T(8,128)} %select_n.237.bias_ref, bf16[1472,1920]{1,0:T(8,128)(2,1)} %add_convert_fusion.qkv_ref, bf16[736,640]{1,0:T(8,128)(2,1)} %get-tuple-element.43.out_ref, bf16[736,640]{1,0:T(8,128)(2,1)} %convolution_convert_fusion.4.dout_ref, ...), custom_call_target="tpu_custom_call", output_to_operand_aliasing={{}: (5, {})} | custom-call | flops 11093934080 | bytes 7536640 | tf_op jit(solution)/shard_map/attention_backward/pallas_call | solution.py:144
  396.8 10.0 %convolution_convert_fusion.2 = bf16[1152,1920]{1,0:T(8,128)(2,1)S(1)} fusion(bf16[1472,1152]{1,0:T(8,128)(2,1)S(1)} %copy-done.14, bf16[1472,1920]{1,0:T(8,128)(2,1)} %attention_backward.3), kind=kOutput, calls=%fused_computation.6 | convolution fusion | flops 6513868800 | bytes 13467648 | tf_op jit(solution)/shard_map/dot_general | solution.py:22
  406.9 3.0 fusion.29
  409.9 3.0 pad_maximum_fusion
  412.9 12.5 %convolution_convert_fusion.3 = bf16[1472,1152]{1,0:T(8,128)(2,1)} fusion(bf16[1472,1920]{1,0:T(8,128)(2,1)} %attention_backward.3, bf16[1152,1920]{1,0:T(8,128)(2,1)} %all-gather.3.cloned.1.call-done), kind=kOutput, calls=%fused_computation.7 | convolution fusion | flops 6513352704 | bytes 13467648 | tf_op jit(solution)/shard_map/dot_general | solution.py:22
  425.5 9.2 %convolution_convert_fusion = bf16[1152,2176]{1,0:T(8,128)(2,1)S(1)} fusion(bf16[1472,1152]{1,0:T(8,128)(2,1)S(1)} %copy-done.13, bf16[1472,2304]{1,0:T(8,128)(2,1)S(1)} %bitcast.150), kind=kOutput, calls=%fused_computation | convolution fusion | flops 7382384640 | bytes 14811136 | tf_op jit(solution)/shard_map/dot_general | solution.py:22
  447.5 3.4 convert_reduce_fusion
  451.0 3.3 fusion.7
  457.8 60.1 %collective-permute-done.12 = bf16[2,368,1152]{2,1,0:T(8,128)(2,1)} collective-permute-done((bf16[2,368,1152]{2,1,0:T(8,128)(2,1)}, bf16[2,368,1152]{2,1,0:T(8,128)(2,1)}, u32[]{:S(2)}, u32[]{:S(2)}) %collective-permute-start.12) | collective-permute-done | bytes 1695776 | tf_op jit(solution)/shard_map/ppermute | solution.py:263
  517.9 4.8 fusion.38
  533.2 4.0 fusion.49
  541.8 8.4 %collective-permute-done.17 = f32[10216]{0:T(1024)S(1)} collective-permute-done((f32[10216]{0:T(1024)S(1)}, f32[10216]{0:T(1024)S(1)}, u32[]{:S(2)}, u32[]{:S(2)}) %collective-permute-start.17) | collective-permute-done | bytes 40896 | tf_op jit(solution)/shard_map/ppermute | solution.py:298
  556.9 5.6 collective-permute-done.18
  565.5 3.2 collective-permute-done.21
  (268 shorter events, 113.3 us)
Async XLA Ops:
  7.2 58.7 %all-gather.3.cloned.1.call-start = ((), (), s32[]{:S(2)}) async-start(), calls=%async_computation.2 | async-start | bytes 4700160 | tf_op jit(solution)/shard_map/all_gather | solution.py:346
  9.4 192.9 %all-gather.5.cloned.1.call-start = ((), (), s32[]{:S(2)}) async-start(), calls=%async_computation.3 | async-start | bytes 11280384 | tf_op jit(solution)/shard_map/all_gather | solution.py:352
  11.4 558.3 %reduce-scatter.7.cloned.1.call-start = ((), (), s32[]{:S(2)}) async-start(), calls=%async_computation.5 | async-start | bytes 5326848
  15.9 43.9 %collective-permute-start = (bf16[2,368,1152]{2,1,0:T(8,128)(2,1)}, bf16[2,368,1152]{2,1,0:T(8,128)(2,1)}, u32[]{:S(2)}, u32[]{:S(2)}) collective-permute-start(bf16[2,368,1152]{2,1,0:T(8,128)(2,1)} %get-tuple-element.155), channel_id=1, source_target_pairs={{1,0},{0,1},{3,2},{2,3},{5,4},{4,5},{7,6},{6,7},{9,8},{8,9},{11,10... | collective-permute-start | bytes 5087240 | tf_op jit(solution)/shard_map/ppermute | solution.py:240
  18.9 39.3 %collective-permute-start.3 = (bf16[72,640]{1,0:T(8,128)(2,1)S(1)}, bf16[72,640]{1,0:T(8,128)(2,1)}, u32[]{:S(2)}, u32[]{:S(2)}) collective-permute-start(bf16[72,640]{1,0:T(8,128)(2,1)S(1)} %pad.33), channel_id=1, source_target_pairs={{1,0},{0,1},{3,2},{2,3},{5,4},{4,5},{7,6},{6,7},{9,8},{8,9},{11,10... | collective-permute-start | bytes 276488 | tf_op jit(solution)/shard_map/ppermute | solution.py:240
  20.9 42.3 %copy-start.27 = (f32[1152]{0:T(1024)}, f32[1152]{0:T(1024)S(1)}, u32[]{:S(2)}) copy-start(f32[1152]{0:T(1024)S(1)} %get-tuple-element.129) | copy-start | bytes 13828
  65.9 15.1 %collective-permute-start.4 = (bf16[1,72,1280]{2,1,0:T(8,128)(2,1)}, bf16[1,72,1280]{2,1,0:T(8,128)(2,1)S(1)}, u32[]{:S(2)}, u32[]{:S(2)}) collective-permute-start(bf16[1,72,1280]{2,1,0:T(8,128)(2,1)} %bitcast.142), channel_id=1, source_target_pairs={{0,16},{2,18},{4,20},{6,22},{8,24},{10,26},{12,28},{14,30},{16,0},... | collective-permute-start | bytes 552968 | tf_op jit(solution)/shard_map/ppermute | solution.py:273
  81.2 25.4 %collective-permute-start.5 = (bf16[2,72,1280]{2,1,0:T(8,128)(2,1)S(1)}, bf16[2,72,1280]{2,1,0:T(8,128)(2,1)S(1)}, u32[]{:S(2)}, u32[]{:S(2)}) collective-permute-start(bf16[2,72,1280]{2,1,0:T(8,128)(2,1)S(1)} %maximum_bitcast_fusion), channel_id=1, source_target_pairs={{0,8},{2,10},{4,12},{6,14},{8,0},{10,2},{12,4},{14,6},{16,24},{18,... | collective-permute-start | bytes 1105928 | tf_op jit(solution)/shard_map/ppermute | solution.py:273
  107.5 31.6 %collective-permute-start.6 = (bf16[4,72,1280]{2,1,0:T(8,128)(2,1)}, bf16[4,72,1280]{2,1,0:T(8,128)(2,1)}, u32[]{:S(2)}, u32[]{:S(2)}) collective-permute-start(bf16[4,72,1280]{2,1,0:T(8,128)(2,1)} %bitcast.10), channel_id=1, source_target_pairs={{0,4},{2,6},{4,0},{6,2},{8,12},{10,14},{12,8},{14,10},{16,20},{18,... | collective-permute-start | bytes 2211848 | tf_op jit(solution)/shard_map/ppermute | solution.py:273
  112.1 38.9 %collective-permute-start.8 = (bf16[2,368,1152]{2,1,0:T(8,128)(2,1)}, bf16[2,368,1152]{2,1,0:T(8,128)(2,1)}, u32[]{:S(2)}, u32[]{:S(2)}) collective-permute-start(bf16[2,368,1152]{2,1,0:T(8,128)(2,1)} %get-tuple-element.135), channel_id=1, source_target_pairs={{1,0},{0,1},{3,2},{2,3},{5,4},{4,5},{7,6},{6,7},{9,8},{8,9},{11,10... | collective-permute-start | bytes 5087240 | tf_op jit(solution)/shard_map/ppermute | solution.py:240
  142.0 11.8 %collective-permute-start.7 = (bf16[8,72,1280]{2,1,0:T(8,128)(2,1)}, bf16[8,72,1280]{2,1,0:T(8,128)(2,1)}, u32[]{:S(2)}, u32[]{:S(2)}) collective-permute-start(bf16[8,72,1280]{2,1,0:T(8,128)(2,1)} %bitcast.13), channel_id=1, source_target_pairs={{0,2},{2,0},{4,6},{6,4},{8,10},{10,8},{12,14},{14,12},{16,18},{18,... | collective-permute-start | bytes 4423688 | tf_op jit(solution)/shard_map/ppermute | solution.py:273
  147.9 23.7 %collective-permute-start.2 = (bf16[736,640]{1,0:T(8,128)(2,1)S(1)}, bf16[736,640]{1,0:T(8,128)(2,1)S(1)}, u32[]{:S(2)}, u32[]{:S(2)}) collective-permute-start(bf16[736,640]{1,0:T(8,128)(2,1)S(1)} %copy-done.42), channel_id=1, source_target_pairs={{1,0},{0,1},{3,2},{2,3},{5,4},{4,5},{7,6},{6,7},{9,8},{8,9},{11,10... | collective-permute-start | bytes 2826248 | tf_op jit(solution)/shard_map/ppermute | solution.py:240
  149.4 42.0 %collective-permute-start.1 = (bf16[736,640]{1,0:T(8,128)(2,1)S(1)}, bf16[736,640]{1,0:T(8,128)(2,1)S(1)}, u32[]{:S(2)}, u32[]{:S(2)}) collective-permute-start(bf16[736,640]{1,0:T(8,128)(2,1)S(1)} %copy-done.40), channel_id=1, source_target_pairs={{1,0},{0,1},{3,2},{2,3},{5,4},{4,5},{7,6},{6,7},{9,8},{8,9},{11,10... | collective-permute-start | bytes 2826248 | tf_op jit(solution)/shard_map/ppermute | solution.py:240
  156.3 40.6 %copy-start.16 = (bf16[8,2,72,1280]{3,2,1,0:T(8,128)(2,1)}, bf16[8,2,72,1280]{3,2,1,0:T(8,128)(2,1)S(1)}, u32[]{:S(2)}) copy-start(bf16[8,2,72,1280]{3,2,1,0:T(8,128)(2,1)S(1)} %copy.70) | copy-start | bytes 8847364
  171.6 25.3 %copy-start.44 = (bf16[736,640]{1,0:T(8,128)(2,1)}, bf16[736,640]{1,0:T(8,128)(2,1)S(1)}, u32[]{:S(2)}) copy-start(bf16[736,640]{1,0:T(8,128)(2,1)S(1)} %collective-permute-done.2) | copy-start | bytes 2826244
  227.9 27.6 %copy-start.9 = (bf16[736,1152]{1,0:T(8,128)(2,1)S(1)}, bf16[736,1152]{1,0:T(8,128)(2,1)}, u32[]{:S(2)}) copy-start(bf16[736,1152]{1,0:T(8,128)(2,1)} %get-tuple-element.55) | copy-start | bytes 5087236
  254.0 109.6 %collective-permute-start.9 = (bf16[736,1152]{1,0:T(8,128)(2,1)}, bf16[736,1152]{1,0:T(8,128)(2,1)}, u32[]{:S(2)}, u32[]{:S(2)}) collective-permute-start(bf16[736,1152]{1,0:T(8,128)(2,1)} %get-tuple-element.53), channel_id=1, source_target_pairs={{1,0},{0,1},{3,2},{2,3},{5,4},{4,5},{7,6},{6,7},{9,8},{8,9},{11,10... | collective-permute-start | bytes 5087240 | tf_op jit(solution)/shard_map/ppermute | solution.py:240
  255.5 73.7 %collective-permute-start.10 = (bf16[736,1152]{1,0:T(8,128)(2,1)S(1)}, bf16[736,1152]{1,0:T(8,128)(2,1)S(1)}, u32[]{:S(2)}, u32[]{:S(2)}) collective-permute-start(bf16[736,1152]{1,0:T(8,128)(2,1)S(1)} %copy-done.9), channel_id=1, source_target_pairs={{1,0},{0,1},{3,2},{2,3},{5,4},{4,5},{7,6},{6,7},{9,8},{8,9},{11,10... | collective-permute-start | bytes 5087240 | tf_op jit(solution)/shard_map/ppermute | solution.py:240
  270.2 301.5 %reduce-scatter.5.cloned.1.call-start = ((), (), s32[]{:S(2)}) async-start(), calls=%async_computation.4 | async-start | bytes 6266880 | tf_op jit(solution)/shard_map/reduce_scatter | solution.py:465
  340.4 23.2 %slice-start = ((s8[6782976]{0:T(1024)(128)(4,1)}), s8[4194304]{0:T(1024)(128)(4,1)S(1)}, s32[]{:S(2)}) async-start(s8[6782976]{0:T(1024)(128)(4,1)} %bitcast.121), calls=%async_computation.6 | async-start | bytes 8388608
  438.6 12.3 %collective-permute-start.13 = (bf16[8,72,2176]{2,1,0:T(8,128)(2,1)}, bf16[8,72,2176]{2,1,0:T(8,128)(2,1)}, u32[]{:S(2)}, u32[]{:S(2)}) collective-permute-start(bf16[8,72,2176]{2,1,0:T(8,128)(2,1)} %dynamic-slice_bitcast_fusion), channel_id=1, source_target_pairs={{0,2},{2,0},{4,6},{6,4},{8,10},{10,8},{12,14},{14,12},{16,18},{18,... | collective-permute-start | bytes 7520264 | tf_op jit(solution)/shard_map/ppermute | solution.py:289
  442.0 91.2 %collective-permute-start.11 = (bf16[2,368,1152]{2,1,0:T(8,128)(2,1)}, bf16[2,368,1152]{2,1,0:T(8,128)(2,1)}, u32[]{:S(2)}, u32[]{:S(2)}) collective-permute-start(bf16[2,368,1152]{2,1,0:T(8,128)(2,1)} %constant_dynamic-slice_fusion.2), channel_id=1, source_target_pairs={{0,1},{1,0},{2,3},{3,2},{4,5},{5,4},{6,7},{7,6},{8,9},{9,8},{10,11... | collective-permute-start | bytes 5087240 | tf_op jit(solution)/shard_map/ppermute | solution.py:263
  445.9 72.0 %collective-permute-start.12 = (bf16[2,368,1152]{2,1,0:T(8,128)(2,1)}, bf16[2,368,1152]{2,1,0:T(8,128)(2,1)}, u32[]{:S(2)}, u32[]{:S(2)}) collective-permute-start(bf16[2,368,1152]{2,1,0:T(8,128)(2,1)} %get-tuple-element.148), channel_id=1, source_target_pairs={{0,1},{1,0},{2,3},{3,2},{4,5},{5,4},{6,7},{7,6},{8,9},{9,8},{10,11... | collective-permute-start | bytes 5087240 | tf_op jit(solution)/shard_map/ppermute | solution.py:263
  454.3 63.7 %copy-start.28 = (f32[1152]{0:T(1024)S(1)}, f32[1152]{0:T(1024)}, u32[]{:S(2)}) copy-start(f32[1152]{0:T(1024)} %copy-done.27) | copy-start | bytes 13828
  455.9 75.5 %collective-permute-start.19 = (bf16[4,72,2176]{2,1,0:T(8,128)(2,1)}, bf16[4,72,2176]{2,1,0:T(8,128)(2,1)}, u32[]{:S(2)}, u32[]{:S(2)}) collective-permute-start(bf16[4,72,2176]{2,1,0:T(8,128)(2,1)} %get-tuple-element.152), channel_id=1, source_target_pairs={{0,4},{2,6},{4,0},{6,2},{8,12},{10,14},{12,8},{14,10},{16,20},{18,... | collective-permute-start | bytes 3760136 | tf_op jit(solution)/shard_map/ppermute | solution.py:289
  522.8 4.0 collective-permute-start.14
  526.9 2.4 collective-permute-start.15
  529.3 10.5 %collective-permute-start.16 = (f32[10216]{0:T(1024)S(1)}, f32[10216]{0:T(1024)S(1)}, u32[]{:S(2)}, u32[]{:S(2)}) collective-permute-start(f32[10216]{0:T(1024)S(1)} %add.374), channel_id=1, source_target_pairs={{0,4},{2,6},{4,0},{6,2},{8,12},{10,14},{12,8},{14,10},{16,20},{18,... | collective-permute-start | bytes 122600 | tf_op jit(solution)/shard_map/ppermute | solution.py:298
  533.1 18.5 %collective-permute-start.20 = (bf16[2,72,2176]{2,1,0:T(8,128)(2,1)S(1)}, bf16[2,72,2176]{2,1,0:T(8,128)(2,1)S(1)}, u32[]{:S(2)}, u32[]{:S(2)}) collective-permute-start(bf16[2,72,2176]{2,1,0:T(8,128)(2,1)S(1)} %dynamic-slice_bitcast_fusion.5), channel_id=1, source_target_pairs={{0,8},{2,10},{4,12},{6,14},{8,0},{10,2},{12,4},{14,6},{16,24},{18,... | collective-permute-start | bytes 1880072 | tf_op jit(solution)/shard_map/ppermute | solution.py:289
  539.8 10.4 %collective-permute-start.17 = (f32[10216]{0:T(1024)S(1)}, f32[10216]{0:T(1024)S(1)}, u32[]{:S(2)}, u32[]{:S(2)}) collective-permute-start(f32[10216]{0:T(1024)S(1)} %add.375), channel_id=1, source_target_pairs={{0,8},{2,10},{4,12},{6,14},{8,0},{10,2},{12,4},{14,6},{16,24},{18,... | collective-permute-start | bytes 122600 | tf_op jit(solution)/shard_map/ppermute | solution.py:298
  550.2 12.2 %collective-permute-start.18 = (f32[10216]{0:T(1024)S(1)}, f32[10216]{0:T(1024)S(1)}, u32[]{:S(2)}, u32[]{:S(2)}) collective-permute-start(f32[10216]{0:T(1024)S(1)} %add.376), channel_id=1, source_target_pairs={{0,16},{2,18},{4,20},{6,22},{8,24},{10,26},{12,28},{14,30},{16,0},... | collective-permute-start | bytes 122600 | tf_op jit(solution)/shard_map/ppermute | solution.py:298
  551.8 16.9 %collective-permute-start.21 = (bf16[1,72,2176]{2,1,0:T(8,128)(2,1)S(1)}, bf16[1,72,2176]{2,1,0:T(8,128)(2,1)S(1)}, u32[]{:S(2)}, u32[]{:S(2)}) collective-permute-start(bf16[1,72,2176]{2,1,0:T(8,128)(2,1)S(1)} %constant_dynamic-slice_fusion.3), channel_id=1, source_target_pairs={{0,16},{2,18},{4,20},{6,22},{8,24},{10,26},{12,28},{14,30},{16,0},... | collective-permute-start | bytes 940040 | tf_op jit(solution)/shard_map/ppermute | solution.py:289
  (46 other events, 319.8 us)
Sparse Core Ops, SparseCore 0:
  10.7 54.5 all-gather.2
  67.6 104.5 all-gather.4
  270.3 77.1 reduce-scatter.6
  447.6 88.3 reduce-scatter.4

commit v5 on v4

--- a/solution.py
+++ b/solution.py
@@ -22,19 +22,19 @@
     return lax.dot_general(a, b, (((ca,), (cb,)), ((), ())), preferred_element_type=fl)
 
 
-def normalize(values, gain, shift):
+def moments(values):
     mean = jnp.mean(values, axis=-1, keepdims=True)
     centred = values - mean
     variance = jnp.mean(centred * centred, axis=-1, keepdims=True)
-    return centred * lax.rsqrt(variance + epsilon) * gain + shift
-
-
-def normalize_back(values, gain, grad):
-    mean = jnp.mean(values, axis=-1, keepdims=True)
-    centred = values - mean
-    variance = jnp.mean(centred * centred, axis=-1, keepdims=True)
-    inverse = lax.rsqrt(variance + epsilon)
-    hat = centred * inverse
+    return mean, lax.rsqrt(variance + epsilon)
+
+
+def normalize(values, mean, inverse, gain, shift):
+    return (values - mean) * inverse * gain + shift
+
+
+def normalize_back(values, mean, inverse, gain, grad):
+    hat = (values - mean) * inverse
     scaled = grad * gain
     first = jnp.mean(scaled, axis=-1, keepdims=True)
     second = jnp.mean(scaled * hat, axis=-1, keepdims=True)
@@ -255,7 +255,8 @@
 
 def send_blocks(values, where, parts, rows):
     def block(k):
-        return lax.dynamic_slice_in_dim(values, (where + k) % parts * rows, rows, 1)
+        start = (where + k) % parts * rows
+        return jnp.stack([lax.dynamic_slice_in_dim(v, start, rows, 0) for v in values])
 
     shares = [block(0)]
     for k in range(1, parts):
@@ -360,7 +361,8 @@
     dy_own = pad_to(jnp.transpose(cotangent, (1, 0, 2)), 1, rowp) * own_valid.astype(bf)
     dy_others = from_others(dy_own, parts)
 
-    xn1 = normalize(x_all.astype(fl), ln_gain[0], ln_bias[0]).astype(bf)
+    mean1, inverse1 = lax.optimization_barrier(moments(x_all.astype(fl)))
+    xn1 = normalize(x_all.astype(fl), mean1, inverse1, ln_gain[0], ln_bias[0]).astype(bf)
     bias_three = pad_to(
         jnp.stack([qv_bias[0], jnp.zeros_like(qv_bias[0]), qv_bias[1]]), 1, colp
     ).reshape(1, 3 * colp)
@@ -386,8 +388,8 @@
         out, lse = attention_forward(qkv, key_bias, i, size, heads)
         attended.append(out)
         lses.append(lse)
-        if halving:
-            pending, doubling = next_double(pending, doubling, out)
+    if halving:
+        pending, doubling = next_double(pending, doubling, *attended)
     attended = after(attended, *attended)
     for i in range(images):
         others = from_others(attended[i], parts)
@@ -405,7 +407,8 @@
     attended_all = joined[:, :colp]
 
     h1 = x_all.astype(fl) + dot(joined, full_out, 1, 1) + out_bias[0]
-    xn2 = normalize(h1, ln_gain[1], ln_bias[1]).astype(bf)
+    mean2, inverse2 = lax.optimization_barrier(moments(h1))
+    xn2 = normalize(h1, mean2, inverse2, ln_gain[1], ln_bias[1]).astype(bf)
     bias_up = pad_to(up_bias, 0, hidp)[None]
     wide, y_parts, dxn_parts, received, grad_b1 = (), [], [], [], 0.0
     for i in range(images):
@@ -441,7 +444,7 @@
         total = dxn_parts[i].astype(fl)
         for other in got:
             total = total + other.astype(fl)
-        back, hat = normalize_back(h1[at], ln_gain[1], total)
+        back, hat = normalize_back(h1[at], mean2[at], inverse2[at], ln_gain[1], total)
         g2 = g2 + jnp.sum(total * hat, axis=0)
         c2 = c2 + jnp.sum(total, axis=0)
         full = dy_all[at].astype(fl) + back
@@ -454,9 +457,9 @@
         )
     (d_qkv,) = d_qkv
 
-    y_all = after(jnp.stack(y_parts), got)
+    y_parts = after(y_parts, got)
     h1_own = lax.dynamic_slice_in_dim(h1.reshape(images, size, width), where * rowp, rowp, 1)
-    y_own = h1_own + sum_of(send_blocks(y_all, where, parts, rowp)) + out_bias[1]
+    y_own = h1_own + sum_of(send_blocks(y_parts, where, parts, rowp)) + out_bias[1]
     output = jnp.where(own_valid, y_own, 0.0).astype(bf)
 
     grad_qkv = dot(xn1, d_qkv, 0, 0).astype(bf)
@@ -464,22 +467,29 @@
     att_grads = jnp.concatenate([grad_qkv, grad_out], axis=1)
     att_sums = lax.psum_scatter(att_grads, "dp", scatter_dimension=0, tiled=True)
 
-    d_qkv = after(d_qkv, att_grads)
-    sums_qkv = jnp.sum(d_qkv.astype(fl), axis=0)
-    d_xn1 = dot(d_qkv, full_qkv, 1, 1).astype(bf).reshape(images, size, width)
-    shares = send_blocks(d_xn1, where, parts, rowp)
-    d_pre = after(d_pre, d_xn1)
+    d_pre = after(d_pre, att_grads)
     grad_up = dot(xn2, d_pre[:, :hids], 0, 0).astype(bf)
     if halving:
         up_sums, step = grad_up.reshape(ring, here, hids), 1
         pending = exchange_half(up_sums, "dp", step)
     else:
         up_sums, step, pending = lax.psum_scatter(grad_up, "dp", tiled=True), ring, ()
-    pending, step = next_half(pending, step)
+    d_qkv = after(d_qkv, grad_up)
+    sums_qkv = jnp.sum(d_qkv.astype(fl), axis=0)
+    d_xn1 = dot(d_qkv, full_qkv, 1, 1).astype(bf).reshape(images, size, width)
+    d_xn1 = [d_xn1[i] for i in range(images)]
+    shares = send_blocks(d_xn1, where, parts, rowp)
+    pending, step = next_half(pending, step, d_xn1)
     if halving:
         shares = after(shares, *pending[:1])
     d_xn1 = sum_of(shares)
-    back, hat = normalize_back(x_own.astype(fl), ln_gain[0], d_xn1)
+
+    def own_part(values):
+        return lax.dynamic_slice_in_dim(values.reshape(images, size, 1), where * rowp, rowp, 1)
+
+    back, hat = normalize_back(
+        x_own.astype(fl), own_part(mean1), own_part(inverse1), ln_gain[0], d_xn1
+    )
     g1 = jnp.sum(d_xn1 * hat, axis=(0, 1))
     c1 = jnp.sum(d_xn1, axis=(0, 1))
     pending, step = next_half(pending, step, g1)

time: 592 us -> 601 us (1.015)
  local copies, waits for them, and re-layouts: 49.7 us -> 60.6 us
    ppermute x2, waiting for transfers between devices: 60.1 us -> 26.7 us  [send_blocks(): shares.append(lax.ppermute(block(k), 'tensor', pairs))]
    ppermute x4, waiting for transfers between devices: 3.16 us -> 22 us  [exchange_half(): lax.ppermute(send, axis, [(j, j ^ step) for j in range(size)])]
    ppermute x4, waiting for transfers between devices: 8.86 us -> 19.1 us  [start_doubling(): lax.ppermute(have, axis, [(j, j ^ step) for j in range(size)])]
    unnamed x111 -> x119, local copies, waits for them, and re-layouts: 21.4 us -> 26.4 us
  transfers between devices with their start and end apart: 26 -> 26, of which waited for: 11 -> 12; matrix products, arithmetic and copies ran while one was open for 29% -> 30% of each run, Pallas kernels for 14% -> 14%
where the time goes in v5:
time: 601 us; the launch traced here: 593 us
  waiting for transfers between devices  223 us (37%)
  Pallas kernels  134 us (22%)
  matrix products  76.8 us (13%)
  local copies, waits for them, and re-layouts  60.6 us (10%)
  other arithmetic  59.7 us (10%)
  starting transfers between devices  24.1 us (4%)
  between operations  15.2 us (3%)
    ppermute x7, waiting for transfers between devices, from_others(): lax.ppermute(values, 'tensor', [((j + k) % parts, j) for j in range(parts)])  133 us
    dot_general x11, matrix products, dot(): lax.dot_general(a, b, (((ca,), (cb,)), ((), ())), preferred_element_type=fl)  76.8 us
    pallas_call x2, Pallas kernels, mlp(): pl.pallas_call(mlp_kernel, grid=(steps,), out_shape=(jax.ShapeDtypeStruct...  51.7 us
    pallas_call x2, Pallas kernels, attention_backward(): pl.pallas_call(functools.partial(backward_kernel, heads=heads, colp=colp,...  41.2 us
    pallas_call x2, Pallas kernels, attention_forward(): pl.pallas_call(functools.partial(forward_kernel, heads=heads, colp=colp,...  40.6 us
    ppermute x2, waiting for transfers between devices, send_blocks(): shares.append(lax.ppermute(block(k), 'tensor', pairs))  26.7 us
    unnamed x119, local copies, waits for them, and re-layouts  26.4 us
    ppermute x5, waiting for transfers between devices, sum_everywhere(): lax.ppermute(values, axis, [(j, j ^ step) for j in range(size)])  22.1 us
  transfers between devices with their start and end apart: 26, of which 12 were waited for; matrix products, arithmetic and copies ran while one was open for 30% of the time, Pallas kernels for 14%

profile of v5, /device:TPU:0, one launch (start us, length us, event | category | flops | bytes accessed | tf_op | source)
XLA Modules:
  0.0 592.7 jit_solution(3469022511434141401)
XLA Ops:
  20.9 37.2 %collective-permute-done.3 = bf16[72,640]{1,0:T(8,128)(2,1)} collective-permute-done((bf16[72,640]{1,0:T(8,128)(2,1)S(1)}, bf16[72,640]{1,0:T(8,128)(2,1)}, u32[]{:S(2)}, u32[]{:S(2)}) %collective-permute-start.3) | collective-permute-done | bytes 92192 | tf_op jit(solution)/shard_map/ppermute | solution.py:240
  68.8 12.3 %add_convert_fusion.qkv_ref = bf16[1472,1920]{1,0:T(8,128)(2,1)} fusion(bf16[1472,1152]{1,0:T(8,128)(2,1)} %fusion.4, bf16[1152,1920]{1,0:T(8,128)(2,1)} %all-gather.3.cloned.1.call-done, f32[1920]{0:T(1024)S(1)} %add.321), kind=kOutput, calls=%fused_computation.3 | convolution fusion | flops 6517309440 | bytes 13475328 | tf_op jit(solution)/shard_map/dot_general | solution.py:22
  81.2 14.8 %attention_forward.2 = (bf16[736,640]{1,0:T(8,128)(2,1)}, f32[8,736]{1,0:T(8,128)}) custom-call(f32[1472,1]{1,0:T(8,128)} %select_n.243.bias_ref, bf16[1472,1920]{1,0:T(8,128)(2,1)} %add_convert_fusion.qkv_ref), custom_call_target="tpu_custom_call" | custom-call | flops 4437573632 | bytes 3768320 | tf_op jit(solution)/shard_map/attention_forward/pallas_call | solution.py:77
  97.8 25.8 %attention_forward.3 = (bf16[736,640]{1,0:T(8,128)(2,1)}, f32[8,736]{1,0:T(8,128)}) custom-call(f32[1472,1]{1,0:T(8,128)} %select_n.243.bias_ref, bf16[1472,1920]{1,0:T(8,128)(2,1)} %add_convert_fusion.qkv_ref), custom_call_target="tpu_custom_call" | custom-call | flops 4437573632 | bytes 3768320 | tf_op jit(solution)/shard_map/attention_forward/pallas_call | solution.py:77
  134.2 19.0 %collective-permute-done.6 = bf16[4,72,1280]{2,1,0:T(8,128)(2,1)} collective-permute-done((bf16[4,72,1280]{2,1,0:T(8,128)(2,1)}, bf16[4,72,1280]{2,1,0:T(8,128)(2,1)}, u32[]{:S(2)}, u32[]{:S(2)}) %collective-permute-start.6) | collective-permute-done | bytes 737312 | tf_op jit(solution)/shard_map/ppermute | solution.py:274
  165.5 7.4 %collective-permute-done.8 = bf16[2,368,1152]{2,1,0:T(8,128)(2,1)} collective-permute-done((bf16[2,368,1152]{2,1,0:T(8,128)(2,1)}, bf16[2,368,1152]{2,1,0:T(8,128)(2,1)}, u32[]{:S(2)}, u32[]{:S(2)}) %collective-permute-start.8) | collective-permute-done | bytes 1695776 | tf_op jit(solution)/shard_map/ppermute | solution.py:240
  178.2 14.8 %collective-permute-done.2 = bf16[736,640]{1,0:T(8,128)(2,1)S(1)} collective-permute-done((bf16[736,640]{1,0:T(8,128)(2,1)}, bf16[736,640]{1,0:T(8,128)(2,1)S(1)}, u32[]{:S(2)}, u32[]{:S(2)}) %collective-permute-start.2) | collective-permute-done | bytes 942112 | tf_op jit(solution)/shard_map/ppermute | solution.py:240
  193.0 17.4 %collective-permute-done.1 = bf16[736,640]{1,0:T(8,128)(2,1)S(1)} collective-permute-done((bf16[736,640]{1,0:T(8,128)(2,1)}, bf16[736,640]{1,0:T(8,128)(2,1)S(1)}, u32[]{:S(2)}, u32[]{:S(2)}) %collective-permute-start.1) | collective-permute-done | bytes 942112 | tf_op jit(solution)/shard_map/ppermute | solution.py:240
  210.4 5.5 fusion.82
  219.0 4.9 add_convert_fusion.1.xn_ref
  223.9 25.7 %mlp.2 = (bf16[1472,2304]{1,0:T(8,128)(2,1)}, bf16[1472,2304]{1,0:T(8,128)(2,1)}, f32[1,2304]{1,0:T(1,128)}, bf16[736,1152]{1,0:T(8,128)(2,1)}, bf16[736,1152]{1,0:T(8,128)(2,1)}) custom-call(bf16[1472,1152]{1,0:T(8,128)(2,1)} %add_convert_fusion.1.xn_ref, bf16[1472,1152]{1,0:T(8,128)(2,1)} %bitcast.19.dy_ref, ...), custom_call_target="tpu_custom_call" | custom-call | flops 15627976704 | bytes 24182784 | tf_op jit(solution)/shard_map/mlp/pallas_call | solution.py:207
  249.5 26.1 %mlp.3 = (bf16[1472,2304]{1,0:T(8,128)(2,1)}, bf16[1472,2304]{1,0:T(8,128)(2,1)}, f32[1,2304]{1,0:T(1,128)}, bf16[736,1152]{1,0:T(8,128)(2,1)}, bf16[736,1152]{1,0:T(8,128)(2,1)}) custom-call(bf16[1472,1152]{1,0:T(8,128)(2,1)} %add_convert_fusion.1.xn_ref, bf16[1472,1152]{1,0:T(8,128)(2,1)} %bitcast.19.dy_ref, ...), custom_call_target="tpu_custom_call", output_to_operand_aliasing={{0}: (5, {}), {1}: (6, {})} | custom-call | flops 15627976704 | bytes 24182784 | tf_op jit(solution)/shard_map/mlp/pallas_call | solution.py:207
  277.7 14.1 %convolution_convert_fusion.1 = bf16[1152,2176]{1,0:T(8,128)(2,1)} fusion(bf16[1472,1152]{1,0:T(8,128)(2,1)} %bitcast.19.dy_ref, bf16[1472,2304]{1,0:T(8,128)(2,1)} %get-tuple-element.62), kind=kOutput, calls=%fused_computation.1 | convolution fusion | flops 7382384640 | bytes 14811136 | tf_op jit(solution)/shard_map/dot_general | solution.py:22
  292.6 55.9 %collective-permute-done.10 = bf16[736,1152]{1,0:T(8,128)(2,1)S(1)} collective-permute-done((bf16[736,1152]{1,0:T(8,128)(2,1)S(1)}, bf16[736,1152]{1,0:T(8,128)(2,1)S(1)}, u32[]{:S(2)}, u32[]{:S(2)}) %collective-permute-start.10) | collective-permute-done | bytes 1695776 | tf_op jit(solution)/shard_map/ppermute | solution.py:240
  348.5 4.0 multiply_reduce_fusion.3
  352.5 3.4 fusion.74
  361.5 20.6 %attention_backward.2.refs_0_ = bf16[1472,1920]{1,0:T(8,128)(2,1)} custom-call(f32[1472,1]{1,0:T(8,128)} %select_n.243.bias_ref, bf16[1472,1920]{1,0:T(8,128)(2,1)} %add_convert_fusion.qkv_ref, bf16[736,640]{1,0:T(8,128)(2,1)} %get-tuple-element.49.out_ref, bf16[736,640]{1,0:T(8,128)(2,1)} %convolution_convert_fusion.5.dout_ref, ...), custom_call_target="tpu_custom_call" | custom-call | flops 11093934080 | bytes 7536640 | tf_op jit(solution)/shard_map/attention_backward/pallas_call | solution.py:144
  382.2 3.4 dynamic-slice_bitcast_fusion.11
  388.4 3.4 multiply_reduce_fusion.2
  391.8 3.2 fusion.73
  400.6 20.6 %attention_backward.3 = bf16[1472,1920]{1,0:T(8,128)(2,1)} custom-call(f32[1472,1]{1,0:T(8,128)} %select_n.243.bias_ref, bf16[1472,1920]{1,0:T(8,128)(2,1)} %add_convert_fusion.qkv_ref, bf16[736,640]{1,0:T(8,128)(2,1)} %get-tuple-element.50.out_ref, bf16[736,640]{1,0:T(8,128)(2,1)} %convolution_convert_fusion.4.dout_ref, ...), custom_call_target="tpu_custom_call", output_to_operand_aliasing={{}: (5, {})} | custom-call | flops 11093934080 | bytes 7536640 | tf_op jit(solution)/shard_map/attention_backward/pallas_call | solution.py:144
  421.3 10.0 %convolution_convert_fusion.2 = bf16[1152,1920]{1,0:T(8,128)(2,1)S(1)} fusion(bf16[1472,1152]{1,0:T(8,128)(2,1)S(1)} %copy-done.14, bf16[1472,1920]{1,0:T(8,128)(2,1)} %attention_backward.3), kind=kOutput, calls=%fused_computation.6 | convolution fusion | flops 6513868800 | bytes 13467648 | tf_op jit(solution)/shard_map/dot_general | solution.py:22
  437.3 12.2 %convolution_convert_fusion = bf16[1152,2176]{1,0:T(8,128)(2,1)S(1)} fusion(bf16[1472,1152]{1,0:T(8,128)(2,1)} %add_convert_fusion.1.xn_ref, bf16[1472,2304]{1,0:T(8,128)(2,1)} %get-tuple-element.71), kind=kOutput, calls=%fused_computation | convolution fusion | flops 7382384640 | bytes 14811136 | tf_op jit(solution)/shard_map/dot_general | solution.py:22
  453.5 10.7 %convolution_convert_fusion.3 = bf16[1472,1152]{1,0:T(8,128)(2,1)S(1)} fusion(bf16[1472,1920]{1,0:T(8,128)(2,1)S(1)} %bitcast.146, bf16[1152,1920]{1,0:T(8,128)(2,1)} %all-gather.3.cloned.1.call-done), kind=kOutput, calls=%fused_computation.7 | convolution fusion | flops 6513352704 | bytes 13467648 | tf_op jit(solution)/shard_map/dot_general | solution.py:22
  469.3 3.4 dynamic-slice_bitcast_fusion.1
  472.7 3.5 fusion.7
  480.3 26.7 %collective-permute-done.12 = bf16[2,368,1152]{2,1,0:T(8,128)(2,1)} collective-permute-done((bf16[2,368,1152]{2,1,0:T(8,128)(2,1)}, bf16[2,368,1152]{2,1,0:T(8,128)(2,1)}, u32[]{:S(2)}, u32[]{:S(2)}) %collective-permute-start.12) | collective-permute-done | bytes 1695776 | tf_op jit(solution)/shard_map/ppermute | solution.py:264
  507.1 4.3 fusion.35
  512.2 3.3 collective-permute-done.14
  519.4 3.2 fusion.46
  531.2 15.8 %collective-permute-done.17 = f32[10216]{0:T(1024)S(1)} collective-permute-done((f32[10216]{0:T(1024)S(1)}, f32[10216]{0:T(1024)S(1)}, u32[]{:S(2)}, u32[]{:S(2)}) %collective-permute-start.17) | collective-permute-done | bytes 40896 | tf_op jit(solution)/shard_map/ppermute | solution.py:299
  557.6 20.3 %collective-permute-done.21 = bf16[1,72,2176]{2,1,0:T(8,128)(2,1)} collective-permute-done((bf16[1,72,2176]{2,1,0:T(8,128)(2,1)}, bf16[1,72,2176]{2,1,0:T(8,128)(2,1)}, u32[]{:S(2)}, u32[]{:S(2)}) %collective-permute-start.21) | collective-permute-done | bytes 313376 | tf_op jit(solution)/shard_map/ppermute | solution.py:290
  (282 shorter events, 124.5 us)
Async XLA Ops:
  7.2 58.8 %all-gather.3.cloned.1.call-start = ((), (), s32[]{:S(2)}) async-start(), calls=%async_computation.2 | async-start | bytes 4700160 | tf_op jit(solution)/shard_map/all_gather | solution.py:347
  9.4 214.5 %all-gather.5.cloned.1.call-start = ((), (), s32[]{:S(2)}) async-start(), calls=%async_computation.3 | async-start | bytes 11280384 | tf_op jit(solution)/shard_map/all_gather | solution.py:353
  11.4 568.5 %reduce-scatter.7.cloned.1.call-start = ((), (), s32[]{:S(2)}) async-start(), calls=%async_computation.5 | async-start | bytes 5326848
  15.9 43.9 %collective-permute-start = (bf16[2,368,1152]{2,1,0:T(8,128)(2,1)}, bf16[2,368,1152]{2,1,0:T(8,128)(2,1)}, u32[]{:S(2)}, u32[]{:S(2)}) collective-permute-start(bf16[2,368,1152]{2,1,0:T(8,128)(2,1)} %get-tuple-element.174), channel_id=1, source_target_pairs={{1,0},{0,1},{3,2},{2,3},{5,4},{4,5},{7,6},{6,7},{9,8},{8,9},{11,10... | collective-permute-start | bytes 5087240 | tf_op jit(solution)/shard_map/ppermute | solution.py:240
  18.9 39.3 %collective-permute-start.3 = (bf16[72,640]{1,0:T(8,128)(2,1)S(1)}, bf16[72,640]{1,0:T(8,128)(2,1)}, u32[]{:S(2)}, u32[]{:S(2)}) collective-permute-start(bf16[72,640]{1,0:T(8,128)(2,1)S(1)} %pad.33), channel_id=1, source_target_pairs={{1,0},{0,1},{3,2},{2,3},{5,4},{4,5},{7,6},{6,7},{9,8},{8,9},{11,10... | collective-permute-start | bytes 276488 | tf_op jit(solution)/shard_map/ppermute | solution.py:240
  20.9 42.4 %copy-start.27 = (f32[1152]{0:T(1024)}, f32[1152]{0:T(1024)S(1)}, u32[]{:S(2)}) copy-start(f32[1152]{0:T(1024)S(1)} %get-tuple-element.136) | copy-start | bytes 13828
  66.0 29.9 %collective-permute-start.4 = (bf16[1,72,1280]{2,1,0:T(8,128)(2,1)}, bf16[1,72,1280]{2,1,0:T(8,128)(2,1)S(1)}, u32[]{:S(2)}, u32[]{:S(2)}) collective-permute-start(bf16[1,72,1280]{2,1,0:T(8,128)(2,1)} %bitcast.158), channel_id=1, source_target_pairs={{0,16},{2,18},{4,20},{6,22},{8,24},{10,26},{12,28},{14,30},{16,0},... | collective-permute-start | bytes 552968 | tf_op jit(solution)/shard_map/ppermute | solution.py:274
  96.1 27.6 %collective-permute-start.5 = (bf16[2,72,1280]{2,1,0:T(8,128)(2,1)S(1)}, bf16[2,72,1280]{2,1,0:T(8,128)(2,1)S(1)}, u32[]{:S(2)}, u32[]{:S(2)}) collective-permute-start(bf16[2,72,1280]{2,1,0:T(8,128)(2,1)S(1)} %maximum_bitcast_fusion), channel_id=1, source_target_pairs={{0,8},{2,10},{4,12},{6,14},{8,0},{10,2},{12,4},{14,6},{16,24},{18,... | collective-permute-start | bytes 1105928 | tf_op jit(solution)/shard_map/ppermute | solution.py:274
  124.6 28.6 %collective-permute-start.6 = (bf16[4,72,1280]{2,1,0:T(8,128)(2,1)}, bf16[4,72,1280]{2,1,0:T(8,128)(2,1)}, u32[]{:S(2)}, u32[]{:S(2)}) collective-permute-start(bf16[4,72,1280]{2,1,0:T(8,128)(2,1)} %bitcast.10), channel_id=1, source_target_pairs={{0,4},{2,6},{4,0},{6,2},{8,12},{10,14},{12,8},{14,10},{16,20},{18,... | collective-permute-start | bytes 2211848 | tf_op jit(solution)/shard_map/ppermute | solution.py:274
  132.7 40.2 %collective-permute-start.8 = (bf16[2,368,1152]{2,1,0:T(8,128)(2,1)}, bf16[2,368,1152]{2,1,0:T(8,128)(2,1)}, u32[]{:S(2)}, u32[]{:S(2)}) collective-permute-start(bf16[2,368,1152]{2,1,0:T(8,128)(2,1)} %get-tuple-element.146), channel_id=1, source_target_pairs={{1,0},{0,1},{3,2},{2,3},{5,4},{4,5},{7,6},{6,7},{9,8},{8,9},{11,10... | collective-permute-start | bytes 5087240 | tf_op jit(solution)/shard_map/ppermute | solution.py:240
  156.1 19.6 %collective-permute-start.7 = (bf16[8,72,1280]{2,1,0:T(8,128)(2,1)}, bf16[8,72,1280]{2,1,0:T(8,128)(2,1)}, u32[]{:S(2)}, u32[]{:S(2)}) collective-permute-start(bf16[8,72,1280]{2,1,0:T(8,128)(2,1)} %bitcast.13), channel_id=1, source_target_pairs={{0,2},{2,0},{4,6},{6,4},{8,10},{10,8},{12,14},{14,12},{16,18},{18,... | collective-permute-start | bytes 4423688 | tf_op jit(solution)/shard_map/ppermute | solution.py:274
  163.5 29.5 %collective-permute-start.2 = (bf16[736,640]{1,0:T(8,128)(2,1)}, bf16[736,640]{1,0:T(8,128)(2,1)S(1)}, u32[]{:S(2)}, u32[]{:S(2)}) collective-permute-start(bf16[736,640]{1,0:T(8,128)(2,1)} %get-tuple-element.50.out_ref), channel_id=1, source_target_pairs={{1,0},{0,1},{3,2},{2,3},{5,4},{4,5},{7,6},{6,7},{9,8},{8,9},{11,10... | collective-permute-start | bytes 2826248 | tf_op jit(solution)/shard_map/ppermute | solution.py:240
  165.0 45.4 %collective-permute-start.1 = (bf16[736,640]{1,0:T(8,128)(2,1)}, bf16[736,640]{1,0:T(8,128)(2,1)S(1)}, u32[]{:S(2)}, u32[]{:S(2)}) collective-permute-start(bf16[736,640]{1,0:T(8,128)(2,1)} %get-tuple-element.49.out_ref), channel_id=1, source_target_pairs={{1,0},{0,1},{3,2},{2,3},{5,4},{4,5},{7,6},{6,7},{9,8},{8,9},{11,10... | collective-permute-start | bytes 2826248 | tf_op jit(solution)/shard_map/ppermute | solution.py:240
  178.0 32.4 %copy-start.42 = (bf16[736,640]{1,0:T(8,128)(2,1)S(1)}, bf16[736,640]{1,0:T(8,128)(2,1)}, u32[]{:S(2)}) copy-start(bf16[736,640]{1,0:T(8,128)(2,1)} %get-tuple-element.49.out_ref) | copy-start | bytes 2826244
  178.0 32.4 %copy-start.44 = (bf16[736,640]{1,0:T(8,128)(2,1)S(1)}, bf16[736,640]{1,0:T(8,128)(2,1)}, u32[]{:S(2)}) copy-start(bf16[736,640]{1,0:T(8,128)(2,1)} %get-tuple-element.50.out_ref) | copy-start | bytes 2826244
  178.2 37.7 %copy-start.17 = (bf16[8,2,72,1280]{3,2,1,0:T(8,128)(2,1)}, bf16[8,2,72,1280]{3,2,1,0:T(8,128)(2,1)S(1)}, u32[]{:S(2)}) copy-start(bf16[8,2,72,1280]{3,2,1,0:T(8,128)(2,1)S(1)} %copy.71) | copy-start | bytes 8847364
  275.6 106.5 %collective-permute-start.9 = (bf16[736,1152]{1,0:T(8,128)(2,1)}, bf16[736,1152]{1,0:T(8,128)(2,1)}, u32[]{:S(2)}, u32[]{:S(2)}) collective-permute-start(bf16[736,1152]{1,0:T(8,128)(2,1)} %get-tuple-element.61), channel_id=1, source_target_pairs={{1,0},{0,1},{3,2},{2,3},{5,4},{4,5},{7,6},{6,7},{9,8},{8,9},{11,10... | collective-permute-start | bytes 5087240 | tf_op jit(solution)/shard_map/ppermute | solution.py:240
  277.2 71.3 %collective-permute-start.10 = (bf16[736,1152]{1,0:T(8,128)(2,1)S(1)}, bf16[736,1152]{1,0:T(8,128)(2,1)S(1)}, u32[]{:S(2)}, u32[]{:S(2)}) collective-permute-start(bf16[736,1152]{1,0:T(8,128)(2,1)S(1)} %copy-done.10), channel_id=1, source_target_pairs={{1,0},{0,1},{3,2},{2,3},{5,4},{4,5},{7,6},{6,7},{9,8},{8,9},{11,10... | collective-permute-start | bytes 5087240 | tf_op jit(solution)/shard_map/ppermute | solution.py:240
  291.8 290.1 %reduce-scatter.5.cloned.1.call-start = ((), (), s32[]{:S(2)}) async-start(), calls=%async_computation.4 | async-start | bytes 6266880 | tf_op jit(solution)/shard_map/reduce_scatter | solution.py:468
  359.0 29.4 %slice-start = ((s8[6782976]{0:T(1024)(128)(4,1)}), s8[4194304]{0:T(1024)(128)(4,1)S(1)}, s32[]{:S(2)}) async-start(s8[6782976]{0:T(1024)(128)(4,1)} %bitcast.138), calls=%async_computation.6 | async-start | bytes 8388608
  386.9 132.5 %collective-permute-start.11 = (bf16[2,368,1152]{2,1,0:T(8,128)(2,1)}, bf16[2,368,1152]{2,1,0:T(8,128)(2,1)}, u32[]{:S(2)}, u32[]{:S(2)}) collective-permute-start(bf16[2,368,1152]{2,1,0:T(8,128)(2,1)} %pad_maximum_fusion.3), channel_id=1, source_target_pairs={{0,1},{1,0},{2,3},{3,2},{4,5},{5,4},{6,7},{7,6},{8,9},{9,8},{10,11... | collective-permute-start | bytes 5087240 | tf_op jit(solution)/shard_map/ppermute | solution.py:264
  453.5 19.2 %collective-permute-start.13 = (bf16[8,72,2176]{2,1,0:T(8,128)(2,1)}, bf16[8,72,2176]{2,1,0:T(8,128)(2,1)}, u32[]{:S(2)}, u32[]{:S(2)}) collective-permute-start(bf16[8,72,2176]{2,1,0:T(8,128)(2,1)} %dynamic-slice_bitcast_fusion), channel_id=1, source_target_pairs={{0,2},{2,0},{4,6},{6,4},{8,10},{10,8},{12,14},{14,12},{16,18},{18,... | collective-permute-start | bytes 7520264 | tf_op jit(solution)/shard_map/ppermute | solution.py:290
  467.3 39.7 %collective-permute-start.12 = (bf16[2,368,1152]{2,1,0:T(8,128)(2,1)}, bf16[2,368,1152]{2,1,0:T(8,128)(2,1)}, u32[]{:S(2)}, u32[]{:S(2)}) collective-permute-start(bf16[2,368,1152]{2,1,0:T(8,128)(2,1)} %pad_maximum_fusion.5), channel_id=1, source_target_pairs={{0,1},{1,0},{2,3},{3,2},{4,5},{5,4},{6,7},{7,6},{8,9},{9,8},{10,11... | collective-permute-start | bytes 5087240 | tf_op jit(solution)/shard_map/ppermute | solution.py:264
  477.9 39.4 %collective-permute-start.19 = (bf16[4,72,2176]{2,1,0:T(8,128)(2,1)}, bf16[4,72,2176]{2,1,0:T(8,128)(2,1)}, u32[]{:S(2)}, u32[]{:S(2)}) collective-permute-start(bf16[4,72,2176]{2,1,0:T(8,128)(2,1)} %get-tuple-element.163), channel_id=1, source_target_pairs={{0,4},{2,6},{4,0},{6,2},{8,12},{10,14},{12,8},{14,10},{16,20},{18,... | collective-permute-start | bytes 3760136 | tf_op jit(solution)/shard_map/ppermute | solution.py:290
  511.5 4.0 collective-permute-start.14
  515.6 9.5 %collective-permute-start.15 = (f32[10216]{0:T(1024)S(1)}, f32[10216]{0:T(1024)S(1)}, u32[]{:S(2)}, u32[]{:S(2)}) collective-permute-start(f32[10216]{0:T(1024)S(1)} %concatenate.31), channel_id=1, source_target_pairs={{0,2},{2,0},{4,6},{6,4},{8,10},{10,8},{12,14},{14,12},{16,18},{18,... | collective-permute-start | bytes 122600 | tf_op jit(solution)/shard_map/ppermute | solution.py:299
  519.3 29.5 %collective-permute-start.20 = (bf16[2,72,2176]{2,1,0:T(8,128)(2,1)S(1)}, bf16[2,72,2176]{2,1,0:T(8,128)(2,1)S(1)}, u32[]{:S(2)}, u32[]{:S(2)}) collective-permute-start(bf16[2,72,2176]{2,1,0:T(8,128)(2,1)S(1)} %dynamic-slice_bitcast_fusion.13), channel_id=1, source_target_pairs={{0,8},{2,10},{4,12},{6,14},{8,0},{10,2},{12,4},{14,6},{16,24},{18,... | collective-permute-start | bytes 1880072 | tf_op jit(solution)/shard_map/ppermute | solution.py:290
  519.4 31.5 %copy-start.8 = (f32[1,368,1152]{2,1,0:T(8,128)S(1)}, f32[1,368,1152]{2,1,0:T(8,128)}, u32[]{:S(2)}) copy-start(f32[1,368,1152]{2,1,0:T(8,128)} %get-tuple-element.196) | copy-start | bytes 5087236
  525.1 4.1 collective-permute-start.16
  529.2 17.8 %collective-permute-start.17 = (f32[10216]{0:T(1024)S(1)}, f32[10216]{0:T(1024)S(1)}, u32[]{:S(2)}, u32[]{:S(2)}) collective-permute-start(f32[10216]{0:T(1024)S(1)} %add.357), channel_id=1, source_target_pairs={{0,8},{2,10},{4,12},{6,14},{8,0},{10,2},{12,4},{14,6},{16,24},{18,... | collective-permute-start | bytes 122600 | tf_op jit(solution)/shard_map/ppermute | solution.py:299
  547.0 7.4 %collective-permute-start.18 = (f32[10216]{0:T(1024)S(1)}, f32[10216]{0:T(1024)S(1)}, u32[]{:S(2)}, u32[]{:S(2)}) collective-permute-start(f32[10216]{0:T(1024)S(1)} %add.358), channel_id=1, source_target_pairs={{0,16},{2,18},{4,20},{6,22},{8,24},{10,26},{12,28},{14,30},{16,0},... | collective-permute-start | bytes 122600 | tf_op jit(solution)/shard_map/ppermute | solution.py:299
  549.8 28.1 %collective-permute-start.21 = (bf16[1,72,2176]{2,1,0:T(8,128)(2,1)}, bf16[1,72,2176]{2,1,0:T(8,128)(2,1)}, u32[]{:S(2)}, u32[]{:S(2)}) collective-permute-start(bf16[1,72,2176]{2,1,0:T(8,128)(2,1)} %constant_dynamic-slice_fusion), channel_id=1, source_target_pairs={{0,16},{2,18},{4,20},{6,22},{8,24},{10,26},{12,28},{14,30},{16,0},... | collective-permute-start | bytes 940040 | tf_op jit(solution)/shard_map/ppermute | solution.py:290
  (50 other events, 508.7 us)
Sparse Core Ops, SparseCore 0:
  10.7 54.4 all-gather.2
  67.5 100.9 all-gather.4
  292.0 73.6 reduce-scatter.6
  468.1 110.3 reduce-scatter.4

commit v6 on v5

--- a/solution.py
+++ b/solution.py
@@ -423,6 +423,13 @@
     grad_down = dot(dy_all, act[:, :hids], 0, 0).astype(bf)
     down_sums = lax.psum_scatter(grad_down, "dp", scatter_dimension=0, tiled=True)
     down_sums = lax.optimization_barrier(down_sums)
+    d_pre = after(d_pre, grad_down)
+    grad_up = dot(xn2, d_pre[:, :hids], 0, 0).astype(bf)
+    if halving:
+        up_sums, step = grad_up.reshape(ring, here, hids), 1
+        pending = exchange_half(up_sums, "dp", step)
+    else:
+        up_sums, step, pending = lax.psum_scatter(grad_up, "dp", tiled=True), ring, ()
 
     def next_half(pending, step, *others):
         if not halving or step == ring:
@@ -440,7 +447,7 @@
     g2, c2, bo = 0.0, 0.0, 0.0
     for i in range(images):
         at = slice(i * size, (i + 1) * size)
-        got = after(received[i], grad_down, *d_qkv)
+        got = after(received[i], grad_up, grad_down, *d_qkv)
         total = dxn_parts[i].astype(fl)
         for other in got:
             total = total + other.astype(fl)
@@ -455,31 +462,29 @@
         d_qkv = (
             attention_backward(qkv, key_bias, attended[i], d_att, lses[i], d_qkv, i, size, heads),
         )
+        if i < images - 1:
+            pending, step = next_half(pending, step, *d_qkv)
     (d_qkv,) = d_qkv
 
     y_parts = after(y_parts, got)
-    h1_own = lax.dynamic_slice_in_dim(h1.reshape(images, size, width), where * rowp, rowp, 1)
-    y_own = h1_own + sum_of(send_blocks(y_parts, where, parts, rowp)) + out_bias[1]
-    output = jnp.where(own_valid, y_own, 0.0).astype(bf)
+    y_shares = send_blocks(y_parts, where, parts, rowp)
 
     grad_qkv = dot(xn1, d_qkv, 0, 0).astype(bf)
     grad_out = dot(jnp.concatenate(d_h1_b, axis=0), attended_all, 0, 0).astype(bf)
     att_grads = jnp.concatenate([grad_qkv, grad_out], axis=1)
     att_sums = lax.psum_scatter(att_grads, "dp", scatter_dimension=0, tiled=True)
 
-    d_pre = after(d_pre, att_grads)
-    grad_up = dot(xn2, d_pre[:, :hids], 0, 0).astype(bf)
-    if halving:
-        up_sums, step = grad_up.reshape(ring, here, hids), 1
-        pending = exchange_half(up_sums, "dp", step)
-    else:
-        up_sums, step, pending = lax.psum_scatter(grad_up, "dp", tiled=True), ring, ()
-    d_qkv = after(d_qkv, grad_up)
+    pending, step = next_half(pending, step, att_grads)
+    d_qkv = after(d_qkv, att_grads, *pending[:1])
     sums_qkv = jnp.sum(d_qkv.astype(fl), axis=0)
     d_xn1 = dot(d_qkv, full_qkv, 1, 1).astype(bf).reshape(images, size, width)
     d_xn1 = [d_xn1[i] for i in range(images)]
     shares = send_blocks(d_xn1, where, parts, rowp)
-    pending, step = next_half(pending, step, d_xn1)
+    y_shares = after(y_shares, *d_xn1)
+    h1_own = lax.dynamic_slice_in_dim(h1.reshape(images, size, width), where * rowp, rowp, 1)
+    y_own = h1_own + sum_of(y_shares) + out_bias[1]
+    output = jnp.where(own_valid, y_own, 0.0).astype(bf)
+    pending, step = next_half(pending, step, *d_xn1)
     if halving:
         shares = after(shares, *pending[:1])
     d_xn1 = sum_of(shares)
@@ -492,7 +497,6 @@
     )
     g1 = jnp.sum(d_xn1 * hat, axis=(0, 1))
     c1 = jnp.sum(d_xn1, axis=(0, 1))
-    pending, step = next_half(pending, step, g1)
     d_h1_own = jnp.stack([lax.dynamic_slice_in_dim(d, where * rowp, rowp, 0) for d in d_h1])
     d_inputs = (d_h1_own + back).astype(bf)
 

time: 601 us -> 556 us (0.925)
  waiting for transfers between devices: 223 us -> 173 us
  starting transfers between devices: 24.1 us -> 31.2 us
  local copies, waits for them, and re-layouts: 60.6 us -> 53.6 us
    ppermute x2, waiting for transfers between devices: 26.7 us -> 0.01 us  [send_blocks(): shares.append(lax.ppermute(block(k), 'tensor', pairs))]
    ppermute x5, waiting for transfers between devices: 22.1 us -> 6.55 us  [sum_everywhere(): lax.ppermute(values, axis, [(j, j ^ step) for j in range(size)])]
    ppermute x7, waiting for transfers between devices: 133 us -> 119 us  [from_others(): lax.ppermute(values, 'tensor', [((j + k) % parts, j) for j in range(parts)])]
    ppermute x4, waiting for transfers between devices: 22 us -> 29.3 us  [exchange_half(): lax.ppermute(send, axis, [(j, j ^ step) for j in range(size)])]
    unnamed x119 -> x105, local copies, waits for them, and re-layouts: 26.4 us -> 24.5 us
  transfers between devices with their start and end apart: 26 -> 26, of which waited for: 12 -> 10; matrix products, arithmetic and copies ran while one was open for 30% -> 32% of each run, Pallas kernels for 14% -> 15%
where the time goes in v6:
time: 556 us; the launch traced here: 547 us
  waiting for transfers between devices  173 us (31%)
  Pallas kernels  133 us (24%)
  matrix products  79.5 us (14%)
  other arithmetic  60.9 us (11%)
  local copies, waits for them, and re-layouts  53.6 us (10%)
  starting transfers between devices  31.2 us (6%)
  between operations  15.2 us (3%)
    ppermute x7, waiting for transfers between devices, from_others(): lax.ppermute(values, 'tensor', [((j + k) % parts, j) for j in range(parts)])  119 us
    dot_general x11, matrix products, dot(): lax.dot_general(a, b, (((ca,), (cb,)), ((), ())), preferred_element_type=fl)  79.5 us
    pallas_call x2, Pallas kernels, mlp(): pl.pallas_call(mlp_kernel, grid=(steps,), out_shape=(jax.ShapeDtypeStruct...  51.6 us
    pallas_call x2, Pallas kernels, attention_backward(): pl.pallas_call(functools.partial(backward_kernel, heads=heads, colp=colp,...  41 us
    pallas_call x2, Pallas kernels, attention_forward(): pl.pallas_call(functools.partial(forward_kernel, heads=heads, colp=colp,...  40.6 us
    ppermute x4, waiting for transfers between devices, exchange_half(): lax.ppermute(send, axis, [(j, j ^ step) for j in range(size)])  29.3 us
    unnamed x105, local copies, waits for them, and re-layouts  24.5 us
    ppermute x4, waiting for transfers between devices, start_doubling(): lax.ppermute(have, axis, [(j, j ^ step) for j in range(size)])  18.5 us
  transfers between devices with their start and end apart: 26, of which 10 were waited for; matrix products, arithmetic and copies ran while one was open for 32% of the time, Pallas kernels for 15%

profile of v6, /device:TPU:0, one launch (start us, length us, event | category | flops | bytes accessed | tf_op | source)
XLA Modules:
  0.0 547.0 jit_solution(9205543952081638046)
XLA Ops:
  21.0 37.2 %collective-permute-done.3 = bf16[72,640]{1,0:T(8,128)(2,1)} collective-permute-done((bf16[72,640]{1,0:T(8,128)(2,1)S(1)}, bf16[72,640]{1,0:T(8,128)(2,1)}, u32[]{:S(2)}, u32[]{:S(2)}) %collective-permute-start.3) | collective-permute-done | bytes 92192 | tf_op jit(solution)/shard_map/ppermute | solution.py:240
  68.9 12.3 %add_convert_fusion.qkv_ref = bf16[1472,1920]{1,0:T(8,128)(2,1)} fusion(bf16[1472,1152]{1,0:T(8,128)(2,1)} %fusion.4, bf16[1152,1920]{1,0:T(8,128)(2,1)} %all-gather.3.cloned.1.call-done, f32[1920]{0:T(1024)S(1)} %add.321), kind=kOutput, calls=%fused_computation.3 | convolution fusion | flops 6517309440 | bytes 13475328 | tf_op jit(solution)/shard_map/dot_general | solution.py:22
  81.2 14.8 %attention_forward.2 = (bf16[736,640]{1,0:T(8,128)(2,1)}, f32[8,736]{1,0:T(8,128)}) custom-call(f32[1472,1]{1,0:T(8,128)} %select_n.243.bias_ref, bf16[1472,1920]{1,0:T(8,128)(2,1)} %add_convert_fusion.qkv_ref), custom_call_target="tpu_custom_call" | custom-call | flops 4437573632 | bytes 3768320 | tf_op jit(solution)/shard_map/attention_forward/pallas_call | solution.py:77
  97.8 25.9 %attention_forward.3 = (bf16[736,640]{1,0:T(8,128)(2,1)}, f32[8,736]{1,0:T(8,128)}) custom-call(f32[1472,1]{1,0:T(8,128)} %select_n.243.bias_ref, bf16[1472,1920]{1,0:T(8,128)(2,1)} %add_convert_fusion.qkv_ref), custom_call_target="tpu_custom_call" | custom-call | flops 4437573632 | bytes 3768320 | tf_op jit(solution)/shard_map/attention_forward/pallas_call | solution.py:77
  134.3 18.5 %collective-permute-done.6 = bf16[4,72,1280]{2,1,0:T(8,128)(2,1)} collective-permute-done((bf16[4,72,1280]{2,1,0:T(8,128)(2,1)}, bf16[4,72,1280]{2,1,0:T(8,128)(2,1)}, u32[]{:S(2)}, u32[]{:S(2)}) %collective-permute-start.6) | collective-permute-done | bytes 737312 | tf_op jit(solution)/shard_map/ppermute | solution.py:274
  165.0 8.0 %collective-permute-done.8 = bf16[2,368,1152]{2,1,0:T(8,128)(2,1)} collective-permute-done((bf16[2,368,1152]{2,1,0:T(8,128)(2,1)}, bf16[2,368,1152]{2,1,0:T(8,128)(2,1)}, u32[]{:S(2)}, u32[]{:S(2)}) %collective-permute-start.8) | collective-permute-done | bytes 1695776 | tf_op jit(solution)/shard_map/ppermute | solution.py:240
  178.3 14.8 %collective-permute-done.2 = bf16[736,640]{1,0:T(8,128)(2,1)S(1)} collective-permute-done((bf16[736,640]{1,0:T(8,128)(2,1)}, bf16[736,640]{1,0:T(8,128)(2,1)S(1)}, u32[]{:S(2)}, u32[]{:S(2)}) %collective-permute-start.2) | collective-permute-done | bytes 942112 | tf_op jit(solution)/shard_map/ppermute | solution.py:240
  193.1 17.3 %collective-permute-done.1 = bf16[736,640]{1,0:T(8,128)(2,1)S(1)} collective-permute-done((bf16[736,640]{1,0:T(8,128)(2,1)}, bf16[736,640]{1,0:T(8,128)(2,1)S(1)}, u32[]{:S(2)}, u32[]{:S(2)}) %collective-permute-start.1) | collective-permute-done | bytes 942112 | tf_op jit(solution)/shard_map/ppermute | solution.py:240
  210.4 5.6 %fusion.82 = (f32[1472]{0:T(1024)S(1)}, f32[1472,1152]{1,0:T(8,128)S(1)}) fusion(f32[1152]{0:T(1024)S(1)} %get-tuple-element.146, bf16[1152,1280]{1,0:T(8,128)(2,1)S(1)} %bitcast.153, bf16[736,640]{1,0:T(8,128)(2,1)S(1)} %collective-permute-done.2, bf16[736,640]{1,0:T(8,128)(2,1)S(1)} %copy-done.33, bf16[736,640]{1,0:T(8,128)(2,1)S(1)} %collective-permute-done.1, ...), kind=kOutput, calls=%fused_computation.199 | convolution fusion | flops 4362959360 | bytes 16902400 | tf_op jit(solution)/shard_map/dot_general | solution.py:22
  219.0 4.8 add_convert_fusion.1.xn_ref
  223.9 25.6 %mlp.2 = (bf16[1472,2304]{1,0:T(8,128)(2,1)}, bf16[1472,2304]{1,0:T(8,128)(2,1)}, f32[1,2304]{1,0:T(1,128)}, bf16[736,1152]{1,0:T(8,128)(2,1)}, bf16[736,1152]{1,0:T(8,128)(2,1)}) custom-call(bf16[1472,1152]{1,0:T(8,128)(2,1)} %add_convert_fusion.1.xn_ref, bf16[1472,1152]{1,0:T(8,128)(2,1)} %bitcast.19.dy_ref, ...), custom_call_target="tpu_custom_call" | custom-call | flops 15627976704 | bytes 24182784 | tf_op jit(solution)/shard_map/mlp/pallas_call | solution.py:207
  249.5 26.0 %mlp.3 = (bf16[1472,2304]{1,0:T(8,128)(2,1)}, bf16[1472,2304]{1,0:T(8,128)(2,1)}, f32[1,2304]{1,0:T(1,128)}, bf16[736,1152]{1,0:T(8,128)(2,1)}, bf16[736,1152]{1,0:T(8,128)(2,1)}) custom-call(bf16[1472,1152]{1,0:T(8,128)(2,1)} %add_convert_fusion.1.xn_ref, bf16[1472,1152]{1,0:T(8,128)(2,1)} %bitcast.19.dy_ref, ...), custom_call_target="tpu_custom_call", output_to_operand_aliasing={{0}: (5, {}), {1}: (6, {})} | custom-call | flops 15627976704 | bytes 24182784 | tf_op jit(solution)/shard_map/mlp/pallas_call | solution.py:207
  277.1 14.1 %convolution_convert_fusion.1 = bf16[1152,2176]{1,0:T(8,128)(2,1)} fusion(bf16[1472,1152]{1,0:T(8,128)(2,1)} %bitcast.19.dy_ref, bf16[1472,2304]{1,0:T(8,128)(2,1)} %get-tuple-element.66), kind=kOutput, calls=%fused_computation.1 | convolution fusion | flops 7382384640 | bytes 14811136 | tf_op jit(solution)/shard_map/dot_general | solution.py:22
  291.9 13.1 %convolution_convert_fusion = bf16[1152,2176]{1,0:T(8,128)(2,1)S(1)} fusion(bf16[1472,1152]{1,0:T(8,128)(2,1)} %add_convert_fusion.1.xn_ref, bf16[1472,2304]{1,0:T(8,128)(2,1)} %get-tuple-element.67), kind=kOutput, calls=%fused_computation | convolution fusion | flops 7382384640 | bytes 14811136 | tf_op jit(solution)/shard_map/dot_general | solution.py:22
  306.7 41.6 %collective-permute-done.10 = bf16[736,1152]{1,0:T(8,128)(2,1)S(1)} collective-permute-done((bf16[736,1152]{1,0:T(8,128)(2,1)}, bf16[736,1152]{1,0:T(8,128)(2,1)S(1)}, u32[]{:S(2)}, u32[]{:S(2)}) %collective-permute-start.10) | collective-permute-done | bytes 1695776 | tf_op jit(solution)/shard_map/ppermute | solution.py:240
  359.2 20.4 %attention_backward.2.refs_0_ = bf16[1472,1920]{1,0:T(8,128)(2,1)} custom-call(f32[1472,1]{1,0:T(8,128)} %select_n.243.bias_ref, bf16[1472,1920]{1,0:T(8,128)(2,1)} %add_convert_fusion.qkv_ref, bf16[736,640]{1,0:T(8,128)(2,1)} %get-tuple-element.52.out_ref, bf16[736,640]{1,0:T(8,128)(2,1)} %convolution_convert_fusion.5.dout_ref, ...), custom_call_target="tpu_custom_call" | custom-call | flops 11093934080 | bytes 7536640 | tf_op jit(solution)/shard_map/attention_backward/pallas_call | solution.py:144
  384.8 3.3 multiply_reduce_fusion.2
  388.2 3.4 fusion.73
  400.3 4.1 fusion.28
  408.5 20.6 %attention_backward.3 = bf16[1472,1920]{1,0:T(8,128)(2,1)} custom-call(f32[1472,1]{1,0:T(8,128)} %select_n.243.bias_ref, bf16[1472,1920]{1,0:T(8,128)(2,1)} %add_convert_fusion.qkv_ref, bf16[736,640]{1,0:T(8,128)(2,1)} %get-tuple-element.53.out_ref, bf16[736,640]{1,0:T(8,128)(2,1)} %convolution_convert_fusion.4.dout_ref, ...), custom_call_target="tpu_custom_call", output_to_operand_aliasing={{}: (5, {})} | custom-call | flops 11093934080 | bytes 7536640 | tf_op jit(solution)/shard_map/attention_backward/pallas_call | solution.py:144
  429.1 9.6 %convolution_convert_fusion.2 = bf16[1152,1920]{1,0:T(8,128)(2,1)S(1)} fusion(bf16[1472,1152]{1,0:T(8,128)(2,1)S(1)} %copy-done.9, bf16[1472,1920]{1,0:T(8,128)(2,1)} %attention_backward.3), kind=kOutput, calls=%fused_computation.6 | convolution fusion | flops 6513868800 | bytes 13467648 | tf_op jit(solution)/shard_map/dot_general | solution.py:22
  438.7 4.4 pad_maximum_fusion
  444.8 11.7 %convolution_convert_fusion.3 = bf16[1472,1152]{1,0:T(8,128)(2,1)S(1)} fusion(bf16[1472,1920]{1,0:T(8,128)(2,1)} %attention_backward.3, bf16[1152,1920]{1,0:T(8,128)(2,1)} %all-gather.3.cloned.1.call-done), kind=kOutput, calls=%fused_computation.7 | convolution fusion | flops 6513352704 | bytes 13467648 | tf_op jit(solution)/shard_map/dot_general | solution.py:22
  460.7 4.2 fusion.47
  464.9 4.7 collective-permute-done.15
  469.8 3.6 collective-permute-start.21
  474.4 24.6 %collective-permute-done.21 = bf16[1,72,2176]{2,1,0:T(8,128)(2,1)S(1)} collective-permute-done((bf16[1,72,2176]{2,1,0:T(8,128)(2,1)S(1)}, bf16[1,72,2176]{2,1,0:T(8,128)(2,1)S(1)}, u32[]{:S(2)}, u32[]{:S(2)}) %collective-permute-start.21) | collective-permute-done | bytes 313376 | tf_op jit(solution)/shard_map/ppermute | solution.py:290
  499.8 3.3 fusion.35
  504.1 3.9 copy.74
  516.9 4.3 collective-permute-done.19
  521.3 3.9 collective-permute-start.20
  525.2 3.4 fusion.48
  (270 shorter events, 118.7 us)
Async XLA Ops:
  7.2 58.9 %all-gather.3.cloned.1.call-start = ((), (), s32[]{:S(2)}) async-start(), calls=%async_computation.2 | async-start | bytes 4700160 | tf_op jit(solution)/shard_map/all_gather | solution.py:347
  9.4 214.5 %all-gather.5.cloned.1.call-start = ((), (), s32[]{:S(2)}) async-start(), calls=%async_computation.3 | async-start | bytes 11280384 | tf_op jit(solution)/shard_map/all_gather | solution.py:353
  11.5 522.8 %reduce-scatter.7.cloned.1.call-start = ((), (), s32[]{:S(2)}) async-start(), calls=%async_computation.5 | async-start | bytes 5326848
  15.9 43.9 %collective-permute-start = (bf16[2,368,1152]{2,1,0:T(8,128)(2,1)}, bf16[2,368,1152]{2,1,0:T(8,128)(2,1)}, u32[]{:S(2)}, u32[]{:S(2)}) collective-permute-start(bf16[2,368,1152]{2,1,0:T(8,128)(2,1)} %get-tuple-element.180), channel_id=1, source_target_pairs={{1,0},{0,1},{3,2},{2,3},{5,4},{4,5},{7,6},{6,7},{9,8},{8,9},{11,10... | collective-permute-start | bytes 5087240 | tf_op jit(solution)/shard_map/ppermute | solution.py:240
  18.9 39.3 %collective-permute-start.3 = (bf16[72,640]{1,0:T(8,128)(2,1)S(1)}, bf16[72,640]{1,0:T(8,128)(2,1)}, u32[]{:S(2)}, u32[]{:S(2)}) collective-permute-start(bf16[72,640]{1,0:T(8,128)(2,1)S(1)} %pad.33), channel_id=1, source_target_pairs={{1,0},{0,1},{3,2},{2,3},{5,4},{4,5},{7,6},{6,7},{9,8},{8,9},{11,10... | collective-permute-start | bytes 276488 | tf_op jit(solution)/shard_map/ppermute | solution.py:240
  21.0 42.4 %copy-start.18 = (f32[1152]{0:T(1024)}, f32[1152]{0:T(1024)S(1)}, u32[]{:S(2)}) copy-start(f32[1152]{0:T(1024)S(1)} %get-tuple-element.142) | copy-start | bytes 13828
  66.1 29.9 %collective-permute-start.4 = (bf16[1,72,1280]{2,1,0:T(8,128)(2,1)}, bf16[1,72,1280]{2,1,0:T(8,128)(2,1)S(1)}, u32[]{:S(2)}, u32[]{:S(2)}) collective-permute-start(bf16[1,72,1280]{2,1,0:T(8,128)(2,1)} %bitcast.158), channel_id=1, source_target_pairs={{0,16},{2,18},{4,20},{6,22},{8,24},{10,26},{12,28},{14,30},{16,0},... | collective-permute-start | bytes 552968 | tf_op jit(solution)/shard_map/ppermute | solution.py:274
  96.1 27.6 %collective-permute-start.5 = (bf16[2,72,1280]{2,1,0:T(8,128)(2,1)S(1)}, bf16[2,72,1280]{2,1,0:T(8,128)(2,1)S(1)}, u32[]{:S(2)}, u32[]{:S(2)}) collective-permute-start(bf16[2,72,1280]{2,1,0:T(8,128)(2,1)S(1)} %maximum_bitcast_fusion), channel_id=1, source_target_pairs={{0,8},{2,10},{4,12},{6,14},{8,0},{10,2},{12,4},{14,6},{16,24},{18,... | collective-permute-start | bytes 1105928 | tf_op jit(solution)/shard_map/ppermute | solution.py:274
  124.7 28.1 %collective-permute-start.6 = (bf16[4,72,1280]{2,1,0:T(8,128)(2,1)}, bf16[4,72,1280]{2,1,0:T(8,128)(2,1)}, u32[]{:S(2)}, u32[]{:S(2)}) collective-permute-start(bf16[4,72,1280]{2,1,0:T(8,128)(2,1)} %bitcast.10), channel_id=1, source_target_pairs={{0,4},{2,6},{4,0},{6,2},{8,12},{10,14},{12,8},{14,10},{16,20},{18,... | collective-permute-start | bytes 2211848 | tf_op jit(solution)/shard_map/ppermute | solution.py:274
  132.8 40.2 %collective-permute-start.8 = (bf16[2,368,1152]{2,1,0:T(8,128)(2,1)}, bf16[2,368,1152]{2,1,0:T(8,128)(2,1)}, u32[]{:S(2)}, u32[]{:S(2)}) collective-permute-start(bf16[2,368,1152]{2,1,0:T(8,128)(2,1)} %get-tuple-element.154), channel_id=1, source_target_pairs={{1,0},{0,1},{3,2},{2,3},{5,4},{4,5},{7,6},{6,7},{9,8},{8,9},{11,10... | collective-permute-start | bytes 5087240 | tf_op jit(solution)/shard_map/ppermute | solution.py:240
  155.6 20.1 %collective-permute-start.7 = (bf16[8,72,1280]{2,1,0:T(8,128)(2,1)}, bf16[8,72,1280]{2,1,0:T(8,128)(2,1)}, u32[]{:S(2)}, u32[]{:S(2)}) collective-permute-start(bf16[8,72,1280]{2,1,0:T(8,128)(2,1)} %bitcast.13), channel_id=1, source_target_pairs={{0,2},{2,0},{4,6},{6,4},{8,10},{10,8},{12,14},{14,12},{16,18},{18,... | collective-permute-start | bytes 4423688 | tf_op jit(solution)/shard_map/ppermute | solution.py:274
  163.0 30.1 %collective-permute-start.2 = (bf16[736,640]{1,0:T(8,128)(2,1)}, bf16[736,640]{1,0:T(8,128)(2,1)S(1)}, u32[]{:S(2)}, u32[]{:S(2)}) collective-permute-start(bf16[736,640]{1,0:T(8,128)(2,1)} %get-tuple-element.53.out_ref), channel_id=1, source_target_pairs={{1,0},{0,1},{3,2},{2,3},{5,4},{4,5},{7,6},{6,7},{9,8},{8,9},{11,10... | collective-permute-start | bytes 2826248 | tf_op jit(solution)/shard_map/ppermute | solution.py:240
  164.4 46.0 %collective-permute-start.1 = (bf16[736,640]{1,0:T(8,128)(2,1)}, bf16[736,640]{1,0:T(8,128)(2,1)S(1)}, u32[]{:S(2)}, u32[]{:S(2)}) collective-permute-start(bf16[736,640]{1,0:T(8,128)(2,1)} %get-tuple-element.52.out_ref), channel_id=1, source_target_pairs={{1,0},{0,1},{3,2},{2,3},{5,4},{4,5},{7,6},{6,7},{9,8},{8,9},{11,10... | collective-permute-start | bytes 2826248 | tf_op jit(solution)/shard_map/ppermute | solution.py:240
  178.3 37.7 %copy-start.10 = (bf16[8,2,72,1280]{3,2,1,0:T(8,128)(2,1)}, bf16[8,2,72,1280]{3,2,1,0:T(8,128)(2,1)S(1)}, u32[]{:S(2)}) copy-start(bf16[8,2,72,1280]{3,2,1,0:T(8,128)(2,1)S(1)} %copy.68) | copy-start | bytes 8847364
  275.5 104.1 %collective-permute-start.9 = (bf16[736,1152]{1,0:T(8,128)(2,1)}, bf16[736,1152]{1,0:T(8,128)(2,1)}, u32[]{:S(2)}, u32[]{:S(2)}) collective-permute-start(bf16[736,1152]{1,0:T(8,128)(2,1)} %get-tuple-element.64), channel_id=1, source_target_pairs={{1,0},{0,1},{3,2},{2,3},{5,4},{4,5},{7,6},{6,7},{9,8},{8,9},{11,10... | collective-permute-start | bytes 5087240 | tf_op jit(solution)/shard_map/ppermute | solution.py:240
  291.2 57.1 %slice-start = ((s8[6782976]{0:T(1024)(128)(4,1)}), s8[2588672]{0:T(1024)(128)(4,1)S(1)}, s32[]{:S(2)}) async-start(s8[6782976]{0:T(1024)(128)(4,1)} %bitcast.135), calls=%async_computation.6 | async-start | bytes 5177344
  291.3 245.0 %reduce-scatter.5.cloned.1.call-start = ((), (), s32[]{:S(2)}) async-start(), calls=%async_computation.4 | async-start | bytes 6266880 | tf_op jit(solution)/shard_map/reduce_scatter | solution.py:475
  291.3 57.0 %slice-start.1 = ((s8[6782976]{0:T(1024)(128)(4,1)}), s8[4194304]{0:T(1024)(128)(4,1)S(1)}, s32[]{:S(2)}) async-start(s8[6782976]{0:T(1024)(128)(4,1)} %bitcast.135), calls=%async_computation.7 | async-start | bytes 8388608
  291.3 57.0 %collective-permute-start.10 = (bf16[736,1152]{1,0:T(8,128)(2,1)}, bf16[736,1152]{1,0:T(8,128)(2,1)S(1)}, u32[]{:S(2)}, u32[]{:S(2)}) collective-permute-start(bf16[736,1152]{1,0:T(8,128)(2,1)} %get-tuple-element.68), channel_id=1, source_target_pairs={{1,0},{0,1},{3,2},{2,3},{5,4},{4,5},{7,6},{6,7},{9,8},{8,9},{11,10... | collective-permute-start | bytes 5087240 | tf_op jit(solution)/shard_map/ppermute | solution.py:240
  305.0 45.6 %copy-start.8 = (bf16[1152,2176]{1,0:T(8,128)(2,1)}, bf16[1152,2176]{1,0:T(8,128)(2,1)S(1)}, u32[]{:S(2)}) copy-start(bf16[1152,2176]{1,0:T(8,128)(2,1)S(1)} %convolution_convert_fusion) | copy-start | bytes 15040516
  305.1 43.3 %copy-start.7 = (bf16[736,1152]{1,0:T(8,128)(2,1)S(1)}, bf16[736,1152]{1,0:T(8,128)(2,1)}, u32[]{:S(2)}) copy-start(bf16[736,1152]{1,0:T(8,128)(2,1)} %get-tuple-element.68) | copy-start | bytes 5087236
  306.7 97.8 %collective-permute-start.12 = (bf16[8,72,2176]{2,1,0:T(8,128)(2,1)}, bf16[8,72,2176]{2,1,0:T(8,128)(2,1)}, u32[]{:S(2)}, u32[]{:S(2)}) collective-permute-start(bf16[8,72,2176]{2,1,0:T(8,128)(2,1)} %dynamic-slice_bitcast_fusion), channel_id=1, source_target_pairs={{0,2},{2,0},{4,6},{6,4},{8,10},{10,8},{12,14},{14,12},{16,18},{18,... | collective-permute-start | bytes 7520264 | tf_op jit(solution)/shard_map/ppermute | solution.py:290
  383.3 73.6 %collective-permute-start.11 = (bf16[2,368,1152]{2,1,0:T(8,128)(2,1)}, bf16[2,368,1152]{2,1,0:T(8,128)(2,1)}, u32[]{:S(2)}, u32[]{:S(2)}) collective-permute-start(bf16[2,368,1152]{2,1,0:T(8,128)(2,1)} %pad_maximum_fusion.4), channel_id=1, source_target_pairs={{0,1},{1,0},{2,3},{3,2},{4,5},{5,4},{6,7},{7,6},{8,9},{9,8},{10,11... | collective-permute-start | bytes 5087240 | tf_op jit(solution)/shard_map/ppermute | solution.py:264
  408.0 35.2 %collective-permute-start.13 = (bf16[4,72,2176]{2,1,0:T(8,128)(2,1)}, bf16[4,72,2176]{2,1,0:T(8,128)(2,1)}, u32[]{:S(2)}, u32[]{:S(2)}) collective-permute-start(bf16[4,72,2176]{2,1,0:T(8,128)(2,1)} %dynamic-slice_bitcast_fusion.3), channel_id=1, source_target_pairs={{0,4},{2,6},{4,0},{6,2},{8,12},{10,14},{12,8},{14,10},{16,20},{18,... | collective-permute-start | bytes 3760136 | tf_op jit(solution)/shard_map/ppermute | solution.py:290
  457.4 42.4 %collective-permute-start.14 = (bf16[2,368,1152]{2,1,0:T(8,128)(2,1)S(1)}, bf16[2,368,1152]{2,1,0:T(8,128)(2,1)S(1)}, u32[]{:S(2)}, u32[]{:S(2)}) collective-permute-start(bf16[2,368,1152]{2,1,0:T(8,128)(2,1)S(1)} %pad_maximum_fusion.6), channel_id=1, source_target_pairs={{0,1},{1,0},{2,3},{3,2},{4,5},{5,4},{6,7},{7,6},{8,9},{9,8},{10,11... | collective-permute-start | bytes 5087240 | tf_op jit(solution)/shard_map/ppermute | solution.py:264
  457.8 11.8 %collective-permute-start.15 = (bf16[2,72,2176]{2,1,0:T(8,128)(2,1)S(1)}, bf16[2,72,2176]{2,1,0:T(8,128)(2,1)S(1)}, u32[]{:S(2)}, u32[]{:S(2)}) collective-permute-start(bf16[2,72,2176]{2,1,0:T(8,128)(2,1)S(1)} %get-tuple-element.184), channel_id=1, source_target_pairs={{0,8},{2,10},{4,12},{6,14},{8,0},{10,2},{12,4},{14,6},{16,24},{18,... | collective-permute-start | bytes 1880072 | tf_op jit(solution)/shard_map/ppermute | solution.py:290
  469.8 29.2 %collective-permute-start.21 = (bf16[1,72,2176]{2,1,0:T(8,128)(2,1)S(1)}, bf16[1,72,2176]{2,1,0:T(8,128)(2,1)S(1)}, u32[]{:S(2)}, u32[]{:S(2)}) collective-permute-start(bf16[1,72,2176]{2,1,0:T(8,128)(2,1)S(1)} %constant_dynamic-slice_fusion), channel_id=1, source_target_pairs={{0,16},{2,18},{4,20},{6,22},{8,24},{10,26},{12,28},{14,30},{16,0},... | collective-permute-start | bytes 940040 | tf_op jit(solution)/shard_map/ppermute | solution.py:290
  503.2 4.9 collective-permute-start.16
  508.2 1.9 collective-permute-start.17
  510.0 4.4 collective-permute-start.18
  514.4 6.9 %collective-permute-start.19 = (f32[10216]{0:T(1024)S(1)}, f32[10216]{0:T(1024)S(1)}, u32[]{:S(2)}, u32[]{:S(2)}) collective-permute-start(f32[10216]{0:T(1024)S(1)} %add.363), channel_id=1, source_target_pairs={{0,8},{2,10},{4,12},{6,14},{8,0},{10,2},{12,4},{14,6},{16,24},{18,... | collective-permute-start | bytes 122600 | tf_op jit(solution)/shard_map/ppermute | solution.py:299
  521.3 9.8 %collective-permute-start.20 = (f32[10216]{0:T(1024)S(1)}, f32[10216]{0:T(1024)S(1)}, u32[]{:S(2)}, u32[]{:S(2)}) collective-permute-start(f32[10216]{0:T(1024)S(1)} %add.364), channel_id=1, source_target_pairs={{0,16},{2,18},{4,20},{6,22},{8,24},{10,26},{12,28},{14,30},{16,0},... | collective-permute-start | bytes 122600 | tf_op jit(solution)/shard_map/ppermute | solution.py:299
  (43 other events, 367.5 us)
Sparse Core Ops, SparseCore 0:
  10.7 54.2 all-gather.2
  67.3 100.2 all-gather.4
  291.4 72.9 reduce-scatter.6
  443.2 91.1 reduce-scatter.4
